TPU v7x, 256 devices: a whole 4x4x8 slice. The times are simulated.
256 devices in a mesh: out: 16 (over z, x_lo), inp: 16 (over y, x_hi, core).
Axes of the slice: x: 4 (x_hi: 2, x_lo: 2; x = x_hi * 2 + x_lo), y: 4, z: 8, core: 2. Of those that a mesh axis runs over, the one named last changes fastest.
Arguments:
- tensor: bfloat16 [1024, 1024, 1024], P('out', 'inp'), may hold values from -0.005859375 to 0.005859375
- state: bfloat16 [1536, 1024], P('out'), may hold values from -6 to 6
Outputs:
- collision: bfloat16 [1536, 1024], P('inp', 'out')
All inputs are finite; a program needn't handle non-finite values.
Results may differ from a plain program's by a relative error of at most 0.001.
Values may be sent and summed in bfloat16 or wider, within the bound.
No kernel may reach another device: no remote copies, remote signals or barrier semaphores. Data moves between devices by JAX's collectives and lax.ppermute only.
A program may use at most 64 MiB of HBM per device.

v0:
```python
import jax
import jax.numpy as jnp
from jax import lax
from jax.sharding import PartitionSpec as P


def local(tensor, state):
    rows_out = tensor.shape[0]
    rows_inp = tensor.shape[1]
    width = tensor.shape[2]
    flat = tensor.reshape(rows_out * rows_inp, width)
    first_col = lax.axis_index("inp") * rows_inp
    piece = lax.all_gather(state, "out", axis=0, tiled=True)
    inner = lax.dot_general(
        piece, flat, (((1,), (1,)), ((), ())), preferred_element_type=jnp.float32
    )
    inner = inner.reshape(piece.shape[0], rows_out, rows_inp)
    chosen = lax.dynamic_slice_in_dim(piece, first_col, rows_inp, 1).astype(jnp.float32)
    partial_sum = jnp.sum(inner * chosen[:, None, :], axis=2)
    owned = lax.psum_scatter(partial_sum, "inp", scatter_dimension=0, tiled=True)
    return owned.astype(jnp.bfloat16)


def solution(mesh):
    placed = (P("out", "inp", None), P("out", None))
    return jax.shard_map(
        local, mesh=mesh, in_specs=placed, out_specs=P("inp", "out"), check_vma=False
    )
```

profile of v0, /device:TPU:32, one launch (start us, length us, event | category | flops | bytes accessed | tf_op | source)
XLA Modules:
  0.0 193.3 jit_solution(1378106309602096802)
XLA Ops:
  6.5 0.0 all-gather.2.cloned.1.call-start
  6.5 0.7 all-gather.2.cloned.1.call-update
  7.3 0.0 reduce-scatter.4.cloned.1.call-start
  7.3 84.7 %all-gather.2.cloned.1.call-done = bf16[1536,1024]{1,0:T(8,128)(2,1)} async-done(((bf16[96,1024]{1,0:T(8,128)(2,1)}), bf16[1536,1024]{1,0:T(8,128)(2,1)}) %all-gather.2.cloned.1.call-update) | async-done | bytes 3145744 | tf_op jit(solution)/shard_map/all_gather | solution.py:13
  92.0 1.2 constant_dynamic-slice_fusion
  93.2 0.2 copy.10
  93.4 16.8 %multiply_reduce_fusion = f32[1536,64]{0,1:T(8,128)S(1)} fusion(bf16[64,64,1024]{2,1,0:T(8,128)(2,1)} %param.2, f32[1536,64]{0,1:T(8,128)S(1)} %convert_element_type.6, bf16[1536,1024]{1,0:T(8,128)(2,1)} %all-gather.2.cloned.1.call-done), kind=kOutput, calls=%fused_computation | convolution fusion | flops 12897386496 | bytes 12320768 | tf_op jit(solution)/shard_map/dot_general | solution.py:14
  110.2 1.2 copy.8
  111.4 0.0 reduce-scatter.4.cloned.1.call-update
  111.4 73.5 %reduce-scatter.4.cloned.1.call-done = f32[96,64]{1,0:T(8,128)} async-done(((f32[1536,64]{1,0:T(8,128)}), f32[96,64]{1,0:T(8,128)}) %reduce-scatter.4.cloned.1.call-update) | async-done | bytes 24592
  184.9 1.5 copy.9
  (1 shorter events, 0.0 us)
Async XLA Ops:
  6.5 85.5 %all-gather.2.cloned.1.call-start = ((), (), s32[]{:S(2)}) async-start(), calls=%async_computation.1 | async-start | bytes 3342336 | tf_op jit(solution)/shard_map/all_gather | solution.py:13
  7.3 177.7 %reduce-scatter.4.cloned.1.call-start = ((), (), s32[]{:S(2)}) async-start(), calls=%async_computation.2 | async-start | bytes 835584
Sparse Core Ops, SparseCore 0:
  9.1 82.8 all-gather.1
  111.5 73.3 reduce-scatter.3
where the time goes:
time: 193 us
  waiting for transfers between devices  159 us (82%)
  matrix products  16.8 us (9%)
  between operations  13.4 us (7%)
  local copies, waits for them, and re-layouts  3.97 us (2%)
    all_gather x1, waiting for transfers between devices, local(): piece = lax.all_gather(state, 'out', axis=0, tiled=True)  84.7 us
    unnamed x3, waiting for transfers between devices  74.2 us
    dot_general x1, matrix products, local(): lax.dot_general(piece, flat, (((1,), (1,)), ((), ())), preferred_element_...  16.8 us
  transfers between devices with their start and end apart: 2, of which 2 were waited for; matrix products, arithmetic and copies ran while one was open for 0% of the time, Pallas kernels for 0%

commit v1 on v0

v1 whole, which is shorter than its diff:
```python
import functools

import jax
import jax.numpy as jnp
from jax import lax
from jax.experimental import pallas as pl
from jax.experimental.pallas import tpu as pltpu
from jax.sharding import PartitionSpec as P

NZ, NX, NY, NC = 8, 4, 4, 2
AXES = ("out", "inp")
BLOCK = 96
HALF = BLOCK // 2
K_OUT = 64
K_INP = 64
K_STEP = 32
TILE = 256
NEAR = (0, 1, 2, -1, -2)
FAR = (3, -3, 4)
VMEM = pl.BlockSpec(memory_space=pltpu.VMEM)
SMEM = pl.BlockSpec(memory_space=pltpu.SMEM)
HBM = pl.BlockSpec(memory_space=pltpu.HBM)

SMALL = pltpu.CompilerParams(vmem_limit_bytes=4 << 20)


def device(x, y, z, core):
    out = (z % NZ) * 2 + (x % NX) % 2
    inp = (y % NY) * 4 + ((x % NX) // 2) * 2 + core % NC
    return out * 16 + inp


def hop(way):
    pairs = []
    for z in range(NZ):
        for y in range(NY):
            for x in range(NX):
                for c in range(NC):
                    dx, dy, dz, dc = way(c)
                    pairs.append((device(x, y, z, c), device(x + dx, y + dy, z + dz, c + dc)))
    return pairs


def sign(core):
    return 1 - 2 * core


def along_z(array, d):
    return lax.ppermute(array, AXES, hop(lambda c: (0, 0, d * sign(c), 0)))


def along_x(array):
    return lax.ppermute(array, AXES, hop(lambda c: (sign(c), 0, 0, 0)))


def swap(array):
    return lax.ppermute(array, AXES, hop(lambda c: (0, 0, 0, 1)))


def rows(*arrays):
    return jnp.concatenate(arrays, axis=0)


def pack(block):
    last = block[48:64]
    side = jnp.concatenate([last[:, 0:32], last[:, 32:64], last[:, 64:96]], axis=0)
    return jnp.concatenate([block[0:48], side], axis=1)


def unpack(packed):
    side = packed[:, 96:128]
    last = jnp.concatenate([side[0:16], side[16:32], side[32:48]], axis=1)
    return jnp.concatenate([packed[:, 0:96], last], axis=0)


def place_group(cells, start, shards, mine, theirs, core):
    source = [0, 0]
    for n, d in enumerate(shards):
        at = start + n * BLOCK
        if d in (0, 4):
            for which, piece in enumerate((mine, theirs)):
                half = core if which == 0 else 1 - core
                first = 0 if d == 0 else BLOCK
                spot = pl.multiple_of(at + half * HALF, 16)
                cells[pl.ds(spot, HALF), :] = piece[first : first + HALF, :]
                if d == 0:
                    source[which] = HALF
        else:
            which, piece = (0, mine) if d > 0 else (1, theirs)
            first = source[which]
            cells[at : at + BLOCK, :] = piece[first : first + BLOCK, :]
            source[which] = first + BLOCK


def collide(groups, first_call, where, *refs):
    refs = list(refs)
    tensor_in = refs.pop(0)
    pieces = [(refs.pop(0), refs.pop(0)) for _ in groups]
    if first_call:
        give, keep, tensor, cells, weight, total, arrived = refs
        copies = [
            pltpu.make_async_copy(
                tensor_in.at[pl.ds(k, K_STEP)], tensor.at[pl.ds(k, K_STEP)], arrived.at[k // K_STEP]
            )
            for k in range(0, K_OUT, K_STEP)
        ]
        for copy in copies:
            copy.start()
    else:
        tensor = tensor_in
        _, _, give, keep, cells, weight, total = refs
        copies = None
    first, z, odd, core = where[0], where[1], where[2], where[3]
    start = 0
    for (shards, _), (mine, theirs) in zip(groups, pieces):
        place_group(cells, start, shards, mine, theirs, core)
        start += BLOCK * len(shards)
    base = pl.multiple_of((first // 128) * 128, 128)
    weight[...] = cells[:, pl.ds(base, 128)].astype(jnp.float32).T
    off = pl.multiple_of(lax.rem(first, 128), K_INP)
    size = cells.shape[0]

    def step(k):
        left = tensor[pl.ds(k, K_STEP)].reshape(K_STEP * K_INP, tensor.shape[2])
        for c in range(0, size, TILE):
            w = min(TILE, size - c)
            inner = lax.dot_general(
                left,
                cells[c : c + w, :],
                (((1,), (1,)), ((), ())),
                preferred_element_type=jnp.float32,
            )
            chosen = weight[pl.ds(off, K_INP), c : c + w]
            total[pl.ds(k, K_STEP), c : c + w] = jnp.sum(
                inner.reshape(K_STEP, K_INP, w) * chosen[None], axis=1
            )

    if copies is None:

        def body(s, carry):
            step(pl.multiple_of(s * K_STEP, K_STEP))
            return carry

        lax.fori_loop(0, K_OUT // K_STEP, body, 0)
    else:
        for n, copy in enumerate(copies):
            copy.wait()
            step(n * K_STEP)

    at = 0
    for shards, own in groups:
        kept = (odd == core) if own else (odd != core)
        blocks = []
        for d in shards:
            owner = lax.rem(z - d * (1 - 2 * core) + NZ, NZ)
            blocks.append((owner, pack(total[:, at : at + BLOCK])))
            at += BLOCK

        @pl.when(kept)
        def _():
            for owner, block in blocks:
                keep[owner] = block

        @pl.when(jnp.logical_not(kept))
        def _():
            for owner, block in blocks:
                give[owner] = block


def partial_sums(groups, where, tensor, pieces, before):
    size = BLOCK * sum(len(shards) for shards, _ in groups)
    first_call = before is None
    args = [where, tensor] + [piece for pair in pieces for piece in pair]
    in_specs = [SMEM, HBM if first_call else VMEM] + [VMEM] * (len(args) - 2)
    part = jax.ShapeDtypeStruct((NZ, 48, 128), jnp.float32)
    out_shape, aliases = [part, part], {}
    scratch = [
        pltpu.VMEM((size, 1024), jnp.bfloat16),
        pltpu.VMEM((128, size), jnp.float32),
        pltpu.VMEM((K_OUT, size), jnp.float32),
    ]
    if first_call:
        out_shape.append(jax.ShapeDtypeStruct(tensor.shape, tensor.dtype))
        scratch.append(pltpu.SemaphoreType.DMA((K_OUT // K_STEP,)))
    else:
        aliases = {len(args): 0, len(args) + 1: 1}
        args += before
        in_specs += [VMEM, VMEM]
    return pl.pallas_call(
        functools.partial(collide, groups, first_call),
        in_specs=in_specs,
        out_specs=[VMEM] * len(out_shape),
        out_shape=out_shape,
        input_output_aliases=aliases,
        scratch_shapes=scratch,
        compiler_params=pltpu.CompilerParams(vmem_limit_bytes=(42 if first_call else 24) << 20),
        cost_estimate=pl.CostEstimate(
            flops=2 * K_OUT * K_INP * 1024 * size,
            bytes_accessed=1 << 20,
            transcendentals=0,
        ),
    )(*args)


def add_pair(mine, theirs, out):
    out[...] = mine[...] + theirs[...]


def add_up(shares, out):
    out[...] = unpack(jnp.sum(shares[...], axis=0)).astype(jnp.bfloat16)


def local(tensor, state):
    out_at, inp_at = lax.axis_index("out"), lax.axis_index("inp")
    z, odd, core = out_at // 2, out_at % 2, inp_at % 2
    where = jnp.stack([inp_at * K_INP, z, odd, core]).astype(jnp.int32)

    def half(array):
        return lax.dynamic_slice_in_dim(array, core * HALF, HALF, 0)

    one = along_z(state, 1)
    two = along_z(state, 2)
    near = rows(half(state), one, two)
    three = along_z(two, 1)
    four = along_z(half(two), 2)
    near_x = along_x(near)
    near_swap = swap(near)
    give, keep, held = partial_sums(
        ((NEAR, True),), where, tensor, [(near, near_swap)], None
    )

    three, four, give = lax.optimization_barrier((three, four, give))
    far = rows(three, four)
    far_x = along_x(far)
    far_swap = swap(far)
    near_x_swap = swap(near_x)
    give, keep = partial_sums(
        ((FAR, True), (NEAR, False)),
        where,
        held,
        [(far, far_swap), (near_x, near_x_swap)],
        [give, keep],
    )

    far_x, give = lax.optimization_barrier((far_x, give))
    far_x_swap = swap(far_x)
    give, keep = partial_sums(
        ((FAR, False),), where, held, [(far_x, far_x_swap)], [give, keep]
    )

    got = swap(give)
    pair = pl.pallas_call(
        add_pair,
        in_specs=[VMEM, VMEM],
        out_specs=VMEM,
        out_shape=jax.ShapeDtypeStruct(keep.shape, keep.dtype),
        compiler_params=SMALL,
    )(keep, got)
    groups = [[c + NC * i for i in range(NZ)] for c in range(NC)]
    shares = lax.all_to_all(pair, "inp", 0, 0, tiled=True, axis_index_groups=groups)
    done = pl.pallas_call(
        add_up,
        in_specs=[VMEM],
        out_specs=VMEM,
        out_shape=jax.ShapeDtypeStruct((K_OUT, BLOCK), jnp.bfloat16),
        compiler_params=SMALL,
    )(shares)
    return done.T


def solution(mesh):
    placed = (P("out", "inp", None), P("out", None))
    return jax.shard_map(
        local, mesh=mesh, in_specs=placed, out_specs=P("inp", "out"), check_vma=False
    )
```

time: 193 us -> 63.1 us (0.33)
  waiting for transfers between devices: 159 us -> 7.03 us
  Pallas kernels: 0 us -> 22.5 us
  starting transfers between devices: 0.04 us -> 17.4 us
  matrix products: 16.8 us -> 0 us
  blocking collectives: 0 us -> 14.9 us
  between operations: 13.4 us -> 0.13 us
  local copies, waits for them, and re-layouts: 3.97 us -> 0.96 us
    all_gather x1 -> x0, waiting for transfers between devices: 84.7 us -> none  [local(): piece = lax.all_gather(state, 'out', axis=0, tiled=True)]
    unnamed x3 -> x0, waiting for transfers between devices: 74.2 us -> none
    pallas_call x0 -> x5, Pallas kernels: none -> 22.5 us  [the longest x3 21.8 us: partial_sums(): pl.pallas_call(functools.partial(collide, groups, first_call), in_specs=i...]
    ppermute x0 -> x11, starting transfers between devices: none -> 17.4 us  [the longest x4 13.2 us: along_z(): return lax.ppermute(array, AXES, hop(lambda c: (0, 0, d * sign(c), 0)))]
    dot_general x1 -> x0, matrix products: 16.8 us -> none  [local(): lax.dot_general(piece, flat, (((1,), (1,)), ((), ())), preferred_element_...]
    all_to_all x0 -> x1, blocking collectives: none -> 14.9 us  [local(): lax.all_to_all(pair, 'inp', 0, 0, tiled=True, axis_index_groups=groups)]
    ppermute x0 -> x11, waiting for transfers between devices: none -> 7.03 us  [the longest x4 4.13 us: along_z(): return lax.ppermute(array, AXES, hop(lambda c: (0, 0, d * sign(c), 0)))]
    unnamed x3 -> x1, local copies, waits for them, and re-layouts: 2.81 us -> 0.01 us
  transfers between devices with their start and end apart: 2 -> 11, of which waited for: 2 -> 4; matrix products, arithmetic and copies ran while one was open for 0% -> 2% of each run, Pallas kernels for 0% -> 25%
where the time goes in v1:
time: 63.1 us; the launch traced here: 63 us
  Pallas kernels  22.5 us (36%)
  starting transfers between devices  17.4 us (28%)
  blocking collectives  14.9 us (24%)
  waiting for transfers between devices  7.03 us (11%)
  local copies, waits for them, and re-layouts  0.96 us (2%)
    pallas_call x3, Pallas kernels, partial_sums(): pl.pallas_call(functools.partial(collide, groups, first_call), in_specs=i...  21.8 us
    all_to_all x1, blocking collectives, local(): lax.all_to_all(pair, 'inp', 0, 0, tiled=True, axis_index_groups=groups)  14.9 us
    ppermute x4, starting transfers between devices, along_z(): return lax.ppermute(array, AXES, hop(lambda c: (0, 0, d * sign(c), 0)))  13.2 us
    ppermute x4, waiting for transfers between devices, along_z(): return lax.ppermute(array, AXES, hop(lambda c: (0, 0, d * sign(c), 0)))  4.13 us
    ppermute x2, starting transfers between devices, along_x(): return lax.ppermute(array, AXES, hop(lambda c: (sign(c), 0, 0, 0)))  3.01 us
    ppermute x5, waiting for transfers between devices, swap(): return lax.ppermute(array, AXES, hop(lambda c: (0, 0, 0, 1)))  2.9 us
  transfers between devices with their start and end apart: 11, of which 4 were waited for; matrix products, arithmetic and copies ran while one was open for 2% of the time, Pallas kernels for 25%

profile of v1, /device:TPU:32, one launch (start us, length us, event | category | flops | bytes accessed | tf_op | source)
XLA Modules:
  0.0 63.0 jit_solution(15928572651126052433)
XLA Ops:
  0.0 3.3 %collective-permute-start.1 = (bf16[96,1024]{1,0:T(8,128)(2,1)}, bf16[96,1024]{1,0:T(8,128)(2,1)S(1)}, u32[]{:S(2)}, u32[]{:S(2)}) collective-permute-start(bf16[96,1024]{1,0:T(8,128)(2,1)} %param.3), channel_id=1, source_target_pairs={{0,64},{1,193},{16,80},{17,209},{2,66},{3,195},{18,82},{19,211},{4... | collective-permute-start | bytes 589832 | tf_op jit(solution)/shard_map/ppermute | solution.py:49
  3.3 3.1 %collective-permute-start = (bf16[96,1024]{1,0:T(8,128)(2,1)}, bf16[96,1024]{1,0:T(8,128)(2,1)S(1)}, u32[]{:S(2)}, u32[]{:S(2)}) collective-permute-start(bf16[96,1024]{1,0:T(8,128)(2,1)} %param.3), channel_id=1, source_target_pairs={{0,32},{1,225},{16,48},{17,241},{2,34},{3,227},{18,50},{19,243},{4... | collective-permute-start | bytes 589832 | tf_op jit(solution)/shard_map/ppermute | solution.py:49
  6.4 0.9 %constant_dynamic-slice_fusion.1 = bf16[48,1024]{1,0:T(8,128)(2,1)S(1)} fusion(bf16[96,1024]{1,0:T(8,128)(2,1)} %param.3, s32[]{:T(128)S(6)} %select_n.22), kind=kLoop, calls=%fused_computation.5 | loop fusion | bytes 196612 | tf_op jit(solution)/shard_map/dynamic_slice | solution.py:219
  7.3 4.1 %collective-permute-done.1 = bf16[96,1024]{1,0:T(8,128)(2,1)S(1)} collective-permute-done((bf16[96,1024]{1,0:T(8,128)(2,1)}, bf16[96,1024]{1,0:T(8,128)(2,1)S(1)}, u32[]{:S(2)}, u32[]{:S(2)}) %collective-permute-start.1) | collective-permute-done | bytes 196640 | tf_op jit(solution)/shard_map/ppermute | solution.py:49
  11.4 0.0 collective-permute-done
  11.5 0.1 collective-permute-start.2
  11.6 0.1 pad_add_fusion.where
  11.7 1.5 %collective-permute-start.7 = (bf16[240,1024]{1,0:T(8,128)(2,1)S(1)}, bf16[240,1024]{1,0:T(8,128)(2,1)S(1)}, u32[]{:S(2)}, u32[]{:S(2)}) collective-permute-start(bf16[240,1024]{1,0:T(8,128)(2,1)S(1)} %pad_maximum_fusion.refs_1_), channel_id=1, source_target_pairs={{0,16},{1,19},{16,2},{17,1},{2,18},{3,17},{18,0},{19,3},{4,20},{5,... | collective-permute-start | bytes 1474568 | tf_op jit(solution)/shard_map/ppermute | solution.py:53
  13.2 4.5 %collective-permute-start.4 = (bf16[48,1024]{1,0:T(8,128)(2,1)S(1)}, bf16[48,1024]{1,0:T(8,128)(2,1)S(1)}, u32[]{:S(2)}, u32[]{:S(2)}) collective-permute-start(bf16[48,1024]{1,0:T(8,128)(2,1)S(1)} %constant_dynamic-slice_fusion), channel_id=1, source_target_pairs={{0,64},{1,193},{16,80},{17,209},{2,66},{3,195},{18,82},{19,211},{4... | collective-permute-start | bytes 294920 | tf_op jit(solution)/shard_map/ppermute | solution.py:49
  17.7 2.3 %collective-permute-start.3 = (bf16[96,1024]{1,0:T(8,128)(2,1)S(1)}, bf16[96,1024]{1,0:T(8,128)(2,1)S(1)}, u32[]{:S(2)}, u32[]{:S(2)}) collective-permute-start(bf16[96,1024]{1,0:T(8,128)(2,1)S(1)} %collective-permute-done.1), channel_id=1, source_target_pairs={{0,32},{1,225},{16,48},{17,241},{2,34},{3,227},{18,50},{19,243},{4... | collective-permute-start | bytes 589832 | tf_op jit(solution)/shard_map/ppermute | solution.py:49
  20.0 7.9 %shard_map.28 = (f32[8,48,128]{2,1,0:T(8,128)S(1)}, f32[8,48,128]{2,1,0:T(8,128)S(1)}, bf16[64,64,1024]{2,1,0:T(8,128)(2,1)S(1)}) custom-call(s32[4]{0:T(128)S(1)} %pad_add_fusion.where, bf16[64,64,1024]{2,1,0:T(8,128)(2,1)} %refs_0_.1, bf16[240,1024]{1,0:T(8,128)(2,1)S(1)} %pad_maximum_fusion.refs_1_, bf16[240,1024]{1,0:T(8,128)(2,1)S(1)} %collective-permute-done.2.refs_2_), custom_call_target="tpu_custom_call" | custom-call | flops 4026531840 | bytes 1048576 | tf_op jit(solution)/shard_map/pallas_call | solution.py:189
  27.9 0.0 collective-permute-done.3
  27.9 0.1 collective-permute-start.8
  28.0 0.6 collective-permute-start.6
  28.6 1.5 %collective-permute-start.5 = (bf16[144,1024]{1,0:T(8,128)(2,1)S(1)}, bf16[144,1024]{1,0:T(8,128)(2,1)S(1)}, u32[]{:S(2)}, u32[]{:S(2)}) collective-permute-start(bf16[144,1024]{1,0:T(8,128)(2,1)S(1)} %constant_dynamic-update-slice_fusion.refs_1_), channel_id=1, source_target_pairs={{0,16},{1,19},{16,2},{17,1},{2,18},{3,17},{18,0},{19,3},{4,20},{5,... | collective-permute-start | bytes 884744 | tf_op jit(solution)/shard_map/ppermute | solution.py:53
  30.1 0.2 collective-permute-done.6.refs_2_
  30.3 8.2 %shard_map.29 = (f32[8,48,128]{2,1,0:T(8,128)S(1)}, f32[8,48,128]{2,1,0:T(8,128)S(1)}) custom-call(s32[4]{0:T(128)S(1)} %pad_add_fusion.where, bf16[64,64,1024]{2,1,0:T(8,128)(2,1)S(1)} %get-tuple-element.17.refs_0_, bf16[144,1024]{1,0:T(8,128)(2,1)S(1)} %constant_dynamic-update-slice_fusion.refs_1_, ...), custom_call_target="tpu_custom_call", output_to_operand_aliasing={{0}: (6, {}), {1}: (7, {})} | custom-call | flops 6442450944 | bytes 1048576 | tf_op jit(solution)/shard_map/pallas_call | solution.py:189
  38.5 0.2 collective-permute-start.9
  38.7 1.4 %collective-permute-done.9.refs_2_ = bf16[144,1024]{1,0:T(8,128)(2,1)S(1)} collective-permute-done((bf16[144,1024]{1,0:T(8,128)(2,1)S(1)}, bf16[144,1024]{1,0:T(8,128)(2,1)S(1)}, u32[]{:S(2)}, u32[]{:S(2)}) %collective-permute-start.9) | collective-permute-done | bytes 294944 | tf_op jit(solution)/shard_map/ppermute | solution.py:57
  40.2 5.7 %shard_map.30 = (f32[8,48,128]{2,1,0:T(8,128)S(1)}, f32[8,48,128]{2,1,0:T(8,128)S(1)}) custom-call(s32[4]{0:T(128)S(1)} %pad_add_fusion.where, bf16[64,64,1024]{2,1,0:T(8,128)(2,1)S(1)} %get-tuple-element.17.refs_0_, bf16[144,1024]{1,0:T(8,128)(2,1)S(1)} %collective-permute-done.5.refs_1_, ...), custom_call_target="tpu_custom_call", output_to_operand_aliasing={{0}: (4, {}), {1}: (5, {})} | custom-call | flops 2415919104 | bytes 1048576 | tf_op jit(solution)/shard_map/pallas_call | solution.py:189
  45.9 0.2 collective-permute-start.10
  46.1 1.3 %collective-permute-done.10.theirs = f32[8,48,128]{2,1,0:T(8,128)S(1)} collective-permute-done((f32[8,48,128]{2,1,0:T(8,128)S(1)}, f32[8,48,128]{2,1,0:T(8,128)S(1)}, u32[]{:S(2)}, u32[]{:S(2)}) %collective-permute-start.10) | collective-permute-done | bytes 196640 | tf_op jit(solution)/shard_map/ppermute | solution.py:57
  47.4 14.9 %all_to_all.5.shares = f32[8,48,128]{2,1,0:T(8,128)S(1)} all-to-all(f32[8,48,128]{2,1,0:T(8,128)S(1)} %shard_map.31), channel_id=1, replica_groups={{0,2,4,6,8,10,12,14},{1,3,5,7,9,11,13,15},{16,18,20,22,24,26,28,30},{17..., dimensions={0} | all-to-all | bytes 393216 | tf_op jit(solution)/shard_map/all_to_all | solution.py:260
  62.3 0.7 %shard_map.32 = bf16[64,96]{1,0:T(8,128)(2,1)} custom-call(f32[8,48,128]{2,1,0:T(8,128)S(1)} %all_to_all.5.shares), custom_call_target="tpu_custom_call" | custom-call | tf_op jit(solution)/shard_map/pallas_call | solution.py:261
  (10 shorter events, 0.1 us)
Async XLA Ops:
  0.0 11.4 %collective-permute-start.1 = (bf16[96,1024]{1,0:T(8,128)(2,1)}, bf16[96,1024]{1,0:T(8,128)(2,1)S(1)}, u32[]{:S(2)}, u32[]{:S(2)}) collective-permute-start(bf16[96,1024]{1,0:T(8,128)(2,1)} %param.3), channel_id=1, source_target_pairs={{0,64},{1,193},{16,80},{17,209},{2,66},{3,195},{18,82},{19,211},{4... | collective-permute-start | bytes 589832 | tf_op jit(solution)/shard_map/ppermute | solution.py:49
  3.3 8.2 %collective-permute-start = (bf16[96,1024]{1,0:T(8,128)(2,1)}, bf16[96,1024]{1,0:T(8,128)(2,1)S(1)}, u32[]{:S(2)}, u32[]{:S(2)}) collective-permute-start(bf16[96,1024]{1,0:T(8,128)(2,1)} %param.3), channel_id=1, source_target_pairs={{0,32},{1,225},{16,48},{17,241},{2,34},{3,227},{18,50},{19,243},{4... | collective-permute-start | bytes 589832 | tf_op jit(solution)/shard_map/ppermute | solution.py:49
  11.5 8.5 %collective-permute-start.2 = (bf16[240,1024]{1,0:T(8,128)(2,1)S(1)}, bf16[240,1024]{1,0:T(8,128)(2,1)S(1)}, u32[]{:S(2)}, u32[]{:S(2)}) collective-permute-start(bf16[240,1024]{1,0:T(8,128)(2,1)S(1)} %pad_maximum_fusion.refs_1_), channel_id=1, source_target_pairs={{0,1},{1,0},{16,17},{17,16},{2,3},{3,2},{18,19},{19,18},{4,5},{5,4... | collective-permute-start | bytes 1474568 | tf_op jit(solution)/shard_map/ppermute | solution.py:57
  11.7 16.2 %collective-permute-start.7 = (bf16[240,1024]{1,0:T(8,128)(2,1)S(1)}, bf16[240,1024]{1,0:T(8,128)(2,1)S(1)}, u32[]{:S(2)}, u32[]{:S(2)}) collective-permute-start(bf16[240,1024]{1,0:T(8,128)(2,1)S(1)} %pad_maximum_fusion.refs_1_), channel_id=1, source_target_pairs={{0,16},{1,19},{16,2},{17,1},{2,18},{3,17},{18,0},{19,3},{4,20},{5,... | collective-permute-start | bytes 1474568 | tf_op jit(solution)/shard_map/ppermute | solution.py:53
  13.2 14.7 %collective-permute-start.4 = (bf16[48,1024]{1,0:T(8,128)(2,1)S(1)}, bf16[48,1024]{1,0:T(8,128)(2,1)S(1)}, u32[]{:S(2)}, u32[]{:S(2)}) collective-permute-start(bf16[48,1024]{1,0:T(8,128)(2,1)S(1)} %constant_dynamic-slice_fusion), channel_id=1, source_target_pairs={{0,64},{1,193},{16,80},{17,209},{2,66},{3,195},{18,82},{19,211},{4... | collective-permute-start | bytes 294920 | tf_op jit(solution)/shard_map/ppermute | solution.py:49
  17.7 10.2 %collective-permute-start.3 = (bf16[96,1024]{1,0:T(8,128)(2,1)S(1)}, bf16[96,1024]{1,0:T(8,128)(2,1)S(1)}, u32[]{:S(2)}, u32[]{:S(2)}) collective-permute-start(bf16[96,1024]{1,0:T(8,128)(2,1)S(1)} %collective-permute-done.1), channel_id=1, source_target_pairs={{0,32},{1,225},{16,48},{17,241},{2,34},{3,227},{18,50},{19,243},{4... | collective-permute-start | bytes 589832 | tf_op jit(solution)/shard_map/ppermute | solution.py:49
  27.9 2.4 %collective-permute-start.8 = (bf16[240,1024]{1,0:T(8,128)(2,1)S(1)}, bf16[240,1024]{1,0:T(8,128)(2,1)S(1)}, u32[]{:S(2)}, u32[]{:S(2)}) collective-permute-start(bf16[240,1024]{1,0:T(8,128)(2,1)S(1)} %collective-permute-done.7.refs_3_), channel_id=1, source_target_pairs={{0,1},{1,0},{16,17},{17,16},{2,3},{3,2},{18,19},{19,18},{4,5},{5,4... | collective-permute-start | bytes 1474568 | tf_op jit(solution)/shard_map/ppermute | solution.py:57
  28.0 2.2 %collective-permute-start.6 = (bf16[144,1024]{1,0:T(8,128)(2,1)S(1)}, bf16[144,1024]{1,0:T(8,128)(2,1)S(1)}, u32[]{:S(2)}, u32[]{:S(2)}) collective-permute-start(bf16[144,1024]{1,0:T(8,128)(2,1)S(1)} %constant_dynamic-update-slice_fusion.refs_1_), channel_id=1, source_target_pairs={{0,1},{1,0},{16,17},{17,16},{2,3},{3,2},{18,19},{19,18},{4,5},{5,4... | collective-permute-start | bytes 884744 | tf_op jit(solution)/shard_map/ppermute | solution.py:57
  28.6 9.9 %collective-permute-start.5 = (bf16[144,1024]{1,0:T(8,128)(2,1)S(1)}, bf16[144,1024]{1,0:T(8,128)(2,1)S(1)}, u32[]{:S(2)}, u32[]{:S(2)}) collective-permute-start(bf16[144,1024]{1,0:T(8,128)(2,1)S(1)} %constant_dynamic-update-slice_fusion.refs_1_), channel_id=1, source_target_pairs={{0,16},{1,19},{16,2},{17,1},{2,18},{3,17},{18,0},{19,3},{4,20},{5,... | collective-permute-start | bytes 884744 | tf_op jit(solution)/shard_map/ppermute | solution.py:53
  38.5 1.7 %collective-permute-start.9 = (bf16[144,1024]{1,0:T(8,128)(2,1)S(1)}, bf16[144,1024]{1,0:T(8,128)(2,1)S(1)}, u32[]{:S(2)}, u32[]{:S(2)}) collective-permute-start(bf16[144,1024]{1,0:T(8,128)(2,1)S(1)} %collective-permute-done.5.refs_1_), channel_id=1, source_target_pairs={{0,1},{1,0},{16,17},{17,16},{2,3},{3,2},{18,19},{19,18},{4,5},{5,4... | collective-permute-start | bytes 884744 | tf_op jit(solution)/shard_map/ppermute | solution.py:57
  45.9 1.5 %collective-permute-start.10 = (f32[8,48,128]{2,1,0:T(8,128)S(1)}, f32[8,48,128]{2,1,0:T(8,128)S(1)}, u32[]{:S(2)}, u32[]{:S(2)}) collective-permute-start(f32[8,48,128]{2,1,0:T(8,128)S(1)} %get-tuple-element.28), channel_id=1, source_target_pairs={{0,1},{1,0},{16,17},{17,16},{2,3},{3,2},{18,19},{19,18},{4,5},{5,4... | collective-permute-start | bytes 589832 | tf_op jit(solution)/shard_map/ppermute | solution.py:57

commit v2 on v1

--- a/solution.py
+++ b/solution.py
@@ -15,8 +15,6 @@
 K_INP = 64
 K_STEP = 32
 TILE = 256
-NEAR = (0, 1, 2, -1, -2)
-FAR = (3, -3, 4)
 VMEM = pl.BlockSpec(memory_space=pltpu.VMEM)
 SMEM = pl.BlockSpec(memory_space=pltpu.SMEM)
 HBM = pl.BlockSpec(memory_space=pltpu.HBM)
@@ -73,29 +71,10 @@
     return jnp.concatenate([packed[:, 0:96], last], axis=0)
 
 
-def place_group(cells, start, shards, mine, theirs, core):
-    source = [0, 0]
-    for n, d in enumerate(shards):
-        at = start + n * BLOCK
-        if d in (0, 4):
-            for which, piece in enumerate((mine, theirs)):
-                half = core if which == 0 else 1 - core
-                first = 0 if d == 0 else BLOCK
-                spot = pl.multiple_of(at + half * HALF, 16)
-                cells[pl.ds(spot, HALF), :] = piece[first : first + HALF, :]
-                if d == 0:
-                    source[which] = HALF
-        else:
-            which, piece = (0, mine) if d > 0 else (1, theirs)
-            first = source[which]
-            cells[at : at + BLOCK, :] = piece[first : first + BLOCK, :]
-            source[which] = first + BLOCK
-
-
-def collide(groups, first_call, where, *refs):
+def collide(plan, first_call, n_pieces, where, *refs):
     refs = list(refs)
     tensor_in = refs.pop(0)
-    pieces = [(refs.pop(0), refs.pop(0)) for _ in groups]
+    pieces, refs = refs[:n_pieces], refs[n_pieces:]
     if first_call:
         give, keep, tensor, cells, weight, total, arrived = refs
         copies = [
@@ -111,16 +90,20 @@
         _, _, give, keep, cells, weight, total = refs
         copies = None
     first, z, odd, core = where[0], where[1], where[2], where[3]
-    start = 0
-    for (shards, _), (mine, theirs) in zip(groups, pieces):
-        place_group(cells, start, shards, mine, theirs, core)
-        start += BLOCK * len(shards)
+    for n, (_, _, parts) in enumerate(plan):
+        for piece, source, count, half in parts:
+            at = n * BLOCK
+            if half is not None:
+                at = pl.multiple_of(at + (core if half == 0 else 1 - core) * HALF, 16)
+            cells[pl.ds(at, count), :] = pieces[piece][source : source + count, :]
     base = pl.multiple_of((first // 128) * 128, 128)
     weight[...] = cells[:, pl.ds(base, 128)].astype(jnp.float32).T
     off = pl.multiple_of(lax.rem(first, 128), K_INP)
     size = cells.shape[0]
 
-    def step(k):
+    for k in range(0, K_OUT, K_STEP):
+        if copies is not None:
+            copies[k // K_STEP].wait()
         left = tensor[pl.ds(k, K_STEP)].reshape(K_STEP * K_INP, tensor.shape[2])
         for c in range(0, size, TILE):
             w = min(TILE, size - c)
@@ -135,43 +118,25 @@
                 inner.reshape(K_STEP, K_INP, w) * chosen[None], axis=1
             )
 
-    if copies is None:
-
-        def body(s, carry):
-            step(pl.multiple_of(s * K_STEP, K_STEP))
-            return carry
-
-        lax.fori_loop(0, K_OUT // K_STEP, body, 0)
-    else:
-        for n, copy in enumerate(copies):
-            copy.wait()
-            step(n * K_STEP)
-
-    at = 0
-    for shards, own in groups:
+    for n, (d, own, _) in enumerate(plan):
         kept = (odd == core) if own else (odd != core)
-        blocks = []
-        for d in shards:
-            owner = lax.rem(z - d * (1 - 2 * core) + NZ, NZ)
-            blocks.append((owner, pack(total[:, at : at + BLOCK])))
-            at += BLOCK
+        owner = lax.rem(z - d * (1 - 2 * core) + NZ, NZ)
+        block = pack(total[:, n * BLOCK : (n + 1) * BLOCK])
 
         @pl.when(kept)
-        def _():
-            for owner, block in blocks:
-                keep[owner] = block
+        def _(block=block, owner=owner):
+            keep[owner] = block
 
         @pl.when(jnp.logical_not(kept))
-        def _():
-            for owner, block in blocks:
-                give[owner] = block
-
-
-def partial_sums(groups, where, tensor, pieces, before):
-    size = BLOCK * sum(len(shards) for shards, _ in groups)
+        def _(block=block, owner=owner):
+            give[owner] = block
+
+
+def partial_sums(plan, where, tensor, pieces, before):
+    size = BLOCK * len(plan)
     first_call = before is None
-    args = [where, tensor] + [piece for pair in pieces for piece in pair]
-    in_specs = [SMEM, HBM if first_call else VMEM] + [VMEM] * (len(args) - 2)
+    args = [where, tensor, *pieces]
+    in_specs = [SMEM, HBM if first_call else VMEM] + [VMEM] * len(pieces)
     part = jax.ShapeDtypeStruct((NZ, 48, 128), jnp.float32)
     out_shape, aliases = [part, part], {}
     scratch = [
@@ -187,19 +152,29 @@
         args += before
         in_specs += [VMEM, VMEM]
     return pl.pallas_call(
-        functools.partial(collide, groups, first_call),
+        functools.partial(collide, plan, first_call, len(pieces)),
         in_specs=in_specs,
         out_specs=[VMEM] * len(out_shape),
         out_shape=out_shape,
         input_output_aliases=aliases,
         scratch_shapes=scratch,
-        compiler_params=pltpu.CompilerParams(vmem_limit_bytes=(42 if first_call else 24) << 20),
+        compiler_params=pltpu.CompilerParams(
+            vmem_limit_bytes=(42 if first_call else 24) << 20
+        ),
         cost_estimate=pl.CostEstimate(
             flops=2 * K_OUT * K_INP * 1024 * size,
-            bytes_accessed=1 << 20,
+            bytes_accessed=tensor.size * 4 if first_call else 1 << 20,
             transcendentals=0,
         ),
     )(*args)
+
+
+def whole(piece, source=0):
+    return ((piece, source, BLOCK, None),)
+
+
+def halves(mine, theirs, source):
+    return ((mine, source, HALF, 0), (theirs, source, HALF, 1))
 
 
 def add_pair(mine, theirs, out):
@@ -220,32 +195,45 @@
 
     one = along_z(state, 1)
     two = along_z(state, 2)
-    near = rows(half(state), one, two)
+    give, keep, held = partial_sums(((0, True, whole(0)),), where, tensor, [state], None)
+
     three = along_z(two, 1)
     four = along_z(half(two), 2)
-    near_x = along_x(near)
-    near_swap = swap(near)
-    give, keep, held = partial_sums(
-        ((NEAR, True),), where, tensor, [(near, near_swap)], None
-    )
+    near_x = along_x(rows(state, one, two))
+    near_swap = swap(rows(one, two))
+    plan = ((1, True, whole(0)), (2, True, whole(1)))
+    give, keep = partial_sums(plan, where, held, [one, two], [give, keep])
 
     three, four, give = lax.optimization_barrier((three, four, give))
     far = rows(three, four)
     far_x = along_x(far)
     far_swap = swap(far)
-    near_x_swap = swap(near_x)
+    near_x_swap = swap(near_x[BLOCK:])
+    plan = (
+        (-1, True, whole(0)),
+        (-2, True, whole(0, BLOCK)),
+        (3, True, whole(1)),
+        (-3, True, whole(2)),
+        (4, True, halves(1, 2, BLOCK)),
+        (0, False, whole(3)),
+        (1, False, whole(3, BLOCK)),
+        (2, False, whole(3, 2 * BLOCK)),
+    )
     give, keep = partial_sums(
-        ((FAR, True), (NEAR, False)),
-        where,
-        held,
-        [(far, far_swap), (near_x, near_x_swap)],
-        [give, keep],
+        plan, where, held, [near_swap, far, far_swap, near_x], [give, keep]
     )
 
     far_x, give = lax.optimization_barrier((far_x, give))
     far_x_swap = swap(far_x)
+    plan = (
+        (-1, False, whole(0)),
+        (-2, False, whole(0, BLOCK)),
+        (3, False, whole(1)),
+        (-3, False, whole(2)),
+        (4, False, halves(1, 2, BLOCK)),
+    )
     give, keep = partial_sums(
-        ((FAR, False),), where, held, [(far_x, far_x_swap)], [give, keep]
+        plan, where, held, [near_x_swap, far_x, far_x_swap], [give, keep]
     )
 
     got = swap(give)

time: 63.1 us -> 61.7 us (0.978); the launches traced: 63 us -> 60.8 us
  starting transfers between devices: 17.4 us -> 13.5 us
  Pallas kernels: 22.5 us -> 26.1 us
  waiting for transfers between devices: 7.03 us -> 5.69 us
  blocking collectives: 14.9 us -> 14.2 us
    ppermute x4, starting transfers between devices: 13.2 us -> 8.97 us  [along_z(): return lax.ppermute(array, AXES, hop(lambda c: (0, 0, d * sign(c), 0)))]
    pallas_call x3 -> x4, Pallas kernels: 21.8 us -> 25.4 us  [partial_sums(): pl.pallas_call(functools.partial(collide, plan, first_call, len(pieces)),...]
    ppermute x4, waiting for transfers between devices: 4.13 us -> 1.25 us  [along_z(): return lax.ppermute(array, AXES, hop(lambda c: (0, 0, d * sign(c), 0)))]
    ppermute x2, waiting for transfers between devices: 0.01 us -> 2.16 us  [along_x(): return lax.ppermute(array, AXES, hop(lambda c: (sign(c), 0, 0, 0)))]
    unnamed x1 -> x3, local copies, waits for them, and re-layouts: 0.01 us -> 0.94 us
    dynamic_slice x2 -> x1, local copies, waits for them, and re-layouts: 0.94 us -> 0.02 us  [half(): return lax.dynamic_slice_in_dim(array, core * HALF, HALF, 0)]
    all_to_all x1, blocking collectives: 14.9 us -> 14.2 us  [local(): lax.all_to_all(pair, 'inp', 0, 0, tiled=True, axis_index_groups=groups)]
  transfers between devices with their start and end apart: 11 -> 11, of which waited for: 4 -> 4; matrix products, arithmetic and copies ran while one was open for 2% -> 0% of each run, Pallas kernels for 25% -> 32%
where the time goes in v2:
time: 61.7 us; the launch traced here: 60.8 us
  Pallas kernels  26.1 us (42%)
  blocking collectives  14.2 us (23%)
  starting transfers between devices  13.5 us (22%)
  waiting for transfers between devices  5.69 us (9%)
  local copies, waits for them, and re-layouts  0.99 us (2%)
    pallas_call x4, Pallas kernels, partial_sums(): pl.pallas_call(functools.partial(collide, plan, first_call, len(pieces)),...  25.4 us
    all_to_all x1, blocking collectives, local(): lax.all_to_all(pair, 'inp', 0, 0, tiled=True, axis_index_groups=groups)  14.2 us
    ppermute x4, starting transfers between devices, along_z(): return lax.ppermute(array, AXES, hop(lambda c: (0, 0, d * sign(c), 0)))  8.97 us
    ppermute x2, starting transfers between devices, along_x(): return lax.ppermute(array, AXES, hop(lambda c: (sign(c), 0, 0, 0)))  3.14 us
    ppermute x5, waiting for transfers between devices, swap(): return lax.ppermute(array, AXES, hop(lambda c: (0, 0, 0, 1)))  2.29 us
    ppermute x2, waiting for transfers between devices, along_x(): return lax.ppermute(array, AXES, hop(lambda c: (sign(c), 0, 0, 0)))  2.16 us
    ppermute x5, starting transfers between devices, swap(): return lax.ppermute(array, AXES, hop(lambda c: (0, 0, 0, 1)))  1.41 us
    ppermute x4, waiting for transfers between devices, along_z(): return lax.ppermute(array, AXES, hop(lambda c: (0, 0, d * sign(c), 0)))  1.25 us
  transfers between devices with their start and end apart: 11, of which 4 were waited for; matrix products, arithmetic and copies ran while one was open for 0% of the time, Pallas kernels for 32%

profile of v2, /device:TPU:32, one launch (start us, length us, event | category | flops | bytes accessed | tf_op | source)
XLA Modules:
  0.0 60.8 jit_solution(6732052184154282950)
XLA Ops:
  0.0 3.3 %collective-permute-start.1 = (bf16[96,1024]{1,0:T(8,128)(2,1)}, bf16[96,1024]{1,0:T(8,128)(2,1)S(1)}, u32[]{:S(2)}, u32[]{:S(2)}) collective-permute-start(bf16[96,1024]{1,0:T(8,128)(2,1)} %refs_1_.1), channel_id=1, source_target_pairs={{0,64},{1,193},{16,80},{17,209},{2,66},{3,195},{18,82},{19,211},{4... | collective-permute-start | bytes 589832 | tf_op jit(solution)/shard_map/ppermute | solution.py:47
  3.3 3.1 %collective-permute-start = (bf16[96,1024]{1,0:T(8,128)(2,1)}, bf16[96,1024]{1,0:T(8,128)(2,1)S(1)}, u32[]{:S(2)}, u32[]{:S(2)}) collective-permute-start(bf16[96,1024]{1,0:T(8,128)(2,1)} %refs_1_.1), channel_id=1, source_target_pairs={{0,32},{1,225},{16,48},{17,241},{2,34},{3,227},{18,50},{19,243},{4... | collective-permute-start | bytes 589832 | tf_op jit(solution)/shard_map/ppermute | solution.py:47
  6.4 0.1 pad_add_fusion.where
  6.5 0.9 %copy-done = bf16[96,1024]{1,0:T(8,128)(2,1)S(1)} copy-done((bf16[96,1024]{1,0:T(8,128)(2,1)S(1)}, bf16[96,1024]{1,0:T(8,128)(2,1)}, u32[]{:S(2)}) %copy-start) | copy-done | bytes 196632
  7.4 7.6 %shard_map.28 = (f32[8,48,128]{2,1,0:T(8,128)S(1)}, f32[8,48,128]{2,1,0:T(8,128)S(1)}, bf16[64,64,1024]{2,1,0:T(8,128)(2,1)S(1)}) custom-call(s32[4]{0:T(128)S(1)} %pad_add_fusion.where, bf16[64,64,1024]{2,1,0:T(8,128)(2,1)} %refs_0_.1, bf16[96,1024]{1,0:T(8,128)(2,1)S(1)} %copy-done), custom_call_target="tpu_custom_call" | custom-call | flops 805306368 | bytes 16777216 | tf_op jit(solution)/shard_map/pallas_call | solution.py:154
  15.0 0.0 collective-permute-done.1.refs_2_
  15.0 1.5 %collective-permute-start.5 = (bf16[48,1024]{1,0:T(8,128)(2,1)S(1)}, bf16[48,1024]{1,0:T(8,128)(2,1)S(1)}, u32[]{:S(2)}, u32[]{:S(2)}) collective-permute-start(bf16[48,1024]{1,0:T(8,128)(2,1)S(1)} %constant_dynamic-slice_fusion), channel_id=1, source_target_pairs={{0,64},{1,193},{16,80},{17,209},{2,66},{3,195},{18,82},{19,211},{4... | collective-permute-start | bytes 294920 | tf_op jit(solution)/shard_map/ppermute | solution.py:47
  16.6 1.6 %collective-permute-start.2 = (bf16[288,1024]{1,0:T(8,128)(2,1)S(1)}, bf16[288,1024]{1,0:T(8,128)(2,1)S(1)}, u32[]{:S(2)}, u32[]{:S(2)}) collective-permute-start(bf16[288,1024]{1,0:T(8,128)(2,1)S(1)} %pad_maximum_fusion), channel_id=1, source_target_pairs={{0,16},{1,19},{16,2},{17,1},{2,18},{3,17},{18,0},{19,3},{4,20},{5,... | collective-permute-start | bytes 1769480 | tf_op jit(solution)/shard_map/ppermute | solution.py:51
  18.2 1.0 %collective-permute-start.4 = (bf16[96,1024]{1,0:T(8,128)(2,1)S(1)}, bf16[96,1024]{1,0:T(8,128)(2,1)S(1)}, u32[]{:S(2)}, u32[]{:S(2)}) collective-permute-start(bf16[96,1024]{1,0:T(8,128)(2,1)S(1)} %collective-permute-done.1.refs_2_), channel_id=1, source_target_pairs={{0,32},{1,225},{16,48},{17,241},{2,34},{3,227},{18,50},{19,243},{4... | collective-permute-start | bytes 589832 | tf_op jit(solution)/shard_map/ppermute | solution.py:47
  19.2 0.1 collective-permute-start.7
  19.3 3.3 %shard_map.29 = (f32[8,48,128]{2,1,0:T(8,128)S(1)}, f32[8,48,128]{2,1,0:T(8,128)S(1)}) custom-call(s32[4]{0:T(128)S(1)} %pad_add_fusion.where, bf16[64,64,1024]{2,1,0:T(8,128)(2,1)S(1)} %get-tuple-element.19.refs_0_, bf16[96,1024]{1,0:T(8,128)(2,1)S(1)} %collective-permute-done.refs_1_, ...), custom_call_target="tpu_custom_call", output_to_operand_aliasing={{0}: (4, {}), {1}: (5, {})} | custom-call | flops 1610612736 | bytes 1048576 | tf_op jit(solution)/shard_map/pallas_call | solution.py:154
  22.7 1.2 %collective-permute-done.4 = bf16[96,1024]{1,0:T(8,128)(2,1)S(1)} collective-permute-done((bf16[96,1024]{1,0:T(8,128)(2,1)S(1)}, bf16[96,1024]{1,0:T(8,128)(2,1)S(1)}, u32[]{:S(2)}, u32[]{:S(2)}) %collective-permute-start.4) | collective-permute-done | bytes 196640 | tf_op jit(solution)/shard_map/ppermute | solution.py:47
  23.9 0.1 collective-permute-start.8
  24.0 1.6 %collective-permute-start.6 = (bf16[144,1024]{1,0:T(8,128)(2,1)S(1)}, bf16[144,1024]{1,0:T(8,128)(2,1)S(1)}, u32[]{:S(2)}, u32[]{:S(2)}) collective-permute-start(bf16[144,1024]{1,0:T(8,128)(2,1)S(1)} %constant_dynamic-update-slice_fusion.refs_2_), channel_id=1, source_target_pairs={{0,16},{1,19},{16,2},{17,1},{2,18},{3,17},{18,0},{19,3},{4,20},{5,... | collective-permute-start | bytes 884744 | tf_op jit(solution)/shard_map/ppermute | solution.py:51
  25.6 2.2 %collective-permute-done.2.refs_4_ = bf16[288,1024]{1,0:T(8,128)(2,1)S(1)} collective-permute-done((bf16[288,1024]{1,0:T(8,128)(2,1)S(1)}, bf16[288,1024]{1,0:T(8,128)(2,1)S(1)}, u32[]{:S(2)}, u32[]{:S(2)}) %collective-permute-start.2) | collective-permute-done | bytes 589856 | tf_op jit(solution)/shard_map/ppermute | solution.py:51
  27.8 0.3 collective-permute-start.3
  28.1 8.5 %shard_map.30 = (f32[8,48,128]{2,1,0:T(8,128)S(1)}, f32[8,48,128]{2,1,0:T(8,128)S(1)}) custom-call(s32[4]{0:T(128)S(1)} %pad_add_fusion.where, bf16[64,64,1024]{2,1,0:T(8,128)(2,1)S(1)} %get-tuple-element.19.refs_0_, bf16[192,1024]{1,0:T(8,128)(2,1)S(1)} %collective-permute-done.7.refs_1_, ...), custom_call_target="tpu_custom_call", output_to_operand_aliasing={{0}: (6, {}), {1}: (7, {})} | custom-call | flops 6442450944 | bytes 1048576 | tf_op jit(solution)/shard_map/pallas_call | solution.py:154
  36.6 0.6 collective-permute-start.9
  37.2 1.2 %collective-permute-done.9.refs_3_ = bf16[144,1024]{1,0:T(8,128)(2,1)S(1)} collective-permute-done((bf16[144,1024]{1,0:T(8,128)(2,1)S(1)}, bf16[144,1024]{1,0:T(8,128)(2,1)S(1)}, u32[]{:S(2)}, u32[]{:S(2)}) %collective-permute-start.9) | collective-permute-done | bytes 294944 | tf_op jit(solution)/shard_map/ppermute | solution.py:55
  38.4 6.0 %shard_map.31 = (f32[8,48,128]{2,1,0:T(8,128)S(1)}, f32[8,48,128]{2,1,0:T(8,128)S(1)}) custom-call(s32[4]{0:T(128)S(1)} %pad_add_fusion.where, bf16[64,64,1024]{2,1,0:T(8,128)(2,1)S(1)} %get-tuple-element.19.refs_0_, bf16[192,1024]{1,0:T(8,128)(2,1)S(1)} %collective-permute-done.3.refs_1_, ...), custom_call_target="tpu_custom_call", output_to_operand_aliasing={{0}: (5, {}), {1}: (6, {})} | custom-call | flops 4026531840 | bytes 1048576 | tf_op jit(solution)/shard_map/pallas_call | solution.py:154
  44.4 0.4 collective-permute-start.10
  44.8 1.1 %collective-permute-done.10.theirs = f32[8,48,128]{2,1,0:T(8,128)S(1)} collective-permute-done((f32[8,48,128]{2,1,0:T(8,128)S(1)}, f32[8,48,128]{2,1,0:T(8,128)S(1)}, u32[]{:S(2)}, u32[]{:S(2)}) %collective-permute-start.10) | collective-permute-done | bytes 196640 | tf_op jit(solution)/shard_map/ppermute | solution.py:55
  45.9 14.2 %all_to_all.5.shares = f32[8,48,128]{2,1,0:T(8,128)S(1)} all-to-all(f32[8,48,128]{2,1,0:T(8,128)S(1)} %shard_map.32), channel_id=1, replica_groups={{0,2,4,6,8,10,12,14},{1,3,5,7,9,11,13,15},{16,18,20,22,24,26,28,30},{17..., dimensions={0} | all-to-all | bytes 393216 | tf_op jit(solution)/shard_map/all_to_all | solution.py:248
  60.1 0.7 %shard_map.33 = bf16[64,96]{1,0:T(8,128)(2,1)} custom-call(f32[8,48,128]{2,1,0:T(8,128)S(1)} %all_to_all.5.shares), custom_call_target="tpu_custom_call" | custom-call | tf_op jit(solution)/shard_map/pallas_call | solution.py:249
  (14 shorter events, 0.2 us)
Async XLA Ops:
  0.0 15.0 %collective-permute-start.1 = (bf16[96,1024]{1,0:T(8,128)(2,1)}, bf16[96,1024]{1,0:T(8,128)(2,1)S(1)}, u32[]{:S(2)}, u32[]{:S(2)}) collective-permute-start(bf16[96,1024]{1,0:T(8,128)(2,1)} %refs_1_.1), channel_id=1, source_target_pairs={{0,64},{1,193},{16,80},{17,209},{2,66},{3,195},{18,82},{19,211},{4... | collective-permute-start | bytes 589832 | tf_op jit(solution)/shard_map/ppermute | solution.py:47
  3.3 13.3 %collective-permute-start = (bf16[96,1024]{1,0:T(8,128)(2,1)}, bf16[96,1024]{1,0:T(8,128)(2,1)S(1)}, u32[]{:S(2)}, u32[]{:S(2)}) collective-permute-start(bf16[96,1024]{1,0:T(8,128)(2,1)} %refs_1_.1), channel_id=1, source_target_pairs={{0,32},{1,225},{16,48},{17,241},{2,34},{3,227},{18,50},{19,243},{4... | collective-permute-start | bytes 589832 | tf_op jit(solution)/shard_map/ppermute | solution.py:47
  6.5 0.9 %copy-start = (bf16[96,1024]{1,0:T(8,128)(2,1)S(1)}, bf16[96,1024]{1,0:T(8,128)(2,1)}, u32[]{:S(2)}) copy-start(bf16[96,1024]{1,0:T(8,128)(2,1)} %refs_1_.1) | copy-start | bytes 589828
  15.0 7.7 %collective-permute-start.5 = (bf16[48,1024]{1,0:T(8,128)(2,1)S(1)}, bf16[48,1024]{1,0:T(8,128)(2,1)S(1)}, u32[]{:S(2)}, u32[]{:S(2)}) collective-permute-start(bf16[48,1024]{1,0:T(8,128)(2,1)S(1)} %constant_dynamic-slice_fusion), channel_id=1, source_target_pairs={{0,64},{1,193},{16,80},{17,209},{2,66},{3,195},{18,82},{19,211},{4... | collective-permute-start | bytes 294920 | tf_op jit(solution)/shard_map/ppermute | solution.py:47
  16.6 11.2 %collective-permute-start.2 = (bf16[288,1024]{1,0:T(8,128)(2,1)S(1)}, bf16[288,1024]{1,0:T(8,128)(2,1)S(1)}, u32[]{:S(2)}, u32[]{:S(2)}) collective-permute-start(bf16[288,1024]{1,0:T(8,128)(2,1)S(1)} %pad_maximum_fusion), channel_id=1, source_target_pairs={{0,16},{1,19},{16,2},{17,1},{2,18},{3,17},{18,0},{19,3},{4,20},{5,... | collective-permute-start | bytes 1769480 | tf_op jit(solution)/shard_map/ppermute | solution.py:51
  18.2 5.7 %collective-permute-start.4 = (bf16[96,1024]{1,0:T(8,128)(2,1)S(1)}, bf16[96,1024]{1,0:T(8,128)(2,1)S(1)}, u32[]{:S(2)}, u32[]{:S(2)}) collective-permute-start(bf16[96,1024]{1,0:T(8,128)(2,1)S(1)} %collective-permute-done.1.refs_2_), channel_id=1, source_target_pairs={{0,32},{1,225},{16,48},{17,241},{2,34},{3,227},{18,50},{19,243},{4... | collective-permute-start | bytes 589832 | tf_op jit(solution)/shard_map/ppermute | solution.py:47
  19.2 8.9 %collective-permute-start.7 = (bf16[192,1024]{1,0:T(8,128)(2,1)S(1)}, bf16[192,1024]{1,0:T(8,128)(2,1)S(1)}, u32[]{:S(2)}, u32[]{:S(2)}) collective-permute-start(bf16[192,1024]{1,0:T(8,128)(2,1)S(1)} %pad_maximum_fusion.1), channel_id=1, source_target_pairs={{0,1},{1,0},{16,17},{17,16},{2,3},{3,2},{18,19},{19,18},{4,5},{5,4... | collective-permute-start | bytes 1179656 | tf_op jit(solution)/shard_map/ppermute | solution.py:55
  23.9 4.1 %collective-permute-start.8 = (bf16[144,1024]{1,0:T(8,128)(2,1)S(1)}, bf16[144,1024]{1,0:T(8,128)(2,1)S(1)}, u32[]{:S(2)}, u32[]{:S(2)}) collective-permute-start(bf16[144,1024]{1,0:T(8,128)(2,1)S(1)} %constant_dynamic-update-slice_fusion.refs_2_), channel_id=1, source_target_pairs={{0,1},{1,0},{16,17},{17,16},{2,3},{3,2},{18,19},{19,18},{4,5},{5,4... | collective-permute-start | bytes 884744 | tf_op jit(solution)/shard_map/ppermute | solution.py:55
  24.0 12.5 %collective-permute-start.6 = (bf16[144,1024]{1,0:T(8,128)(2,1)S(1)}, bf16[144,1024]{1,0:T(8,128)(2,1)S(1)}, u32[]{:S(2)}, u32[]{:S(2)}) collective-permute-start(bf16[144,1024]{1,0:T(8,128)(2,1)S(1)} %constant_dynamic-update-slice_fusion.refs_2_), channel_id=1, source_target_pairs={{0,16},{1,19},{16,2},{17,1},{2,18},{3,17},{18,0},{19,3},{4,20},{5,... | collective-permute-start | bytes 884744 | tf_op jit(solution)/shard_map/ppermute | solution.py:51
  27.8 10.6 %collective-permute-start.3 = (bf16[192,1024]{1,0:T(8,128)(2,1)S(1)}, bf16[192,1024]{1,0:T(8,128)(2,1)S(1)}, u32[]{:S(2)}, u32[]{:S(2)}) collective-permute-start(bf16[192,1024]{1,0:T(8,128)(2,1)S(1)} %slice.4), channel_id=1, source_target_pairs={{0,1},{1,0},{16,17},{17,16},{2,3},{3,2},{18,19},{19,18},{4,5},{5,4... | collective-permute-start | bytes 1179656 | tf_op jit(solution)/shard_map/ppermute | solution.py:55
  36.6 1.8 %collective-permute-start.9 = (bf16[144,1024]{1,0:T(8,128)(2,1)S(1)}, bf16[144,1024]{1,0:T(8,128)(2,1)S(1)}, u32[]{:S(2)}, u32[]{:S(2)}) collective-permute-start(bf16[144,1024]{1,0:T(8,128)(2,1)S(1)} %collective-permute-done.6.refs_2_), channel_id=1, source_target_pairs={{0,1},{1,0},{16,17},{17,16},{2,3},{3,2},{18,19},{19,18},{4,5},{5,4... | collective-permute-start | bytes 884744 | tf_op jit(solution)/shard_map/ppermute | solution.py:55
  44.4 1.5 %collective-permute-start.10 = (f32[8,48,128]{2,1,0:T(8,128)S(1)}, f32[8,48,128]{2,1,0:T(8,128)S(1)}, u32[]{:S(2)}, u32[]{:S(2)}) collective-permute-start(f32[8,48,128]{2,1,0:T(8,128)S(1)} %get-tuple-element.32), channel_id=1, source_target_pairs={{0,1},{1,0},{16,17},{17,16},{2,3},{3,2},{18,19},{19,18},{4,5},{5,4... | collective-permute-start | bytes 589832 | tf_op jit(solution)/shard_map/ppermute | solution.py:55

commit v3 on v2

--- a/solution.py
+++ b/solution.py
@@ -78,17 +78,16 @@
     if first_call:
         give, keep, tensor, cells, weight, total, arrived = refs
         copies = [
-            pltpu.make_async_copy(
-                tensor_in.at[pl.ds(k, K_STEP)], tensor.at[pl.ds(k, K_STEP)], arrived.at[k // K_STEP]
-            )
-            for k in range(0, K_OUT, K_STEP)
+            pltpu.make_async_copy(pieces[0], cells, arrived.at[0]),
+            pltpu.make_async_copy(tensor_in, tensor, arrived.at[1]),
         ]
         for copy in copies:
             copy.start()
+        for copy in copies:
+            copy.wait()
     else:
         tensor = tensor_in
         _, _, give, keep, cells, weight, total = refs
-        copies = None
     first, z, odd, core = where[0], where[1], where[2], where[3]
     for n, (_, _, parts) in enumerate(plan):
         for piece, source, count, half in parts:
@@ -102,8 +101,6 @@
     size = cells.shape[0]
 
     for k in range(0, K_OUT, K_STEP):
-        if copies is not None:
-            copies[k // K_STEP].wait()
         left = tensor[pl.ds(k, K_STEP)].reshape(K_STEP * K_INP, tensor.shape[2])
         for c in range(0, size, TILE):
             w = min(TILE, size - c)
@@ -136,7 +133,7 @@
     size = BLOCK * len(plan)
     first_call = before is None
     args = [where, tensor, *pieces]
-    in_specs = [SMEM, HBM if first_call else VMEM] + [VMEM] * len(pieces)
+    in_specs = [SMEM] + [HBM if first_call else VMEM] * (1 + len(pieces))
     part = jax.ShapeDtypeStruct((NZ, 48, 128), jnp.float32)
     out_shape, aliases = [part, part], {}
     scratch = [
@@ -146,7 +143,7 @@
     ]
     if first_call:
         out_shape.append(jax.ShapeDtypeStruct(tensor.shape, tensor.dtype))
-        scratch.append(pltpu.SemaphoreType.DMA((K_OUT // K_STEP,)))
+        scratch.append(pltpu.SemaphoreType.DMA((2,)))
     else:
         aliases = {len(args): 0, len(args) + 1: 1}
         args += before
@@ -158,9 +155,7 @@
         out_shape=out_shape,
         input_output_aliases=aliases,
         scratch_shapes=scratch,
-        compiler_params=pltpu.CompilerParams(
-            vmem_limit_bytes=(42 if first_call else 24) << 20
-        ),
+        compiler_params=pltpu.CompilerParams(vmem_limit_bytes=16 << 20),
         cost_estimate=pl.CostEstimate(
             flops=2 * K_OUT * K_INP * 1024 * size,
             bytes_accessed=tensor.size * 4 if first_call else 1 << 20,
@@ -188,40 +183,48 @@
 def local(tensor, state):
     out_at, inp_at = lax.axis_index("out"), lax.axis_index("inp")
     z, odd, core = out_at // 2, out_at % 2, inp_at % 2
-    where = jnp.stack([inp_at * K_INP, z, odd, core]).astype(jnp.int32)
+    start = core * HALF
+    where = jnp.stack([inp_at * K_INP, z, odd, core, start]).astype(jnp.int32)
 
     def half(array):
-        return lax.dynamic_slice_in_dim(array, core * HALF, HALF, 0)
-
+        return lax.dynamic_slice(
+            array, (start, 0), (HALF, array.shape[1]), allow_negative_indices=False
+        )
+
+    two = along_z(state, 2)
     one = along_z(state, 1)
-    two = along_z(state, 2)
-    give, keep, held = partial_sums(((0, True, whole(0)),), where, tensor, [state], None)
-
-    three = along_z(two, 1)
-    four = along_z(half(two), 2)
-    near_x = along_x(rows(state, one, two))
-    near_swap = swap(rows(one, two))
-    plan = ((1, True, whole(0)), (2, True, whole(1)))
-    give, keep = partial_sums(plan, where, held, [one, two], [give, keep])
-
-    three, four, give = lax.optimization_barrier((three, four, give))
-    far = rows(three, four)
+    same_x = along_x(state)
+    there = [pltpu.with_memory_space_constraint(a, pltpu.HBM) for a in (tensor, state)]
+    give, keep, held = partial_sums(((0, True, ()),), where, there[0], there[1:], None)
+
+    one, two, same_x, give = lax.optimization_barrier((one, two, same_x, give))
+    near = rows(one, two)
+    near_swap = swap(near)
+    both = rows(one, half(two))
+    near, both = lax.optimization_barrier((near, both))
+    far = along_z(both, 2)
+    near_x = along_x(near)
+    plan = (
+        (1, True, whole(0)),
+        (2, True, whole(0, BLOCK)),
+        (-1, True, whole(1)),
+        (-2, True, whole(1, BLOCK)),
+        (0, False, whole(2)),
+    )
+    give, keep = partial_sums(plan, where, held, [near, near_swap, same_x], [give, keep])
+
+    far, give = lax.optimization_barrier((far, give))
     far_x = along_x(far)
     far_swap = swap(far)
-    near_x_swap = swap(near_x[BLOCK:])
+    near_x_swap = swap(near_x)
     plan = (
-        (-1, True, whole(0)),
-        (-2, True, whole(0, BLOCK)),
-        (3, True, whole(1)),
-        (-3, True, whole(2)),
-        (4, True, halves(1, 2, BLOCK)),
-        (0, False, whole(3)),
-        (1, False, whole(3, BLOCK)),
-        (2, False, whole(3, 2 * BLOCK)),
-    )
-    give, keep = partial_sums(
-        plan, where, held, [near_swap, far, far_swap, near_x], [give, keep]
-    )
+        (3, True, whole(0)),
+        (-3, True, whole(1)),
+        (4, True, halves(0, 1, BLOCK)),
+        (1, False, whole(2)),
+        (2, False, whole(2, BLOCK)),
+    )
+    give, keep = partial_sums(plan, where, held, [far, far_swap, near_x], [give, keep])
 
     far_x, give = lax.optimization_barrier((far_x, give))
     far_x_swap = swap(far_x)

time: 61.7 us -> 59 us (0.956)
  local copies, waits for them, and re-layouts: 0.99 us -> 0.12 us
  Pallas kernels: 26.1 us -> 25.3 us
    ppermute x2 -> x3, waiting for transfers between devices: 2.16 us -> 0.01 us  [along_x(): return lax.ppermute(array, AXES, hop(lambda c: (sign(c), 0, 0, 0)))]
    ppermute x4 -> x3, waiting for transfers between devices: 1.25 us -> 2.55 us  [along_z(): return lax.ppermute(array, AXES, hop(lambda c: (0, 0, d * sign(c), 0)))]
    ppermute x4 -> x3, starting transfers between devices: 8.97 us -> 7.72 us  [along_z(): return lax.ppermute(array, AXES, hop(lambda c: (0, 0, d * sign(c), 0)))]
    ppermute x2 -> x3, starting transfers between devices: 3.14 us -> 4.08 us  [along_x(): return lax.ppermute(array, AXES, hop(lambda c: (sign(c), 0, 0, 0)))]
    unnamed x3 -> x1, local copies, waits for them, and re-layouts: 0.94 us -> 0.01 us
    pallas_call x4, Pallas kernels: 25.4 us -> 24.6 us  [partial_sums(): pl.pallas_call(functools.partial(collide, plan, first_call, len(pieces)),...]
  transfers between devices with their start and end apart: 11 -> 11, of which waited for: 4 -> 3; matrix products, arithmetic and copies ran while one was open for 0% -> 0% of each run, Pallas kernels for 32% -> 32%
where the time goes in v3:
time: 59 us; the launch traced here: 58.3 us
  Pallas kernels  25.3 us (43%)
  blocking collectives  13.8 us (23%)
  starting transfers between devices  13.6 us (23%)
  waiting for transfers between devices  5.44 us (9%)
    pallas_call x4, Pallas kernels, partial_sums(): pl.pallas_call(functools.partial(collide, plan, first_call, len(pieces)),...  24.6 us
    all_to_all x1, blocking collectives, local(): lax.all_to_all(pair, 'inp', 0, 0, tiled=True, axis_index_groups=groups)  13.8 us
    ppermute x3, starting transfers between devices, along_z(): return lax.ppermute(array, AXES, hop(lambda c: (0, 0, d * sign(c), 0)))  7.72 us
    ppermute x3, starting transfers between devices, along_x(): return lax.ppermute(array, AXES, hop(lambda c: (sign(c), 0, 0, 0)))  4.08 us
    ppermute x5, waiting for transfers between devices, swap(): return lax.ppermute(array, AXES, hop(lambda c: (0, 0, 0, 1)))  2.87 us
    ppermute x3, waiting for transfers between devices, along_z(): return lax.ppermute(array, AXES, hop(lambda c: (0, 0, d * sign(c), 0)))  2.55 us
    ppermute x5, starting transfers between devices, swap(): return lax.ppermute(array, AXES, hop(lambda c: (0, 0, 0, 1)))  1.76 us
  transfers between devices with their start and end apart: 11, of which 3 were waited for; matrix products, arithmetic and copies ran while one was open for 0% of the time, Pallas kernels for 32%

profile of v3, /device:TPU:32, one launch (start us, length us, event | category | flops | bytes accessed | tf_op | source)
XLA Modules:
  0.0 58.3 jit_solution(4016422379237308258)
XLA Ops:
  0.0 1.9 %collective-permute-start = (bf16[96,1024]{1,0:T(8,128)(2,1)}, bf16[96,1024]{1,0:T(8,128)(2,1)S(1)}, u32[]{:S(2)}, u32[]{:S(2)}) collective-permute-start(bf16[96,1024]{1,0:T(8,128)(2,1)} %refs_1_.1), channel_id=1, source_target_pairs={{0,32},{1,225},{16,48},{17,241},{2,34},{3,227},{18,50},{19,243},{4... | collective-permute-start | bytes 589832 | tf_op jit(solution)/shard_map/ppermute | solution.py:47
  1.9 4.5 %collective-permute-start.1 = (bf16[96,1024]{1,0:T(8,128)(2,1)}, bf16[96,1024]{1,0:T(8,128)(2,1)S(1)}, u32[]{:S(2)}, u32[]{:S(2)}) collective-permute-start(bf16[96,1024]{1,0:T(8,128)(2,1)} %refs_1_.1), channel_id=1, source_target_pairs={{0,64},{1,193},{16,80},{17,209},{2,66},{3,195},{18,82},{19,211},{4... | collective-permute-start | bytes 589832 | tf_op jit(solution)/shard_map/ppermute | solution.py:47
  6.4 1.5 %collective-permute-start.2 = (bf16[96,1024]{1,0:T(8,128)(2,1)}, bf16[96,1024]{1,0:T(8,128)(2,1)S(1)}, u32[]{:S(2)}, u32[]{:S(2)}) collective-permute-start(bf16[96,1024]{1,0:T(8,128)(2,1)} %refs_1_.1), channel_id=1, source_target_pairs={{0,16},{1,19},{16,2},{17,1},{2,18},{3,17},{18,0},{19,3},{4,20},{5,... | collective-permute-start | bytes 589832 | tf_op jit(solution)/shard_map/ppermute | solution.py:51
  7.9 0.1 stack.23.where
  8.0 6.6 %shard_map.28 = (f32[8,48,128]{2,1,0:T(8,128)S(1)}, f32[8,48,128]{2,1,0:T(8,128)S(1)}, bf16[64,64,1024]{2,1,0:T(8,128)(2,1)S(1)}) custom-call(s32[5]{0:T(128)S(1)} %stack.23.where, bf16[64,64,1024]{2,1,0:T(8,128)(2,1)} %refs_0_.1, bf16[96,1024]{1,0:T(8,128)(2,1)} %refs_1_.1), custom_call_target="tpu_custom_call" | custom-call | flops 805306368 | bytes 16777216 | tf_op jit(solution)/shard_map/pallas_call | solution.py:151
  14.5 0.0 collective-permute-done
  14.6 0.0 collective-permute-done.2.refs_3_
  14.6 0.4 collective-permute-start.6
  15.0 1.3 %collective-permute-start.5 = (bf16[144,1024]{1,0:T(8,128)(2,1)S(1)}, bf16[144,1024]{1,0:T(8,128)(2,1)S(1)}, u32[]{:S(2)}, u32[]{:S(2)}) collective-permute-start(bf16[144,1024]{1,0:T(8,128)(2,1)S(1)} %pad_maximum_fusion), channel_id=1, source_target_pairs={{0,64},{1,193},{16,80},{17,209},{2,66},{3,195},{18,82},{19,211},{4... | collective-permute-start | bytes 884744 | tf_op jit(solution)/shard_map/ppermute | solution.py:47
  16.3 1.5 %collective-permute-start.3 = (bf16[192,1024]{1,0:T(8,128)(2,1)S(1)}, bf16[192,1024]{1,0:T(8,128)(2,1)S(1)}, u32[]{:S(2)}, u32[]{:S(2)}) collective-permute-start(bf16[192,1024]{1,0:T(8,128)(2,1)S(1)} %constant_dynamic-update-slice_fusion.refs_1_), channel_id=1, source_target_pairs={{0,16},{1,19},{16,2},{17,1},{2,18},{3,17},{18,0},{19,3},{4,20},{5,... | collective-permute-start | bytes 1179656 | tf_op jit(solution)/shard_map/ppermute | solution.py:51
  17.8 6.0 %shard_map.29 = (f32[8,48,128]{2,1,0:T(8,128)S(1)}, f32[8,48,128]{2,1,0:T(8,128)S(1)}) custom-call(s32[5]{0:T(128)S(1)} %stack.23.where, bf16[64,64,1024]{2,1,0:T(8,128)(2,1)S(1)} %get-tuple-element.24.refs_0_, bf16[192,1024]{1,0:T(8,128)(2,1)S(1)} %constant_dynamic-update-slice_fusion.refs_1_, ...), custom_call_target="tpu_custom_call", output_to_operand_aliasing={{0}: (5, {}), {1}: (6, {})} | custom-call | flops 4026531840 | bytes 1048576 | tf_op jit(solution)/shard_map/pallas_call | solution.py:151
  23.8 2.5 %collective-permute-done.5.refs_1_ = bf16[144,1024]{1,0:T(8,128)(2,1)S(1)} collective-permute-done((bf16[144,1024]{1,0:T(8,128)(2,1)S(1)}, bf16[144,1024]{1,0:T(8,128)(2,1)S(1)}, u32[]{:S(2)}, u32[]{:S(2)}) %collective-permute-start.5) | collective-permute-done | bytes 294944 | tf_op jit(solution)/shard_map/ppermute | solution.py:47
  26.4 0.0 collective-permute-start.8
  26.4 1.1 %collective-permute-start.7 = (bf16[144,1024]{1,0:T(8,128)(2,1)S(1)}, bf16[144,1024]{1,0:T(8,128)(2,1)S(1)}, u32[]{:S(2)}, u32[]{:S(2)}) collective-permute-start(bf16[144,1024]{1,0:T(8,128)(2,1)S(1)} %collective-permute-done.5.refs_1_), channel_id=1, source_target_pairs={{0,16},{1,19},{16,2},{17,1},{2,18},{3,17},{18,0},{19,3},{4,20},{5,... | collective-permute-start | bytes 884744 | tf_op jit(solution)/shard_map/ppermute | solution.py:51
  27.5 1.2 %collective-permute-start.4 = (bf16[192,1024]{1,0:T(8,128)(2,1)S(1)}, bf16[192,1024]{1,0:T(8,128)(2,1)S(1)}, u32[]{:S(2)}, u32[]{:S(2)}) collective-permute-start(bf16[192,1024]{1,0:T(8,128)(2,1)S(1)} %collective-permute-done.3.refs_3_), channel_id=1, source_target_pairs={{0,1},{1,0},{16,17},{17,16},{2,3},{3,2},{18,19},{19,18},{4,5},{5,4... | collective-permute-start | bytes 1179656 | tf_op jit(solution)/shard_map/ppermute | solution.py:55
  28.6 6.0 %shard_map.30 = (f32[8,48,128]{2,1,0:T(8,128)S(1)}, f32[8,48,128]{2,1,0:T(8,128)S(1)}) custom-call(s32[5]{0:T(128)S(1)} %stack.23.where, bf16[64,64,1024]{2,1,0:T(8,128)(2,1)S(1)} %get-tuple-element.24.refs_0_, bf16[144,1024]{1,0:T(8,128)(2,1)S(1)} %collective-permute-done.5.refs_1_, ...), custom_call_target="tpu_custom_call", output_to_operand_aliasing={{0}: (5, {}), {1}: (6, {})} | custom-call | flops 4026531840 | bytes 1048576 | tf_op jit(solution)/shard_map/pallas_call | solution.py:151
  34.7 0.1 collective-permute-start.9
  34.7 0.0 collective-permute-done.4.refs_1_
  34.8 1.6 %collective-permute-done.9.refs_3_ = bf16[144,1024]{1,0:T(8,128)(2,1)S(1)} collective-permute-done((bf16[144,1024]{1,0:T(8,128)(2,1)S(1)}, bf16[144,1024]{1,0:T(8,128)(2,1)S(1)}, u32[]{:S(2)}, u32[]{:S(2)}) %collective-permute-start.9) | collective-permute-done | bytes 294944 | tf_op jit(solution)/shard_map/ppermute | solution.py:55
  36.3 6.0 %shard_map.31 = (f32[8,48,128]{2,1,0:T(8,128)S(1)}, f32[8,48,128]{2,1,0:T(8,128)S(1)}) custom-call(s32[5]{0:T(128)S(1)} %stack.23.where, bf16[64,64,1024]{2,1,0:T(8,128)(2,1)S(1)} %get-tuple-element.24.refs_0_, bf16[192,1024]{1,0:T(8,128)(2,1)S(1)} %collective-permute-done.4.refs_1_, ...), custom_call_target="tpu_custom_call", output_to_operand_aliasing={{0}: (5, {}), {1}: (6, {})} | custom-call | flops 4026531840 | bytes 1048576 | tf_op jit(solution)/shard_map/pallas_call | solution.py:151
  42.4 0.1 collective-permute-start.10
  42.5 1.3 %collective-permute-done.10.theirs = f32[8,48,128]{2,1,0:T(8,128)S(1)} collective-permute-done((f32[8,48,128]{2,1,0:T(8,128)S(1)}, f32[8,48,128]{2,1,0:T(8,128)S(1)}, u32[]{:S(2)}, u32[]{:S(2)}) %collective-permute-start.10) | collective-permute-done | bytes 196640 | tf_op jit(solution)/shard_map/ppermute | solution.py:55
  43.8 13.8 %all_to_all.5.shares = f32[8,48,128]{2,1,0:T(8,128)S(1)} all-to-all(f32[8,48,128]{2,1,0:T(8,128)S(1)} %shard_map.32), channel_id=1, replica_groups={{0,2,4,6,8,10,12,14},{1,3,5,7,9,11,13,15},{16,18,20,22,24,26,28,30},{17..., dimensions={0} | all-to-all | bytes 393216 | tf_op jit(solution)/shard_map/all_to_all | solution.py:251
  57.6 0.7 %shard_map.33 = bf16[64,96]{1,0:T(8,128)(2,1)} custom-call(f32[8,48,128]{2,1,0:T(8,128)S(1)} %all_to_all.5.shares), custom_call_target="tpu_custom_call" | custom-call | tf_op jit(solution)/shard_map/pallas_call | solution.py:252
  (10 shorter events, 0.1 us)
Async XLA Ops:
  0.0 14.5 %collective-permute-start = (bf16[96,1024]{1,0:T(8,128)(2,1)}, bf16[96,1024]{1,0:T(8,128)(2,1)S(1)}, u32[]{:S(2)}, u32[]{:S(2)}) collective-permute-start(bf16[96,1024]{1,0:T(8,128)(2,1)} %refs_1_.1), channel_id=1, source_target_pairs={{0,32},{1,225},{16,48},{17,241},{2,34},{3,227},{18,50},{19,243},{4... | collective-permute-start | bytes 589832 | tf_op jit(solution)/shard_map/ppermute | solution.py:47
  1.9 12.6 %collective-permute-start.1 = (bf16[96,1024]{1,0:T(8,128)(2,1)}, bf16[96,1024]{1,0:T(8,128)(2,1)S(1)}, u32[]{:S(2)}, u32[]{:S(2)}) collective-permute-start(bf16[96,1024]{1,0:T(8,128)(2,1)} %refs_1_.1), channel_id=1, source_target_pairs={{0,64},{1,193},{16,80},{17,209},{2,66},{3,195},{18,82},{19,211},{4... | collective-permute-start | bytes 589832 | tf_op jit(solution)/shard_map/ppermute | solution.py:47
  6.4 8.2 %collective-permute-start.2 = (bf16[96,1024]{1,0:T(8,128)(2,1)}, bf16[96,1024]{1,0:T(8,128)(2,1)S(1)}, u32[]{:S(2)}, u32[]{:S(2)}) collective-permute-start(bf16[96,1024]{1,0:T(8,128)(2,1)} %refs_1_.1), channel_id=1, source_target_pairs={{0,16},{1,19},{16,2},{17,1},{2,18},{3,17},{18,0},{19,3},{4,20},{5,... | collective-permute-start | bytes 589832 | tf_op jit(solution)/shard_map/ppermute | solution.py:51
  14.6 3.2 %collective-permute-start.6 = (bf16[192,1024]{1,0:T(8,128)(2,1)S(1)}, bf16[192,1024]{1,0:T(8,128)(2,1)S(1)}, u32[]{:S(2)}, u32[]{:S(2)}) collective-permute-start(bf16[192,1024]{1,0:T(8,128)(2,1)S(1)} %constant_dynamic-update-slice_fusion.refs_1_), channel_id=1, source_target_pairs={{0,1},{1,0},{16,17},{17,16},{2,3},{3,2},{18,19},{19,18},{4,5},{5,4... | collective-permute-start | bytes 1179656 | tf_op jit(solution)/shard_map/ppermute | solution.py:55
  15.0 11.3 %collective-permute-start.5 = (bf16[144,1024]{1,0:T(8,128)(2,1)S(1)}, bf16[144,1024]{1,0:T(8,128)(2,1)S(1)}, u32[]{:S(2)}, u32[]{:S(2)}) collective-permute-start(bf16[144,1024]{1,0:T(8,128)(2,1)S(1)} %pad_maximum_fusion), channel_id=1, source_target_pairs={{0,64},{1,193},{16,80},{17,209},{2,66},{3,195},{18,82},{19,211},{4... | collective-permute-start | bytes 884744 | tf_op jit(solution)/shard_map/ppermute | solution.py:47
  16.3 11.1 %collective-permute-start.3 = (bf16[192,1024]{1,0:T(8,128)(2,1)S(1)}, bf16[192,1024]{1,0:T(8,128)(2,1)S(1)}, u32[]{:S(2)}, u32[]{:S(2)}) collective-permute-start(bf16[192,1024]{1,0:T(8,128)(2,1)S(1)} %constant_dynamic-update-slice_fusion.refs_1_), channel_id=1, source_target_pairs={{0,16},{1,19},{16,2},{17,1},{2,18},{3,17},{18,0},{19,3},{4,20},{5,... | collective-permute-start | bytes 1179656 | tf_op jit(solution)/shard_map/ppermute | solution.py:51
  26.4 2.3 %collective-permute-start.8 = (bf16[144,1024]{1,0:T(8,128)(2,1)S(1)}, bf16[144,1024]{1,0:T(8,128)(2,1)S(1)}, u32[]{:S(2)}, u32[]{:S(2)}) collective-permute-start(bf16[144,1024]{1,0:T(8,128)(2,1)S(1)} %collective-permute-done.5.refs_1_), channel_id=1, source_target_pairs={{0,1},{1,0},{16,17},{17,16},{2,3},{3,2},{18,19},{19,18},{4,5},{5,4... | collective-permute-start | bytes 884744 | tf_op jit(solution)/shard_map/ppermute | solution.py:55
  26.4 8.3 %collective-permute-start.7 = (bf16[144,1024]{1,0:T(8,128)(2,1)S(1)}, bf16[144,1024]{1,0:T(8,128)(2,1)S(1)}, u32[]{:S(2)}, u32[]{:S(2)}) collective-permute-start(bf16[144,1024]{1,0:T(8,128)(2,1)S(1)} %collective-permute-done.5.refs_1_), channel_id=1, source_target_pairs={{0,16},{1,19},{16,2},{17,1},{2,18},{3,17},{18,0},{19,3},{4,20},{5,... | collective-permute-start | bytes 884744 | tf_op jit(solution)/shard_map/ppermute | solution.py:51
  27.5 7.3 %collective-permute-start.4 = (bf16[192,1024]{1,0:T(8,128)(2,1)S(1)}, bf16[192,1024]{1,0:T(8,128)(2,1)S(1)}, u32[]{:S(2)}, u32[]{:S(2)}) collective-permute-start(bf16[192,1024]{1,0:T(8,128)(2,1)S(1)} %collective-permute-done.3.refs_3_), channel_id=1, source_target_pairs={{0,1},{1,0},{16,17},{17,16},{2,3},{3,2},{18,19},{19,18},{4,5},{5,4... | collective-permute-start | bytes 1179656 | tf_op jit(solution)/shard_map/ppermute | solution.py:55
  34.7 1.6 %collective-permute-start.9 = (bf16[144,1024]{1,0:T(8,128)(2,1)S(1)}, bf16[144,1024]{1,0:T(8,128)(2,1)S(1)}, u32[]{:S(2)}, u32[]{:S(2)}) collective-permute-start(bf16[144,1024]{1,0:T(8,128)(2,1)S(1)} %collective-permute-done.7.refs_2_), channel_id=1, source_target_pairs={{0,1},{1,0},{16,17},{17,16},{2,3},{3,2},{18,19},{19,18},{4,5},{5,4... | collective-permute-start | bytes 884744 | tf_op jit(solution)/shard_map/ppermute | solution.py:55
  42.4 1.5 %collective-permute-start.10 = (f32[8,48,128]{2,1,0:T(8,128)S(1)}, f32[8,48,128]{2,1,0:T(8,128)S(1)}, u32[]{:S(2)}, u32[]{:S(2)}) collective-permute-start(f32[8,48,128]{2,1,0:T(8,128)S(1)} %get-tuple-element.42), channel_id=1, source_target_pairs={{0,1},{1,0},{16,17},{17,16},{2,3},{3,2},{18,19},{19,18},{4,5},{5,4... | collective-permute-start | bytes 589832 | tf_op jit(solution)/shard_map/ppermute | solution.py:55

commit v4 on v3

--- a/solution.py
+++ b/solution.py
@@ -1,4 +1,5 @@
 import functools
+from typing import NamedTuple
 
 import jax
 import jax.numpy as jnp
@@ -71,11 +72,12 @@
     return jnp.concatenate([packed[:, 0:96], last], axis=0)
 
 
-def collide(plan, first_call, n_pieces, where, *refs):
+def collide(call, where, *refs):
     refs = list(refs)
     tensor_in = refs.pop(0)
-    pieces, refs = refs[:n_pieces], refs[n_pieces:]
-    if first_call:
+    n = len({part[0] for part in call.parts})
+    pieces, refs = refs[:n], refs[n:]
+    if call.kind == "first":
         give, keep, tensor, cells, weight, total, arrived = refs
         copies = [
             pltpu.make_async_copy(pieces[0], cells, arrived.at[0]),
@@ -87,14 +89,19 @@
             copy.wait()
     else:
         tensor = tensor_in
-        _, _, give, keep, cells, weight, total = refs
-    first, z, odd, core = where[0], where[1], where[2], where[3]
-    for n, (_, _, parts) in enumerate(plan):
-        for piece, source, count, half in parts:
-            at = n * BLOCK
+        if call.kind == "open":
+            _, _, give, keep, total, cells, weight = refs
+        elif call.kind == "close":
+            _, _, _, give, keep, total, cells, weight = refs
+        else:
+            _, _, give, keep, cells, weight, total = refs
+        core = where[3]
+        for piece, source, count, at, half in call.parts:
+            at -= call.low
             if half is not None:
                 at = pl.multiple_of(at + (core if half == 0 else 1 - core) * HALF, 16)
             cells[pl.ds(at, count), :] = pieces[piece][source : source + count, :]
+    first, z, odd, core = where[0], where[1], where[2], where[3]
     base = pl.multiple_of((first // 128) * 128, 128)
     weight[...] = cells[:, pl.ds(base, 128)].astype(jnp.float32).T
     off = pl.multiple_of(lax.rem(first, 128), K_INP)
@@ -111,14 +118,14 @@
                 preferred_element_type=jnp.float32,
             )
             chosen = weight[pl.ds(off, K_INP), c : c + w]
-            total[pl.ds(k, K_STEP), c : c + w] = jnp.sum(
+            total[pl.ds(k, K_STEP), call.low + c : call.low + c + w] = jnp.sum(
                 inner.reshape(K_STEP, K_INP, w) * chosen[None], axis=1
             )
 
-    for n, (d, own, _) in enumerate(plan):
+    for at, d, own in call.blocks:
         kept = (odd == core) if own else (odd != core)
         owner = lax.rem(z - d * (1 - 2 * core) + NZ, NZ)
-        block = pack(total[:, n * BLOCK : (n + 1) * BLOCK])
+        block = pack(total[:, at : at + BLOCK])
 
         @pl.when(kept)
         def _(block=block, owner=owner):
@@ -129,27 +136,37 @@
             give[owner] = block
 
 
-def partial_sums(plan, where, tensor, pieces, before):
-    size = BLOCK * len(plan)
-    first_call = before is None
+class Call(NamedTuple):
+    kind: str
+    low: int
+    high: int
+    parts: tuple
+    blocks: tuple
+
+
+def partial_sums(call, where, tensor, pieces, before):
+    size = call.high - call.low
+    first_call = call.kind == "first"
     args = [where, tensor, *pieces]
     in_specs = [SMEM] + [HBM if first_call else VMEM] * (1 + len(pieces))
     part = jax.ShapeDtypeStruct((NZ, 48, 128), jnp.float32)
-    out_shape, aliases = [part, part], {}
+    out_shape = [part, part]
     scratch = [
         pltpu.VMEM((size, 1024), jnp.bfloat16),
         pltpu.VMEM((128, size), jnp.float32),
-        pltpu.VMEM((K_OUT, size), jnp.float32),
     ]
+    if call.kind in ("open", "close"):
+        out_shape.append(jax.ShapeDtypeStruct((K_OUT, 2 * TILE), jnp.float32))
+    else:
+        scratch.append(pltpu.VMEM((K_OUT, size), jnp.float32))
     if first_call:
         out_shape.append(jax.ShapeDtypeStruct(tensor.shape, tensor.dtype))
         scratch.append(pltpu.SemaphoreType.DMA((2,)))
-    else:
-        aliases = {len(args): 0, len(args) + 1: 1}
-        args += before
-        in_specs += [VMEM, VMEM]
+    aliases = {len(args) + n: n for n in range(len(before))}
+    args += before
+    in_specs += [VMEM] * len(before)
     return pl.pallas_call(
-        functools.partial(collide, plan, first_call, len(pieces)),
+        functools.partial(collide, call),
         in_specs=in_specs,
         out_specs=[VMEM] * len(out_shape),
         out_shape=out_shape,
@@ -164,12 +181,29 @@
     )(*args)
 
 
-def whole(piece, source=0):
-    return ((piece, source, BLOCK, None),)
-
-
-def halves(mine, theirs, source):
-    return ((mine, source, HALF, 0), (theirs, source, HALF, 1))
+def far_calls(near_blocks):
+    at = [n * BLOCK for n in range(5)]
+    early = TILE - at[2]
+    first = Call(
+        "open",
+        0,
+        TILE,
+        ((0, 0, 2 * BLOCK, 0, None), (1, 0, early, at[2], None)),
+        tuple((at[n], d, own) for n, (d, own) in enumerate(near_blocks[:2])),
+    )
+    second = Call(
+        "close",
+        TILE,
+        5 * BLOCK,
+        (
+            (0, early, BLOCK - early, TILE, None),
+            (1, 0, BLOCK, at[3], None),
+            (0, BLOCK, HALF, at[4], 0),
+            (1, BLOCK, HALF, at[4], 1),
+        ),
+        tuple((at[2 + n], d, near_blocks[2]) for n, d in enumerate((3, -3, 4))),
+    )
+    return first, second
 
 
 def add_pair(mine, theirs, out):
@@ -195,7 +229,9 @@
     one = along_z(state, 1)
     same_x = along_x(state)
     there = [pltpu.with_memory_space_constraint(a, pltpu.HBM) for a in (tensor, state)]
-    give, keep, held = partial_sums(((0, True, ()),), where, there[0], there[1:], None)
+    give, keep, held = partial_sums(
+        Call("first", 0, BLOCK, ((0, 0, BLOCK, 0, None),), ((0, 0, True),)), where, there[0], there[1:], []
+    )
 
     one, two, same_x, give = lax.optimization_barrier((one, two, same_x, give))
     near = rows(one, two)
@@ -204,39 +240,42 @@
     near, both = lax.optimization_barrier((near, both))
     far = along_z(both, 2)
     near_x = along_x(near)
-    plan = (
-        (1, True, whole(0)),
-        (2, True, whole(0, BLOCK)),
-        (-1, True, whole(1)),
-        (-2, True, whole(1, BLOCK)),
-        (0, False, whole(2)),
-    )
-    give, keep = partial_sums(plan, where, held, [near, near_swap, same_x], [give, keep])
+    call = Call(
+        "plain",
+        0,
+        5 * BLOCK,
+        (
+            (0, 0, 2 * BLOCK, 0, None),
+            (1, 0, 2 * BLOCK, 2 * BLOCK, None),
+            (2, 0, BLOCK, 4 * BLOCK, None),
+        ),
+        tuple(
+            (n * BLOCK, d, own)
+            for n, (d, own) in enumerate(
+                ((1, True), (2, True), (-1, True), (-2, True), (0, False))
+            )
+        ),
+    )
+    give, keep = partial_sums(call, where, held, [near, near_swap, same_x], [give, keep])
 
     far, give = lax.optimization_barrier((far, give))
     far_x = along_x(far)
     far_swap = swap(far)
     near_x_swap = swap(near_x)
-    plan = (
-        (3, True, whole(0)),
-        (-3, True, whole(1)),
-        (4, True, halves(0, 1, BLOCK)),
-        (1, False, whole(2)),
-        (2, False, whole(2, BLOCK)),
-    )
-    give, keep = partial_sums(plan, where, held, [far, far_swap, near_x], [give, keep])
+    first, second = far_calls(((1, False), (2, False), True))
+    give, keep, sums = partial_sums(first, where, held, [near_x, far], [give, keep])
+    give, keep, sums = partial_sums(
+        second, where, held, [far, far_swap], [give, keep, sums]
+    )
 
     far_x, give = lax.optimization_barrier((far_x, give))
     far_x_swap = swap(far_x)
-    plan = (
-        (-1, False, whole(0)),
-        (-2, False, whole(0, BLOCK)),
-        (3, False, whole(1)),
-        (-3, False, whole(2)),
-        (4, False, halves(1, 2, BLOCK)),
-    )
-    give, keep = partial_sums(
-        plan, where, held, [near_x_swap, far_x, far_x_swap], [give, keep]
+    first, second = far_calls(((-1, False), (-2, False), False))
+    give, keep, sums = partial_sums(
+        first, where, held, [near_x_swap, far_x], [give, keep]
+    )
+    give, keep, sums = partial_sums(
+        second, where, held, [far_x, far_x_swap], [give, keep, sums]
     )
 
     got = swap(give)

time: 59 us -> 59.4 us (level)
  waiting for transfers between devices: 5.44 us -> 3.64 us
  Pallas kernels: 25.3 us -> 27 us
    ppermute x5, waiting for transfers between devices: 2.87 us -> 1.08 us  [swap(): return lax.ppermute(array, AXES, hop(lambda c: (0, 0, 0, 1)))]
    pallas_call x4 -> x6, Pallas kernels: 24.6 us -> 26.3 us  [partial_sums(): pl.pallas_call(functools.partial(collide, call), in_specs=in_specs, out_s...]
  transfers between devices with their start and end apart: 11 -> 11, of which waited for: 3 -> 2; matrix products, arithmetic and copies ran while one was open for 0% -> 0% of each run, Pallas kernels for 32% -> 39%
where the time goes in v4:
time: 59.4 us; the launch traced here: 58.6 us
  Pallas kernels  27 us (45%)
  starting transfers between devices  13.9 us (23%)
  blocking collectives  13.8 us (23%)
  waiting for transfers between devices  3.64 us (6%)
    pallas_call x6, Pallas kernels, partial_sums(): pl.pallas_call(functools.partial(collide, call), in_specs=in_specs, out_s...  26.3 us
    all_to_all x1, blocking collectives, local(): lax.all_to_all(pair, 'inp', 0, 0, tiled=True, axis_index_groups=groups)  13.8 us
    ppermute x3, starting transfers between devices, along_z(): return lax.ppermute(array, AXES, hop(lambda c: (0, 0, d * sign(c), 0)))  7.72 us
    ppermute x3, starting transfers between devices, along_x(): return lax.ppermute(array, AXES, hop(lambda c: (sign(c), 0, 0, 0)))  4.08 us
    ppermute x3, waiting for transfers between devices, along_z(): return lax.ppermute(array, AXES, hop(lambda c: (0, 0, d * sign(c), 0)))  2.55 us
    ppermute x5, starting transfers between devices, swap(): return lax.ppermute(array, AXES, hop(lambda c: (0, 0, 0, 1)))  2.1 us
  transfers between devices with their start and end apart: 11, of which 2 were waited for; matrix products, arithmetic and copies ran while one was open for 0% of the time, Pallas kernels for 39%

profile of v4, /device:TPU:32, one launch (start us, length us, event | category | flops | bytes accessed | tf_op | source)
XLA Modules:
  0.0 58.6 jit_solution(2891315942422499643)
XLA Ops:
  0.0 1.9 %collective-permute-start = (bf16[96,1024]{1,0:T(8,128)(2,1)}, bf16[96,1024]{1,0:T(8,128)(2,1)S(1)}, u32[]{:S(2)}, u32[]{:S(2)}) collective-permute-start(bf16[96,1024]{1,0:T(8,128)(2,1)} %refs_1_.1), channel_id=1, source_target_pairs={{0,32},{1,225},{16,48},{17,241},{2,34},{3,227},{18,50},{19,243},{4... | collective-permute-start | bytes 589832 | tf_op jit(solution)/shard_map/ppermute | solution.py:48
  1.9 4.5 %collective-permute-start.1 = (bf16[96,1024]{1,0:T(8,128)(2,1)}, bf16[96,1024]{1,0:T(8,128)(2,1)S(1)}, u32[]{:S(2)}, u32[]{:S(2)}) collective-permute-start(bf16[96,1024]{1,0:T(8,128)(2,1)} %refs_1_.1), channel_id=1, source_target_pairs={{0,64},{1,193},{16,80},{17,209},{2,66},{3,195},{18,82},{19,211},{4... | collective-permute-start | bytes 589832 | tf_op jit(solution)/shard_map/ppermute | solution.py:48
  6.4 1.5 %collective-permute-start.2 = (bf16[96,1024]{1,0:T(8,128)(2,1)}, bf16[96,1024]{1,0:T(8,128)(2,1)S(1)}, u32[]{:S(2)}, u32[]{:S(2)}) collective-permute-start(bf16[96,1024]{1,0:T(8,128)(2,1)} %refs_1_.1), channel_id=1, source_target_pairs={{0,16},{1,19},{16,2},{17,1},{2,18},{3,17},{18,0},{19,3},{4,20},{5,... | collective-permute-start | bytes 589832 | tf_op jit(solution)/shard_map/ppermute | solution.py:52
  7.9 0.1 stack.23.where
  8.0 6.6 %shard_map.28 = (f32[8,48,128]{2,1,0:T(8,128)S(1)}, f32[8,48,128]{2,1,0:T(8,128)S(1)}, bf16[64,64,1024]{2,1,0:T(8,128)(2,1)S(1)}) custom-call(s32[5]{0:T(128)S(1)} %stack.23.where, bf16[64,64,1024]{2,1,0:T(8,128)(2,1)} %refs_0_.1, bf16[96,1024]{1,0:T(8,128)(2,1)} %refs_1_.1), custom_call_target="tpu_custom_call" | custom-call | flops 805306368 | bytes 16777216 | tf_op jit(solution)/shard_map/pallas_call | solution.py:168
  14.5 0.0 collective-permute-done
  14.6 0.0 collective-permute-done.2.refs_3_
  14.6 0.4 collective-permute-start.4
  15.0 1.3 %collective-permute-start.3 = (bf16[144,1024]{1,0:T(8,128)(2,1)S(1)}, bf16[144,1024]{1,0:T(8,128)(2,1)S(1)}, u32[]{:S(2)}, u32[]{:S(2)}) collective-permute-start(bf16[144,1024]{1,0:T(8,128)(2,1)S(1)} %pad_maximum_fusion), channel_id=1, source_target_pairs={{0,64},{1,193},{16,80},{17,209},{2,66},{3,195},{18,82},{19,211},{4... | collective-permute-start | bytes 884744 | tf_op jit(solution)/shard_map/ppermute | solution.py:48
  16.3 1.5 %collective-permute-start.7 = (bf16[192,1024]{1,0:T(8,128)(2,1)S(1)}, bf16[192,1024]{1,0:T(8,128)(2,1)S(1)}, u32[]{:S(2)}, u32[]{:S(2)}) collective-permute-start(bf16[192,1024]{1,0:T(8,128)(2,1)S(1)} %constant_dynamic-update-slice_fusion.refs_1_), channel_id=1, source_target_pairs={{0,16},{1,19},{16,2},{17,1},{2,18},{3,17},{18,0},{19,3},{4,20},{5,... | collective-permute-start | bytes 1179656 | tf_op jit(solution)/shard_map/ppermute | solution.py:52
  17.8 6.0 %shard_map.29 = (f32[8,48,128]{2,1,0:T(8,128)S(1)}, f32[8,48,128]{2,1,0:T(8,128)S(1)}) custom-call(s32[5]{0:T(128)S(1)} %stack.23.where, bf16[64,64,1024]{2,1,0:T(8,128)(2,1)S(1)} %get-tuple-element.30.refs_0_, bf16[192,1024]{1,0:T(8,128)(2,1)S(1)} %constant_dynamic-update-slice_fusion.refs_1_, ...), custom_call_target="tpu_custom_call", output_to_operand_aliasing={{0}: (5, {}), {1}: (6, {})} | custom-call | flops 4026531840 | bytes 1048576 | tf_op jit(solution)/shard_map/pallas_call | solution.py:168
  23.8 2.5 %collective-permute-done.3.refs_2_.refs_1_ = bf16[144,1024]{1,0:T(8,128)(2,1)S(1)} collective-permute-done((bf16[144,1024]{1,0:T(8,128)(2,1)S(1)}, bf16[144,1024]{1,0:T(8,128)(2,1)S(1)}, u32[]{:S(2)}, u32[]{:S(2)}) %collective-permute-start.3) | collective-permute-done | bytes 294944 | tf_op jit(solution)/shard_map/ppermute | solution.py:48
  26.4 1.1 %collective-permute-start.5 = (bf16[144,1024]{1,0:T(8,128)(2,1)S(1)}, bf16[144,1024]{1,0:T(8,128)(2,1)S(1)}, u32[]{:S(2)}, u32[]{:S(2)}) collective-permute-start(bf16[144,1024]{1,0:T(8,128)(2,1)S(1)} %collective-permute-done.3.refs_2_.refs_1_), channel_id=1, source_target_pairs={{0,16},{1,19},{16,2},{17,1},{2,18},{3,17},{18,0},{19,3},{4,20},{5,... | collective-permute-start | bytes 884744 | tf_op jit(solution)/shard_map/ppermute | solution.py:52
  27.5 1.2 %collective-permute-start.9 = (bf16[192,1024]{1,0:T(8,128)(2,1)S(1)}, bf16[192,1024]{1,0:T(8,128)(2,1)S(1)}, u32[]{:S(2)}, u32[]{:S(2)}) collective-permute-start(bf16[192,1024]{1,0:T(8,128)(2,1)S(1)} %collective-permute-done.7.refs_1_), channel_id=1, source_target_pairs={{0,1},{1,0},{16,17},{17,16},{2,3},{3,2},{18,19},{19,18},{4,5},{5,4... | collective-permute-start | bytes 1179656 | tf_op jit(solution)/shard_map/ppermute | solution.py:56
  28.6 3.3 %shard_map.30 = (f32[8,48,128]{2,1,0:T(8,128)S(1)}, f32[8,48,128]{2,1,0:T(8,128)S(1)}, f32[64,512]{1,0:T(8,128)S(1)}) custom-call(s32[5]{0:T(128)S(1)} %stack.23.where, bf16[64,64,1024]{2,1,0:T(8,128)(2,1)S(1)} %get-tuple-element.30.refs_0_, bf16[192,1024]{1,0:T(8,128)(2,1)S(1)} %collective-permute-done.7.refs_1_, ...), custom_call_target="tpu_custom_call", output_to_operand_aliasing={{0}: (4, {}), {1}: (5, {})} | custom-call | flops 2147483648 | bytes 1048576 | tf_op jit(solution)/shard_map/pallas_call | solution.py:168
  32.0 3.6 %shard_map.31 = (f32[8,48,128]{2,1,0:T(8,128)S(1)}, f32[8,48,128]{2,1,0:T(8,128)S(1)}, f32[64,512]{1,0:T(8,128)S(1)}) custom-call(s32[5]{0:T(128)S(1)} %stack.23.where, bf16[64,64,1024]{2,1,0:T(8,128)(2,1)S(1)} %get-tuple-element.30.refs_0_, ...), custom_call_target="tpu_custom_call", output_to_operand_aliasing={{0}: (4, {}), {1}: (5, {}), {2}: (6, {})} | custom-call | flops 1879048192 | bytes 1048576 | tf_op jit(solution)/shard_map/pallas_call | solution.py:168
  35.5 0.1 collective-permute-start.8
  35.6 0.0 collective-permute-done.9.refs_1_
  35.6 3.3 %shard_map.32 = (f32[8,48,128]{2,1,0:T(8,128)S(1)}, f32[8,48,128]{2,1,0:T(8,128)S(1)}, f32[64,512]{1,0:T(8,128)S(1)}) custom-call(s32[5]{0:T(128)S(1)} %stack.23.where, bf16[64,64,1024]{2,1,0:T(8,128)(2,1)S(1)} %get-tuple-element.30.refs_0_, bf16[192,1024]{1,0:T(8,128)(2,1)S(1)} %collective-permute-done.9.refs_1_, ...), custom_call_target="tpu_custom_call", output_to_operand_aliasing={{0}: (4, {}), {1}: (5, {})} | custom-call | flops 2147483648 | bytes 1048576 | tf_op jit(solution)/shard_map/pallas_call | solution.py:168
  38.9 3.6 %shard_map.33 = (f32[8,48,128]{2,1,0:T(8,128)S(1)}, f32[8,48,128]{2,1,0:T(8,128)S(1)}, f32[64,512]{1,0:T(8,128)S(1)}) custom-call(s32[5]{0:T(128)S(1)} %stack.23.where, bf16[64,64,1024]{2,1,0:T(8,128)(2,1)S(1)} %get-tuple-element.30.refs_0_, ...), custom_call_target="tpu_custom_call", output_to_operand_aliasing={{0}: (4, {}), {1}: (5, {}), {2}: (6, {})} | custom-call | flops 1879048192 | bytes 1048576 | tf_op jit(solution)/shard_map/pallas_call | solution.py:168
  42.5 0.5 collective-permute-start.10
  43.0 1.1 %collective-permute-done.10.theirs = f32[8,48,128]{2,1,0:T(8,128)S(1)} collective-permute-done((f32[8,48,128]{2,1,0:T(8,128)S(1)}, f32[8,48,128]{2,1,0:T(8,128)S(1)}, u32[]{:S(2)}, u32[]{:S(2)}) %collective-permute-start.10) | collective-permute-done | bytes 196640 | tf_op jit(solution)/shard_map/ppermute | solution.py:56
  44.1 13.8 %all_to_all.5.shares = f32[8,48,128]{2,1,0:T(8,128)S(1)} all-to-all(f32[8,48,128]{2,1,0:T(8,128)S(1)} %shard_map.34), channel_id=1, replica_groups={{0,2,4,6,8,10,12,14},{1,3,5,7,9,11,13,15},{16,18,20,22,24,26,28,30},{17..., dimensions={0} | all-to-all | bytes 393216 | tf_op jit(solution)/shard_map/all_to_all | solution.py:290
  57.9 0.7 %shard_map.35 = bf16[64,96]{1,0:T(8,128)(2,1)} custom-call(f32[8,48,128]{2,1,0:T(8,128)S(1)} %all_to_all.5.shares), custom_call_target="tpu_custom_call" | custom-call | tf_op jit(solution)/shard_map/pallas_call | solution.py:291
  (12 shorter events, 0.1 us)
Async XLA Ops:
  0.0 14.5 %collective-permute-start = (bf16[96,1024]{1,0:T(8,128)(2,1)}, bf16[96,1024]{1,0:T(8,128)(2,1)S(1)}, u32[]{:S(2)}, u32[]{:S(2)}) collective-permute-start(bf16[96,1024]{1,0:T(8,128)(2,1)} %refs_1_.1), channel_id=1, source_target_pairs={{0,32},{1,225},{16,48},{17,241},{2,34},{3,227},{18,50},{19,243},{4... | collective-permute-start | bytes 589832 | tf_op jit(solution)/shard_map/ppermute | solution.py:48
  1.9 12.6 %collective-permute-start.1 = (bf16[96,1024]{1,0:T(8,128)(2,1)}, bf16[96,1024]{1,0:T(8,128)(2,1)S(1)}, u32[]{:S(2)}, u32[]{:S(2)}) collective-permute-start(bf16[96,1024]{1,0:T(8,128)(2,1)} %refs_1_.1), channel_id=1, source_target_pairs={{0,64},{1,193},{16,80},{17,209},{2,66},{3,195},{18,82},{19,211},{4... | collective-permute-start | bytes 589832 | tf_op jit(solution)/shard_map/ppermute | solution.py:48
  6.4 8.2 %collective-permute-start.2 = (bf16[96,1024]{1,0:T(8,128)(2,1)}, bf16[96,1024]{1,0:T(8,128)(2,1)S(1)}, u32[]{:S(2)}, u32[]{:S(2)}) collective-permute-start(bf16[96,1024]{1,0:T(8,128)(2,1)} %refs_1_.1), channel_id=1, source_target_pairs={{0,16},{1,19},{16,2},{17,1},{2,18},{3,17},{18,0},{19,3},{4,20},{5,... | collective-permute-start | bytes 589832 | tf_op jit(solution)/shard_map/ppermute | solution.py:52
  14.6 3.2 %collective-permute-start.4 = (bf16[192,1024]{1,0:T(8,128)(2,1)S(1)}, bf16[192,1024]{1,0:T(8,128)(2,1)S(1)}, u32[]{:S(2)}, u32[]{:S(2)}) collective-permute-start(bf16[192,1024]{1,0:T(8,128)(2,1)S(1)} %constant_dynamic-update-slice_fusion.refs_1_), channel_id=1, source_target_pairs={{0,1},{1,0},{16,17},{17,16},{2,3},{3,2},{18,19},{19,18},{4,5},{5,4... | collective-permute-start | bytes 1179656 | tf_op jit(solution)/shard_map/ppermute | solution.py:56
  15.0 11.3 %collective-permute-start.3 = (bf16[144,1024]{1,0:T(8,128)(2,1)S(1)}, bf16[144,1024]{1,0:T(8,128)(2,1)S(1)}, u32[]{:S(2)}, u32[]{:S(2)}) collective-permute-start(bf16[144,1024]{1,0:T(8,128)(2,1)S(1)} %pad_maximum_fusion), channel_id=1, source_target_pairs={{0,64},{1,193},{16,80},{17,209},{2,66},{3,195},{18,82},{19,211},{4... | collective-permute-start | bytes 884744 | tf_op jit(solution)/shard_map/ppermute | solution.py:48
  16.3 11.1 %collective-permute-start.7 = (bf16[192,1024]{1,0:T(8,128)(2,1)S(1)}, bf16[192,1024]{1,0:T(8,128)(2,1)S(1)}, u32[]{:S(2)}, u32[]{:S(2)}) collective-permute-start(bf16[192,1024]{1,0:T(8,128)(2,1)S(1)} %constant_dynamic-update-slice_fusion.refs_1_), channel_id=1, source_target_pairs={{0,16},{1,19},{16,2},{17,1},{2,18},{3,17},{18,0},{19,3},{4,20},{5,... | collective-permute-start | bytes 1179656 | tf_op jit(solution)/shard_map/ppermute | solution.py:52
  26.4 5.6 %collective-permute-start.6 = (bf16[144,1024]{1,0:T(8,128)(2,1)S(1)}, bf16[144,1024]{1,0:T(8,128)(2,1)S(1)}, u32[]{:S(2)}, u32[]{:S(2)}) collective-permute-start(bf16[144,1024]{1,0:T(8,128)(2,1)S(1)} %collective-permute-done.3.refs_2_.refs_1_), channel_id=1, source_target_pairs={{0,1},{1,0},{16,17},{17,16},{2,3},{3,2},{18,19},{19,18},{4,5},{5,4... | collective-permute-start | bytes 884744 | tf_op jit(solution)/shard_map/ppermute | solution.py:56
  26.4 9.2 %collective-permute-start.5 = (bf16[144,1024]{1,0:T(8,128)(2,1)S(1)}, bf16[144,1024]{1,0:T(8,128)(2,1)S(1)}, u32[]{:S(2)}, u32[]{:S(2)}) collective-permute-start(bf16[144,1024]{1,0:T(8,128)(2,1)S(1)} %collective-permute-done.3.refs_2_.refs_1_), channel_id=1, source_target_pairs={{0,16},{1,19},{16,2},{17,1},{2,18},{3,17},{18,0},{19,3},{4,20},{5,... | collective-permute-start | bytes 884744 | tf_op jit(solution)/shard_map/ppermute | solution.py:52
  27.5 8.2 %collective-permute-start.9 = (bf16[192,1024]{1,0:T(8,128)(2,1)S(1)}, bf16[192,1024]{1,0:T(8,128)(2,1)S(1)}, u32[]{:S(2)}, u32[]{:S(2)}) collective-permute-start(bf16[192,1024]{1,0:T(8,128)(2,1)S(1)} %collective-permute-done.7.refs_1_), channel_id=1, source_target_pairs={{0,1},{1,0},{16,17},{17,16},{2,3},{3,2},{18,19},{19,18},{4,5},{5,4... | collective-permute-start | bytes 1179656 | tf_op jit(solution)/shard_map/ppermute | solution.py:56
  35.5 3.4 %collective-permute-start.8 = (bf16[144,1024]{1,0:T(8,128)(2,1)S(1)}, bf16[144,1024]{1,0:T(8,128)(2,1)S(1)}, u32[]{:S(2)}, u32[]{:S(2)}) collective-permute-start(bf16[144,1024]{1,0:T(8,128)(2,1)S(1)} %collective-permute-done.5.refs_2_.refs_1_), channel_id=1, source_target_pairs={{0,1},{1,0},{16,17},{17,16},{2,3},{3,2},{18,19},{19,18},{4,5},{5,4... | collective-permute-start | bytes 884744 | tf_op jit(solution)/shard_map/ppermute | solution.py:56
  42.5 1.6 %collective-permute-start.10 = (f32[8,48,128]{2,1,0:T(8,128)S(1)}, f32[8,48,128]{2,1,0:T(8,128)S(1)}, u32[]{:S(2)}, u32[]{:S(2)}) collective-permute-start(f32[8,48,128]{2,1,0:T(8,128)S(1)} %get-tuple-element.54), channel_id=1, source_target_pairs={{0,1},{1,0},{16,17},{17,16},{2,3},{3,2},{18,19},{19,18},{4,5},{5,4... | collective-permute-start | bytes 589832 | tf_op jit(solution)/shard_map/ppermute | solution.py:56

commit v5 on v3

--- a/solution.py
+++ b/solution.py
@@ -115,18 +115,20 @@
                 inner.reshape(K_STEP, K_INP, w) * chosen[None], axis=1
             )
 
+    blocks = []
     for n, (d, own, _) in enumerate(plan):
-        kept = (odd == core) if own else (odd != core)
         owner = lax.rem(z - d * (1 - 2 * core) + NZ, NZ)
-        block = pack(total[:, n * BLOCK : (n + 1) * BLOCK])
-
-        @pl.when(kept)
-        def _(block=block, owner=owner):
-            keep[owner] = block
-
-        @pl.when(jnp.logical_not(kept))
-        def _(block=block, owner=owner):
-            give[owner] = block
+        blocks.append((own, owner, pack(total[:, n * BLOCK : (n + 1) * BLOCK])))
+
+    @pl.when(odd == core)
+    def _():
+        for own, owner, block in blocks:
+            (keep if own else give)[owner] = block
+
+    @pl.when(odd != core)
+    def _():
+        for own, owner, block in blocks:
+            (give if own else keep)[owner] = block
 
 
 def partial_sums(plan, where, tensor, pieces, before):

time: 59 us -> 58.2 us (0.986)
  Pallas kernels: 25.3 us -> 23.8 us
    pallas_call x4, Pallas kernels: 24.6 us -> 23.1 us  [partial_sums(): pl.pallas_call(functools.partial(collide, plan, first_call, len(pieces)),...]
  transfers between devices with their start and end apart: 11 -> 11, of which waited for: 3 -> 4; matrix products, arithmetic and copies ran while one was open for 0% -> 0% of each run, Pallas kernels for 32% -> 31%
where the time goes in v5:
time: 58.2 us; the launch traced here: 57.5 us
  Pallas kernels  23.8 us (41%)
  blocking collectives  13.8 us (24%)
  starting transfers between devices  13.6 us (23%)
  waiting for transfers between devices  6.02 us (10%)
    pallas_call x4, Pallas kernels, partial_sums(): pl.pallas_call(functools.partial(collide, plan, first_call, len(pieces)),...  23.1 us
    all_to_all x1, blocking collectives, local(): lax.all_to_all(pair, 'inp', 0, 0, tiled=True, axis_index_groups=groups)  13.8 us
    ppermute x3, starting transfers between devices, along_z(): return lax.ppermute(array, AXES, hop(lambda c: (0, 0, d * sign(c), 0)))  7.72 us
    ppermute x3, starting transfers between devices, along_x(): return lax.ppermute(array, AXES, hop(lambda c: (sign(c), 0, 0, 0)))  4.08 us
    ppermute x3, waiting for transfers between devices, along_z(): return lax.ppermute(array, AXES, hop(lambda c: (0, 0, d * sign(c), 0)))  3.04 us
    ppermute x5, waiting for transfers between devices, swap(): return lax.ppermute(array, AXES, hop(lambda c: (0, 0, 0, 1)))  2.87 us
    ppermute x5, starting transfers between devices, swap(): return lax.ppermute(array, AXES, hop(lambda c: (0, 0, 0, 1)))  1.77 us
  transfers between devices with their start and end apart: 11, of which 4 were waited for; matrix products, arithmetic and copies ran while one was open for 0% of the time, Pallas kernels for 31%

profile of v5, /device:TPU:32, one launch (start us, length us, event | category | flops | bytes accessed | tf_op | source)
XLA Modules:
  0.0 57.5 jit_solution(750562894897478759)
XLA Ops:
  0.0 1.9 %collective-permute-start = (bf16[96,1024]{1,0:T(8,128)(2,1)}, bf16[96,1024]{1,0:T(8,128)(2,1)S(1)}, u32[]{:S(2)}, u32[]{:S(2)}) collective-permute-start(bf16[96,1024]{1,0:T(8,128)(2,1)} %refs_1_.1), channel_id=1, source_target_pairs={{0,32},{1,225},{16,48},{17,241},{2,34},{3,227},{18,50},{19,243},{4... | collective-permute-start | bytes 589832 | tf_op jit(solution)/shard_map/ppermute | solution.py:47
  1.9 4.5 %collective-permute-start.1 = (bf16[96,1024]{1,0:T(8,128)(2,1)}, bf16[96,1024]{1,0:T(8,128)(2,1)S(1)}, u32[]{:S(2)}, u32[]{:S(2)}) collective-permute-start(bf16[96,1024]{1,0:T(8,128)(2,1)} %refs_1_.1), channel_id=1, source_target_pairs={{0,64},{1,193},{16,80},{17,209},{2,66},{3,195},{18,82},{19,211},{4... | collective-permute-start | bytes 589832 | tf_op jit(solution)/shard_map/ppermute | solution.py:47
  6.4 1.5 %collective-permute-start.2 = (bf16[96,1024]{1,0:T(8,128)(2,1)}, bf16[96,1024]{1,0:T(8,128)(2,1)S(1)}, u32[]{:S(2)}, u32[]{:S(2)}) collective-permute-start(bf16[96,1024]{1,0:T(8,128)(2,1)} %refs_1_.1), channel_id=1, source_target_pairs={{0,16},{1,19},{16,2},{17,1},{2,18},{3,17},{18,0},{19,3},{4,20},{5,... | collective-permute-start | bytes 589832 | tf_op jit(solution)/shard_map/ppermute | solution.py:51
  7.9 0.1 stack.23.where
  8.0 6.6 %shard_map.28 = (f32[8,48,128]{2,1,0:T(8,128)S(1)}, f32[8,48,128]{2,1,0:T(8,128)S(1)}, bf16[64,64,1024]{2,1,0:T(8,128)(2,1)S(1)}) custom-call(s32[5]{0:T(128)S(1)} %stack.23.where, bf16[64,64,1024]{2,1,0:T(8,128)(2,1)} %refs_0_.1, bf16[96,1024]{1,0:T(8,128)(2,1)} %refs_1_.1), custom_call_target="tpu_custom_call" | custom-call | flops 805306368 | bytes 16777216 | tf_op jit(solution)/shard_map/pallas_call | solution.py:153
  14.6 0.0 collective-permute-done.1
  14.6 0.0 collective-permute-done.2.refs_3_
  14.6 0.4 collective-permute-start.6
  15.0 1.3 %collective-permute-start.5 = (bf16[144,1024]{1,0:T(8,128)(2,1)S(1)}, bf16[144,1024]{1,0:T(8,128)(2,1)S(1)}, u32[]{:S(2)}, u32[]{:S(2)}) collective-permute-start(bf16[144,1024]{1,0:T(8,128)(2,1)S(1)} %pad_maximum_fusion), channel_id=1, source_target_pairs={{0,64},{1,193},{16,80},{17,209},{2,66},{3,195},{18,82},{19,211},{4... | collective-permute-start | bytes 884744 | tf_op jit(solution)/shard_map/ppermute | solution.py:47
  16.3 1.5 %collective-permute-start.3 = (bf16[192,1024]{1,0:T(8,128)(2,1)S(1)}, bf16[192,1024]{1,0:T(8,128)(2,1)S(1)}, u32[]{:S(2)}, u32[]{:S(2)}) collective-permute-start(bf16[192,1024]{1,0:T(8,128)(2,1)S(1)} %constant_dynamic-update-slice_fusion.refs_1_), channel_id=1, source_target_pairs={{0,16},{1,19},{16,2},{17,1},{2,18},{3,17},{18,0},{19,3},{4,20},{5,... | collective-permute-start | bytes 1179656 | tf_op jit(solution)/shard_map/ppermute | solution.py:51
  17.8 0.0 collective-permute-done.6.refs_2_
  17.8 5.5 %shard_map.29 = (f32[8,48,128]{2,1,0:T(8,128)S(1)}, f32[8,48,128]{2,1,0:T(8,128)S(1)}) custom-call(s32[5]{0:T(128)S(1)} %stack.23.where, bf16[64,64,1024]{2,1,0:T(8,128)(2,1)S(1)} %get-tuple-element.24.refs_0_, bf16[192,1024]{1,0:T(8,128)(2,1)S(1)} %constant_dynamic-update-slice_fusion.refs_1_, ...), custom_call_target="tpu_custom_call", output_to_operand_aliasing={{0}: (5, {}), {1}: (6, {})} | custom-call | flops 4026531840 | bytes 1048576 | tf_op jit(solution)/shard_map/pallas_call | solution.py:153
  23.3 3.0 %collective-permute-done.5.refs_1_ = bf16[144,1024]{1,0:T(8,128)(2,1)S(1)} collective-permute-done((bf16[144,1024]{1,0:T(8,128)(2,1)S(1)}, bf16[144,1024]{1,0:T(8,128)(2,1)S(1)}, u32[]{:S(2)}, u32[]{:S(2)}) %collective-permute-start.5) | collective-permute-done | bytes 294944 | tf_op jit(solution)/shard_map/ppermute | solution.py:47
  26.4 1.1 %collective-permute-start.7 = (bf16[144,1024]{1,0:T(8,128)(2,1)S(1)}, bf16[144,1024]{1,0:T(8,128)(2,1)S(1)}, u32[]{:S(2)}, u32[]{:S(2)}) collective-permute-start(bf16[144,1024]{1,0:T(8,128)(2,1)S(1)} %collective-permute-done.5.refs_1_), channel_id=1, source_target_pairs={{0,16},{1,19},{16,2},{17,1},{2,18},{3,17},{18,0},{19,3},{4,20},{5,... | collective-permute-start | bytes 884744 | tf_op jit(solution)/shard_map/ppermute | solution.py:51
  27.5 1.2 %collective-permute-start.4 = (bf16[192,1024]{1,0:T(8,128)(2,1)S(1)}, bf16[192,1024]{1,0:T(8,128)(2,1)S(1)}, u32[]{:S(2)}, u32[]{:S(2)}) collective-permute-start(bf16[192,1024]{1,0:T(8,128)(2,1)S(1)} %collective-permute-done.3.refs_3_), channel_id=1, source_target_pairs={{0,1},{1,0},{16,17},{17,16},{2,3},{3,2},{18,19},{19,18},{4,5},{5,4... | collective-permute-start | bytes 1179656 | tf_op jit(solution)/shard_map/ppermute | solution.py:55
  28.6 5.5 %shard_map.30 = (f32[8,48,128]{2,1,0:T(8,128)S(1)}, f32[8,48,128]{2,1,0:T(8,128)S(1)}) custom-call(s32[5]{0:T(128)S(1)} %stack.23.where, bf16[64,64,1024]{2,1,0:T(8,128)(2,1)S(1)} %get-tuple-element.24.refs_0_, bf16[144,1024]{1,0:T(8,128)(2,1)S(1)} %collective-permute-done.5.refs_1_, ...), custom_call_target="tpu_custom_call", output_to_operand_aliasing={{0}: (5, {}), {1}: (6, {})} | custom-call | flops 4026531840 | bytes 1048576 | tf_op jit(solution)/shard_map/pallas_call | solution.py:153
  34.2 0.1 collective-permute-done.7.refs_2_
  34.3 0.0 collective-permute-start.9
  34.3 1.6 %collective-permute-done.9.refs_3_ = bf16[144,1024]{1,0:T(8,128)(2,1)S(1)} collective-permute-done((bf16[144,1024]{1,0:T(8,128)(2,1)S(1)}, bf16[144,1024]{1,0:T(8,128)(2,1)S(1)}, u32[]{:S(2)}, u32[]{:S(2)}) %collective-permute-start.9) | collective-permute-done | bytes 294944 | tf_op jit(solution)/shard_map/ppermute | solution.py:55
  35.9 5.6 %shard_map.31 = (f32[8,48,128]{2,1,0:T(8,128)S(1)}, f32[8,48,128]{2,1,0:T(8,128)S(1)}) custom-call(s32[5]{0:T(128)S(1)} %stack.23.where, bf16[64,64,1024]{2,1,0:T(8,128)(2,1)S(1)} %get-tuple-element.24.refs_0_, bf16[192,1024]{1,0:T(8,128)(2,1)S(1)} %collective-permute-done.4.refs_1_, ...), custom_call_target="tpu_custom_call", output_to_operand_aliasing={{0}: (5, {}), {1}: (6, {})} | custom-call | flops 4026531840 | bytes 1048576 | tf_op jit(solution)/shard_map/pallas_call | solution.py:153
  41.4 0.2 collective-permute-start.10
  41.7 1.3 %collective-permute-done.10.theirs = f32[8,48,128]{2,1,0:T(8,128)S(1)} collective-permute-done((f32[8,48,128]{2,1,0:T(8,128)S(1)}, f32[8,48,128]{2,1,0:T(8,128)S(1)}, u32[]{:S(2)}, u32[]{:S(2)}) %collective-permute-start.10) | collective-permute-done | bytes 196640 | tf_op jit(solution)/shard_map/ppermute | solution.py:55
  43.0 13.8 %all_to_all.5.shares = f32[8,48,128]{2,1,0:T(8,128)S(1)} all-to-all(f32[8,48,128]{2,1,0:T(8,128)S(1)} %shard_map.32), channel_id=1, replica_groups={{0,2,4,6,8,10,12,14},{1,3,5,7,9,11,13,15},{16,18,20,22,24,26,28,30},{17..., dimensions={0} | all-to-all | bytes 393216 | tf_op jit(solution)/shard_map/all_to_all | solution.py:253
  56.8 0.7 %shard_map.33 = bf16[64,96]{1,0:T(8,128)(2,1)} custom-call(f32[8,48,128]{2,1,0:T(8,128)S(1)} %all_to_all.5.shares), custom_call_target="tpu_custom_call" | custom-call | tf_op jit(solution)/shard_map/pallas_call | solution.py:254
  (10 shorter events, 0.1 us)
Async XLA Ops:
  0.0 14.5 %collective-permute-start = (bf16[96,1024]{1,0:T(8,128)(2,1)}, bf16[96,1024]{1,0:T(8,128)(2,1)S(1)}, u32[]{:S(2)}, u32[]{:S(2)}) collective-permute-start(bf16[96,1024]{1,0:T(8,128)(2,1)} %refs_1_.1), channel_id=1, source_target_pairs={{0,32},{1,225},{16,48},{17,241},{2,34},{3,227},{18,50},{19,243},{4... | collective-permute-start | bytes 589832 | tf_op jit(solution)/shard_map/ppermute | solution.py:47
  1.9 12.6 %collective-permute-start.1 = (bf16[96,1024]{1,0:T(8,128)(2,1)}, bf16[96,1024]{1,0:T(8,128)(2,1)S(1)}, u32[]{:S(2)}, u32[]{:S(2)}) collective-permute-start(bf16[96,1024]{1,0:T(8,128)(2,1)} %refs_1_.1), channel_id=1, source_target_pairs={{0,64},{1,193},{16,80},{17,209},{2,66},{3,195},{18,82},{19,211},{4... | collective-permute-start | bytes 589832 | tf_op jit(solution)/shard_map/ppermute | solution.py:47
  6.4 8.2 %collective-permute-start.2 = (bf16[96,1024]{1,0:T(8,128)(2,1)}, bf16[96,1024]{1,0:T(8,128)(2,1)S(1)}, u32[]{:S(2)}, u32[]{:S(2)}) collective-permute-start(bf16[96,1024]{1,0:T(8,128)(2,1)} %refs_1_.1), channel_id=1, source_target_pairs={{0,16},{1,19},{16,2},{17,1},{2,18},{3,17},{18,0},{19,3},{4,20},{5,... | collective-permute-start | bytes 589832 | tf_op jit(solution)/shard_map/ppermute | solution.py:51
  14.6 3.2 %collective-permute-start.6 = (bf16[192,1024]{1,0:T(8,128)(2,1)S(1)}, bf16[192,1024]{1,0:T(8,128)(2,1)S(1)}, u32[]{:S(2)}, u32[]{:S(2)}) collective-permute-start(bf16[192,1024]{1,0:T(8,128)(2,1)S(1)} %constant_dynamic-update-slice_fusion.refs_1_), channel_id=1, source_target_pairs={{0,1},{1,0},{16,17},{17,16},{2,3},{3,2},{18,19},{19,18},{4,5},{5,4... | collective-permute-start | bytes 1179656 | tf_op jit(solution)/shard_map/ppermute | solution.py:55
  15.0 11.3 %collective-permute-start.5 = (bf16[144,1024]{1,0:T(8,128)(2,1)S(1)}, bf16[144,1024]{1,0:T(8,128)(2,1)S(1)}, u32[]{:S(2)}, u32[]{:S(2)}) collective-permute-start(bf16[144,1024]{1,0:T(8,128)(2,1)S(1)} %pad_maximum_fusion), channel_id=1, source_target_pairs={{0,64},{1,193},{16,80},{17,209},{2,66},{3,195},{18,82},{19,211},{4... | collective-permute-start | bytes 884744 | tf_op jit(solution)/shard_map/ppermute | solution.py:47
  16.3 11.1 %collective-permute-start.3 = (bf16[192,1024]{1,0:T(8,128)(2,1)S(1)}, bf16[192,1024]{1,0:T(8,128)(2,1)S(1)}, u32[]{:S(2)}, u32[]{:S(2)}) collective-permute-start(bf16[192,1024]{1,0:T(8,128)(2,1)S(1)} %constant_dynamic-update-slice_fusion.refs_1_), channel_id=1, source_target_pairs={{0,16},{1,19},{16,2},{17,1},{2,18},{3,17},{18,0},{19,3},{4,20},{5,... | collective-permute-start | bytes 1179656 | tf_op jit(solution)/shard_map/ppermute | solution.py:51
  26.4 2.3 %collective-permute-start.8 = (bf16[144,1024]{1,0:T(8,128)(2,1)S(1)}, bf16[144,1024]{1,0:T(8,128)(2,1)S(1)}, u32[]{:S(2)}, u32[]{:S(2)}) collective-permute-start(bf16[144,1024]{1,0:T(8,128)(2,1)S(1)} %collective-permute-done.5.refs_1_), channel_id=1, source_target_pairs={{0,1},{1,0},{16,17},{17,16},{2,3},{3,2},{18,19},{19,18},{4,5},{5,4... | collective-permute-start | bytes 884744 | tf_op jit(solution)/shard_map/ppermute | solution.py:55
  26.4 7.9 %collective-permute-start.7 = (bf16[144,1024]{1,0:T(8,128)(2,1)S(1)}, bf16[144,1024]{1,0:T(8,128)(2,1)S(1)}, u32[]{:S(2)}, u32[]{:S(2)}) collective-permute-start(bf16[144,1024]{1,0:T(8,128)(2,1)S(1)} %collective-permute-done.5.refs_1_), channel_id=1, source_target_pairs={{0,16},{1,19},{16,2},{17,1},{2,18},{3,17},{18,0},{19,3},{4,20},{5,... | collective-permute-start | bytes 884744 | tf_op jit(solution)/shard_map/ppermute | solution.py:51
  27.5 6.8 %collective-permute-start.4 = (bf16[192,1024]{1,0:T(8,128)(2,1)S(1)}, bf16[192,1024]{1,0:T(8,128)(2,1)S(1)}, u32[]{:S(2)}, u32[]{:S(2)}) collective-permute-start(bf16[192,1024]{1,0:T(8,128)(2,1)S(1)} %collective-permute-done.3.refs_3_), channel_id=1, source_target_pairs={{0,1},{1,0},{16,17},{17,16},{2,3},{3,2},{18,19},{19,18},{4,5},{5,4... | collective-permute-start | bytes 1179656 | tf_op jit(solution)/shard_map/ppermute | solution.py:55
  34.3 1.6 %collective-permute-start.9 = (bf16[144,1024]{1,0:T(8,128)(2,1)S(1)}, bf16[144,1024]{1,0:T(8,128)(2,1)S(1)}, u32[]{:S(2)}, u32[]{:S(2)}) collective-permute-start(bf16[144,1024]{1,0:T(8,128)(2,1)S(1)} %collective-permute-done.7.refs_2_), channel_id=1, source_target_pairs={{0,1},{1,0},{16,17},{17,16},{2,3},{3,2},{18,19},{19,18},{4,5},{5,4... | collective-permute-start | bytes 884744 | tf_op jit(solution)/shard_map/ppermute | solution.py:55
  41.4 1.5 %collective-permute-start.10 = (f32[8,48,128]{2,1,0:T(8,128)S(1)}, f32[8,48,128]{2,1,0:T(8,128)S(1)}, u32[]{:S(2)}, u32[]{:S(2)}) collective-permute-start(f32[8,48,128]{2,1,0:T(8,128)S(1)} %get-tuple-element.42), channel_id=1, source_target_pairs={{0,1},{1,0},{16,17},{17,16},{2,3},{3,2},{18,19},{19,18},{4,5},{5,4... | collective-permute-start | bytes 589832 | tf_op jit(solution)/shard_map/ppermute | solution.py:55

commit v6 on v4

--- a/solution.py
+++ b/solution.py
@@ -122,18 +122,20 @@
                 inner.reshape(K_STEP, K_INP, w) * chosen[None], axis=1
             )
 
+    blocks = []
     for at, d, own in call.blocks:
-        kept = (odd == core) if own else (odd != core)
         owner = lax.rem(z - d * (1 - 2 * core) + NZ, NZ)
-        block = pack(total[:, at : at + BLOCK])
-
-        @pl.when(kept)
-        def _(block=block, owner=owner):
-            keep[owner] = block
-
-        @pl.when(jnp.logical_not(kept))
-        def _(block=block, owner=owner):
-            give[owner] = block
+        blocks.append((own, owner, pack(total[:, at : at + BLOCK])))
+
+    @pl.when(odd == core)
+    def _():
+        for own, owner, block in blocks:
+            (keep if own else give)[owner] = block
+
+    @pl.when(odd != core)
+    def _():
+        for own, owner, block in blocks:
+            (give if own else keep)[owner] = block
 
 
 class Call(NamedTuple):
@@ -262,11 +264,25 @@
     far_x = along_x(far)
     far_swap = swap(far)
     near_x_swap = swap(near_x)
-    first, second = far_calls(((1, False), (2, False), True))
-    give, keep, sums = partial_sums(first, where, held, [near_x, far], [give, keep])
-    give, keep, sums = partial_sums(
-        second, where, held, [far, far_swap], [give, keep, sums]
-    )
+    call = Call(
+        "plain",
+        0,
+        5 * BLOCK,
+        (
+            (0, 0, 2 * BLOCK, 0, None),
+            (1, 0, BLOCK, 2 * BLOCK, None),
+            (2, 0, BLOCK, 3 * BLOCK, None),
+            (1, BLOCK, HALF, 4 * BLOCK, 0),
+            (2, BLOCK, HALF, 4 * BLOCK, 1),
+        ),
+        tuple(
+            (n * BLOCK, d, own)
+            for n, (d, own) in enumerate(
+                ((1, False), (2, False), (3, True), (-3, True), (4, True))
+            )
+        ),
+    )
+    give, keep = partial_sums(call, where, held, [near_x, far, far_swap], [give, keep])
 
     far_x, give = lax.optimization_barrier((far_x, give))
     far_x_swap = swap(far_x)

time: 59.4 us -> 57.8 us (0.973)
  Pallas kernels: 27 us -> 24.8 us
    pallas_call x6 -> x5, Pallas kernels: 26.3 us -> 24.1 us  [partial_sums(): pl.pallas_call(functools.partial(collide, call), in_specs=in_specs, out_s...]
  transfers between devices with their start and end apart: 11 -> 11, of which waited for: 2 -> 3; matrix products, arithmetic and copies ran while one was open for 0% -> 0% of each run, Pallas kernels for 39% -> 36%
where the time goes in v6:
time: 57.8 us; the launch traced here: 57.2 us
  Pallas kernels  24.8 us (43%)
  blocking collectives  14 us (24%)
  starting transfers between devices  13.9 us (24%)
  waiting for transfers between devices  4.22 us (7%)
    pallas_call x5, Pallas kernels, partial_sums(): pl.pallas_call(functools.partial(collide, call), in_specs=in_specs, out_s...  24.1 us
    all_to_all x1, blocking collectives, local(): lax.all_to_all(pair, 'inp', 0, 0, tiled=True, axis_index_groups=groups)  14 us
    ppermute x3, starting transfers between devices, along_z(): return lax.ppermute(array, AXES, hop(lambda c: (0, 0, d * sign(c), 0)))  7.72 us
    ppermute x3, starting transfers between devices, along_x(): return lax.ppermute(array, AXES, hop(lambda c: (sign(c), 0, 0, 0)))  4.08 us
    ppermute x3, waiting for transfers between devices, along_z(): return lax.ppermute(array, AXES, hop(lambda c: (0, 0, d * sign(c), 0)))  3.04 us
    ppermute x5, starting transfers between devices, swap(): return lax.ppermute(array, AXES, hop(lambda c: (0, 0, 0, 1)))  2.14 us
  transfers between devices with their start and end apart: 11, of which 3 were waited for; matrix products, arithmetic and copies ran while one was open for 0% of the time, Pallas kernels for 36%

profile of v6, /device:TPU:32, one launch (start us, length us, event | category | flops | bytes accessed | tf_op | source)
XLA Modules:
  0.0 57.2 jit_solution(17597443397646190504)
XLA Ops:
  0.0 1.9 %collective-permute-start = (bf16[96,1024]{1,0:T(8,128)(2,1)}, bf16[96,1024]{1,0:T(8,128)(2,1)S(1)}, u32[]{:S(2)}, u32[]{:S(2)}) collective-permute-start(bf16[96,1024]{1,0:T(8,128)(2,1)} %refs_1_.1), channel_id=1, source_target_pairs={{0,32},{1,225},{16,48},{17,241},{2,34},{3,227},{18,50},{19,243},{4... | collective-permute-start | bytes 589832 | tf_op jit(solution)/shard_map/ppermute | solution.py:48
  1.9 4.5 %collective-permute-start.1 = (bf16[96,1024]{1,0:T(8,128)(2,1)}, bf16[96,1024]{1,0:T(8,128)(2,1)S(1)}, u32[]{:S(2)}, u32[]{:S(2)}) collective-permute-start(bf16[96,1024]{1,0:T(8,128)(2,1)} %refs_1_.1), channel_id=1, source_target_pairs={{0,64},{1,193},{16,80},{17,209},{2,66},{3,195},{18,82},{19,211},{4... | collective-permute-start | bytes 589832 | tf_op jit(solution)/shard_map/ppermute | solution.py:48
  6.4 1.5 %collective-permute-start.2 = (bf16[96,1024]{1,0:T(8,128)(2,1)}, bf16[96,1024]{1,0:T(8,128)(2,1)S(1)}, u32[]{:S(2)}, u32[]{:S(2)}) collective-permute-start(bf16[96,1024]{1,0:T(8,128)(2,1)} %refs_1_.1), channel_id=1, source_target_pairs={{0,16},{1,19},{16,2},{17,1},{2,18},{3,17},{18,0},{19,3},{4,20},{5,... | collective-permute-start | bytes 589832 | tf_op jit(solution)/shard_map/ppermute | solution.py:52
  7.9 0.1 stack.23.where
  8.0 6.6 %shard_map.28 = (f32[8,48,128]{2,1,0:T(8,128)S(1)}, f32[8,48,128]{2,1,0:T(8,128)S(1)}, bf16[64,64,1024]{2,1,0:T(8,128)(2,1)S(1)}) custom-call(s32[5]{0:T(128)S(1)} %stack.23.where, bf16[64,64,1024]{2,1,0:T(8,128)(2,1)} %refs_0_.1, bf16[96,1024]{1,0:T(8,128)(2,1)} %refs_1_.1), custom_call_target="tpu_custom_call" | custom-call | flops 805306368 | bytes 16777216 | tf_op jit(solution)/shard_map/pallas_call | solution.py:170
  14.5 0.0 collective-permute-done
  14.6 0.0 collective-permute-done.2.refs_3_
  14.6 0.4 collective-permute-start.4
  15.0 1.3 %collective-permute-start.3 = (bf16[144,1024]{1,0:T(8,128)(2,1)S(1)}, bf16[144,1024]{1,0:T(8,128)(2,1)S(1)}, u32[]{:S(2)}, u32[]{:S(2)}) collective-permute-start(bf16[144,1024]{1,0:T(8,128)(2,1)S(1)} %pad_maximum_fusion), channel_id=1, source_target_pairs={{0,64},{1,193},{16,80},{17,209},{2,66},{3,195},{18,82},{19,211},{4... | collective-permute-start | bytes 884744 | tf_op jit(solution)/shard_map/ppermute | solution.py:48
  16.3 1.5 %collective-permute-start.6 = (bf16[192,1024]{1,0:T(8,128)(2,1)S(1)}, bf16[192,1024]{1,0:T(8,128)(2,1)S(1)}, u32[]{:S(2)}, u32[]{:S(2)}) collective-permute-start(bf16[192,1024]{1,0:T(8,128)(2,1)S(1)} %constant_dynamic-update-slice_fusion.refs_1_), channel_id=1, source_target_pairs={{0,16},{1,19},{16,2},{17,1},{2,18},{3,17},{18,0},{19,3},{4,20},{5,... | collective-permute-start | bytes 1179656 | tf_op jit(solution)/shard_map/ppermute | solution.py:52
  17.8 5.5 %shard_map.29 = (f32[8,48,128]{2,1,0:T(8,128)S(1)}, f32[8,48,128]{2,1,0:T(8,128)S(1)}) custom-call(s32[5]{0:T(128)S(1)} %stack.23.where, bf16[64,64,1024]{2,1,0:T(8,128)(2,1)S(1)} %get-tuple-element.27.refs_0_, bf16[192,1024]{1,0:T(8,128)(2,1)S(1)} %constant_dynamic-update-slice_fusion.refs_1_, ...), custom_call_target="tpu_custom_call", output_to_operand_aliasing={{0}: (5, {}), {1}: (6, {})} | custom-call | flops 4026531840 | bytes 1048576 | tf_op jit(solution)/shard_map/pallas_call | solution.py:170
  23.3 3.0 %collective-permute-done.3.refs_2_ = bf16[144,1024]{1,0:T(8,128)(2,1)S(1)} collective-permute-done((bf16[144,1024]{1,0:T(8,128)(2,1)S(1)}, bf16[144,1024]{1,0:T(8,128)(2,1)S(1)}, u32[]{:S(2)}, u32[]{:S(2)}) %collective-permute-start.3) | collective-permute-done | bytes 294944 | tf_op jit(solution)/shard_map/ppermute | solution.py:48
  26.4 0.0 collective-permute-start.7
  26.4 1.1 %collective-permute-start.5 = (bf16[144,1024]{1,0:T(8,128)(2,1)S(1)}, bf16[144,1024]{1,0:T(8,128)(2,1)S(1)}, u32[]{:S(2)}, u32[]{:S(2)}) collective-permute-start(bf16[144,1024]{1,0:T(8,128)(2,1)S(1)} %collective-permute-done.3.refs_2_), channel_id=1, source_target_pairs={{0,16},{1,19},{16,2},{17,1},{2,18},{3,17},{18,0},{19,3},{4,20},{5,... | collective-permute-start | bytes 884744 | tf_op jit(solution)/shard_map/ppermute | solution.py:52
  27.5 1.2 %collective-permute-start.9 = (bf16[192,1024]{1,0:T(8,128)(2,1)S(1)}, bf16[192,1024]{1,0:T(8,128)(2,1)S(1)}, u32[]{:S(2)}, u32[]{:S(2)}) collective-permute-start(bf16[192,1024]{1,0:T(8,128)(2,1)S(1)} %collective-permute-done.6.refs_1_), channel_id=1, source_target_pairs={{0,1},{1,0},{16,17},{17,16},{2,3},{3,2},{18,19},{19,18},{4,5},{5,4... | collective-permute-start | bytes 1179656 | tf_op jit(solution)/shard_map/ppermute | solution.py:56
  28.6 5.5 %shard_map.30 = (f32[8,48,128]{2,1,0:T(8,128)S(1)}, f32[8,48,128]{2,1,0:T(8,128)S(1)}) custom-call(s32[5]{0:T(128)S(1)} %stack.23.where, bf16[64,64,1024]{2,1,0:T(8,128)(2,1)S(1)} %get-tuple-element.27.refs_0_, bf16[192,1024]{1,0:T(8,128)(2,1)S(1)} %collective-permute-done.6.refs_1_, ...), custom_call_target="tpu_custom_call", output_to_operand_aliasing={{0}: (5, {}), {1}: (6, {})} | custom-call | flops 4026531840 | bytes 1048576 | tf_op jit(solution)/shard_map/pallas_call | solution.py:170
  34.2 0.1 collective-permute-done.5.refs_2_.refs_1_
  34.3 0.0 collective-permute-start.8
  34.3 3.2 %shard_map.31 = (f32[8,48,128]{2,1,0:T(8,128)S(1)}, f32[8,48,128]{2,1,0:T(8,128)S(1)}, f32[64,512]{1,0:T(8,128)S(1)}) custom-call(s32[5]{0:T(128)S(1)} %stack.23.where, bf16[64,64,1024]{2,1,0:T(8,128)(2,1)S(1)} %get-tuple-element.27.refs_0_, bf16[192,1024]{1,0:T(8,128)(2,1)S(1)} %collective-permute-done.9.refs_1_, ...), custom_call_target="tpu_custom_call", output_to_operand_aliasing={{0}: (4, {}), {1}: (5, {})} | custom-call | flops 2147483648 | bytes 1048576 | tf_op jit(solution)/shard_map/pallas_call | solution.py:170
  37.5 3.3 %shard_map.32 = (f32[8,48,128]{2,1,0:T(8,128)S(1)}, f32[8,48,128]{2,1,0:T(8,128)S(1)}, f32[64,512]{1,0:T(8,128)S(1)}) custom-call(s32[5]{0:T(128)S(1)} %stack.23.where, bf16[64,64,1024]{2,1,0:T(8,128)(2,1)S(1)} %get-tuple-element.27.refs_0_, ...), custom_call_target="tpu_custom_call", output_to_operand_aliasing={{0}: (4, {}), {1}: (5, {}), {2}: (6, {})} | custom-call | flops 1879048192 | bytes 1048576 | tf_op jit(solution)/shard_map/pallas_call | solution.py:170
  40.8 0.6 %collective-permute-start.10 = (f32[8,48,128]{2,1,0:T(8,128)S(1)}, f32[8,48,128]{2,1,0:T(8,128)S(1)}, u32[]{:S(2)}, u32[]{:S(2)}) collective-permute-start(f32[8,48,128]{2,1,0:T(8,128)S(1)} %get-tuple-element.48), channel_id=1, source_target_pairs={{0,1},{1,0},{16,17},{17,16},{2,3},{3,2},{18,19},{19,18},{4,5},{5,4... | collective-permute-start | bytes 589832 | tf_op jit(solution)/shard_map/ppermute | solution.py:56
  41.4 1.1 %collective-permute-done.10.theirs = f32[8,48,128]{2,1,0:T(8,128)S(1)} collective-permute-done((f32[8,48,128]{2,1,0:T(8,128)S(1)}, f32[8,48,128]{2,1,0:T(8,128)S(1)}, u32[]{:S(2)}, u32[]{:S(2)}) %collective-permute-start.10) | collective-permute-done | bytes 196640 | tf_op jit(solution)/shard_map/ppermute | solution.py:56
  42.5 14.0 %all_to_all.5.shares = f32[8,48,128]{2,1,0:T(8,128)S(1)} all-to-all(f32[8,48,128]{2,1,0:T(8,128)S(1)} %shard_map.33), channel_id=1, replica_groups={{0,2,4,6,8,10,12,14},{1,3,5,7,9,11,13,15},{16,18,20,22,24,26,28,30},{17..., dimensions={0} | all-to-all | bytes 393216 | tf_op jit(solution)/shard_map/all_to_all | solution.py:306
  56.5 0.7 %shard_map.34 = bf16[64,96]{1,0:T(8,128)(2,1)} custom-call(f32[8,48,128]{2,1,0:T(8,128)S(1)} %all_to_all.5.shares), custom_call_target="tpu_custom_call" | custom-call | tf_op jit(solution)/shard_map/pallas_call | solution.py:307
  (11 shorter events, 0.1 us)
Async XLA Ops:
  0.0 14.5 %collective-permute-start = (bf16[96,1024]{1,0:T(8,128)(2,1)}, bf16[96,1024]{1,0:T(8,128)(2,1)S(1)}, u32[]{:S(2)}, u32[]{:S(2)}) collective-permute-start(bf16[96,1024]{1,0:T(8,128)(2,1)} %refs_1_.1), channel_id=1, source_target_pairs={{0,32},{1,225},{16,48},{17,241},{2,34},{3,227},{18,50},{19,243},{4... | collective-permute-start | bytes 589832 | tf_op jit(solution)/shard_map/ppermute | solution.py:48
  1.9 12.6 %collective-permute-start.1 = (bf16[96,1024]{1,0:T(8,128)(2,1)}, bf16[96,1024]{1,0:T(8,128)(2,1)S(1)}, u32[]{:S(2)}, u32[]{:S(2)}) collective-permute-start(bf16[96,1024]{1,0:T(8,128)(2,1)} %refs_1_.1), channel_id=1, source_target_pairs={{0,64},{1,193},{16,80},{17,209},{2,66},{3,195},{18,82},{19,211},{4... | collective-permute-start | bytes 589832 | tf_op jit(solution)/shard_map/ppermute | solution.py:48
  6.4 8.2 %collective-permute-start.2 = (bf16[96,1024]{1,0:T(8,128)(2,1)}, bf16[96,1024]{1,0:T(8,128)(2,1)S(1)}, u32[]{:S(2)}, u32[]{:S(2)}) collective-permute-start(bf16[96,1024]{1,0:T(8,128)(2,1)} %refs_1_.1), channel_id=1, source_target_pairs={{0,16},{1,19},{16,2},{17,1},{2,18},{3,17},{18,0},{19,3},{4,20},{5,... | collective-permute-start | bytes 589832 | tf_op jit(solution)/shard_map/ppermute | solution.py:52
  14.6 3.2 %collective-permute-start.4 = (bf16[192,1024]{1,0:T(8,128)(2,1)S(1)}, bf16[192,1024]{1,0:T(8,128)(2,1)S(1)}, u32[]{:S(2)}, u32[]{:S(2)}) collective-permute-start(bf16[192,1024]{1,0:T(8,128)(2,1)S(1)} %constant_dynamic-update-slice_fusion.refs_1_), channel_id=1, source_target_pairs={{0,1},{1,0},{16,17},{17,16},{2,3},{3,2},{18,19},{19,18},{4,5},{5,4... | collective-permute-start | bytes 1179656 | tf_op jit(solution)/shard_map/ppermute | solution.py:56
  15.0 11.3 %collective-permute-start.3 = (bf16[144,1024]{1,0:T(8,128)(2,1)S(1)}, bf16[144,1024]{1,0:T(8,128)(2,1)S(1)}, u32[]{:S(2)}, u32[]{:S(2)}) collective-permute-start(bf16[144,1024]{1,0:T(8,128)(2,1)S(1)} %pad_maximum_fusion), channel_id=1, source_target_pairs={{0,64},{1,193},{16,80},{17,209},{2,66},{3,195},{18,82},{19,211},{4... | collective-permute-start | bytes 884744 | tf_op jit(solution)/shard_map/ppermute | solution.py:48
  16.3 11.1 %collective-permute-start.6 = (bf16[192,1024]{1,0:T(8,128)(2,1)S(1)}, bf16[192,1024]{1,0:T(8,128)(2,1)S(1)}, u32[]{:S(2)}, u32[]{:S(2)}) collective-permute-start(bf16[192,1024]{1,0:T(8,128)(2,1)S(1)} %constant_dynamic-update-slice_fusion.refs_1_), channel_id=1, source_target_pairs={{0,16},{1,19},{16,2},{17,1},{2,18},{3,17},{18,0},{19,3},{4,20},{5,... | collective-permute-start | bytes 1179656 | tf_op jit(solution)/shard_map/ppermute | solution.py:52
  26.4 2.3 %collective-permute-start.7 = (bf16[144,1024]{1,0:T(8,128)(2,1)S(1)}, bf16[144,1024]{1,0:T(8,128)(2,1)S(1)}, u32[]{:S(2)}, u32[]{:S(2)}) collective-permute-start(bf16[144,1024]{1,0:T(8,128)(2,1)S(1)} %collective-permute-done.3.refs_2_), channel_id=1, source_target_pairs={{0,1},{1,0},{16,17},{17,16},{2,3},{3,2},{18,19},{19,18},{4,5},{5,4... | collective-permute-start | bytes 884744 | tf_op jit(solution)/shard_map/ppermute | solution.py:56
  26.4 7.9 %collective-permute-start.5 = (bf16[144,1024]{1,0:T(8,128)(2,1)S(1)}, bf16[144,1024]{1,0:T(8,128)(2,1)S(1)}, u32[]{:S(2)}, u32[]{:S(2)}) collective-permute-start(bf16[144,1024]{1,0:T(8,128)(2,1)S(1)} %collective-permute-done.3.refs_2_), channel_id=1, source_target_pairs={{0,16},{1,19},{16,2},{17,1},{2,18},{3,17},{18,0},{19,3},{4,20},{5,... | collective-permute-start | bytes 884744 | tf_op jit(solution)/shard_map/ppermute | solution.py:52
  27.5 6.9 %collective-permute-start.9 = (bf16[192,1024]{1,0:T(8,128)(2,1)S(1)}, bf16[192,1024]{1,0:T(8,128)(2,1)S(1)}, u32[]{:S(2)}, u32[]{:S(2)}) collective-permute-start(bf16[192,1024]{1,0:T(8,128)(2,1)S(1)} %collective-permute-done.6.refs_1_), channel_id=1, source_target_pairs={{0,1},{1,0},{16,17},{17,16},{2,3},{3,2},{18,19},{19,18},{4,5},{5,4... | collective-permute-start | bytes 1179656 | tf_op jit(solution)/shard_map/ppermute | solution.py:56
  34.3 3.2 %collective-permute-start.8 = (bf16[144,1024]{1,0:T(8,128)(2,1)S(1)}, bf16[144,1024]{1,0:T(8,128)(2,1)S(1)}, u32[]{:S(2)}, u32[]{:S(2)}) collective-permute-start(bf16[144,1024]{1,0:T(8,128)(2,1)S(1)} %collective-permute-done.5.refs_2_.refs_1_), channel_id=1, source_target_pairs={{0,1},{1,0},{16,17},{17,16},{2,3},{3,2},{18,19},{19,18},{4,5},{5,4... | collective-permute-start | bytes 884744 | tf_op jit(solution)/shard_map/ppermute | solution.py:56
  40.8 1.7 %collective-permute-start.10 = (f32[8,48,128]{2,1,0:T(8,128)S(1)}, f32[8,48,128]{2,1,0:T(8,128)S(1)}, u32[]{:S(2)}, u32[]{:S(2)}) collective-permute-start(f32[8,48,128]{2,1,0:T(8,128)S(1)} %get-tuple-element.48), channel_id=1, source_target_pairs={{0,1},{1,0},{16,17},{17,16},{2,3},{3,2},{18,19},{19,18},{4,5},{5,4... | collective-permute-start | bytes 589832 | tf_op jit(solution)/shard_map/ppermute | solution.py:56

commit v7 on v6

--- a/solution.py
+++ b/solution.py
@@ -14,7 +14,7 @@
 HALF = BLOCK // 2
 K_OUT = 64
 K_INP = 64
-K_STEP = 32
+K_STEP = 64
 TILE = 256
 VMEM = pl.BlockSpec(memory_space=pltpu.VMEM)
 SMEM = pl.BlockSpec(memory_space=pltpu.SMEM)
@@ -35,7 +35,7 @@
         for y in range(NY):
             for x in range(NX):
                 for c in range(NC):
-                    dx, dy, dz, dc = way(c)
+                    dx, dy, dz, dc = way(c, x)
                     pairs.append((device(x, y, z, c), device(x + dx, y + dy, z + dz, c + dc)))
     return pairs
 
@@ -45,15 +45,15 @@
 
 
 def along_z(array, d):
-    return lax.ppermute(array, AXES, hop(lambda c: (0, 0, d * sign(c), 0)))
+    return lax.ppermute(array, AXES, hop(lambda c, x: (0, 0, d * sign(c), 0)))
 
 
 def along_x(array):
-    return lax.ppermute(array, AXES, hop(lambda c: (sign(c), 0, 0, 0)))
+    return lax.ppermute(array, AXES, hop(lambda c, x: (sign((x + c) % 2), 0, 0, 0)))
 
 
 def swap(array):
-    return lax.ppermute(array, AXES, hop(lambda c: (0, 0, 0, 1)))
+    return lax.ppermute(array, AXES, hop(lambda c, x: (0, 0, 0, 1)))
 
 
 def rows(*arrays):
@@ -212,10 +212,6 @@
     out[...] = mine[...] + theirs[...]
 
 
-def add_up(shares, out):
-    out[...] = unpack(jnp.sum(shares[...], axis=0)).astype(jnp.bfloat16)
-
-
 def local(tensor, state):
     out_at, inp_at = lax.axis_index("out"), lax.axis_index("inp")
     z, odd, core = out_at // 2, out_at % 2, inp_at % 2
@@ -304,13 +300,7 @@
     )(keep, got)
     groups = [[c + NC * i for i in range(NZ)] for c in range(NC)]
     shares = lax.all_to_all(pair, "inp", 0, 0, tiled=True, axis_index_groups=groups)
-    done = pl.pallas_call(
-        add_up,
-        in_specs=[VMEM],
-        out_specs=VMEM,
-        out_shape=jax.ShapeDtypeStruct((K_OUT, BLOCK), jnp.bfloat16),
-        compiler_params=SMALL,
-    )(shares)
+    done = unpack(jnp.sum(shares, axis=0)).astype(jnp.bfloat16)
     return done.T
 
 

time: 57.8 us -> 57.7 us (level)
  Pallas kernels: 24.8 us -> 23.9 us
  waiting for transfers between devices: 4.22 us -> 5.12 us
  starting transfers between devices: 13.9 us -> 13.1 us
  other arithmetic: 0.02 us -> 0.72 us
    ppermute x11, waiting for transfers between devices: 4.22 us -> 5.12 us  [the longest x3 4.03 us: along_z(): return lax.ppermute(array, AXES, hop(lambda c, x: (0, 0, d * sign(c), 0)))]
    ppermute x11, starting transfers between devices: 13.9 us -> 13.1 us  [the longest x3 7.71 us: along_z(): return lax.ppermute(array, AXES, hop(lambda c, x: (0, 0, d * sign(c), 0)))]
    pallas_call x1 -> x0, Pallas kernels: 0.69 us -> none  [local(): pl.pallas_call(add_up, in_specs=[VMEM], out_specs=VMEM, out_shape=jax.Sha...]
    transpose x0 -> x1, other arithmetic: none -> 0.69 us  [local(): return done.T]
  transfers between devices with their start and end apart: 11 -> 11, of which waited for: 3 -> 2; matrix products, arithmetic and copies ran while one was open for 0% -> 0% of each run, Pallas kernels for 36% -> 36%
where the time goes in v7:
time: 57.7 us; the launch traced here: 57.1 us
  Pallas kernels  23.9 us (41%)
  blocking collectives  14 us (24%)
  starting transfers between devices  13.1 us (23%)
  waiting for transfers between devices  5.12 us (9%)
  other arithmetic  0.72 us (1%)
    pallas_call x5, Pallas kernels, partial_sums(): pl.pallas_call(functools.partial(collide, call), in_specs=in_specs, out_s...  23.9 us
    all_to_all x1, blocking collectives, local(): lax.all_to_all(pair, 'inp', 0, 0, tiled=True, axis_index_groups=groups)  14 us
    ppermute x3, starting transfers between devices, along_z(): return lax.ppermute(array, AXES, hop(lambda c, x: (0, 0, d * sign(c), 0)))  7.71 us
    ppermute x3, waiting for transfers between devices, along_z(): return lax.ppermute(array, AXES, hop(lambda c, x: (0, 0, d * sign(c), 0)))  4.03 us
    ppermute x3, starting transfers between devices, along_x(): lax.ppermute(array, AXES, hop(lambda c, x: (sign((x + c) % 2), 0, 0, 0)))  3.06 us
    ppermute x5, starting transfers between devices, swap(): return lax.ppermute(array, AXES, hop(lambda c, x: (0, 0, 0, 1)))  2.3 us
  transfers between devices with their start and end apart: 11, of which 2 were waited for; matrix products, arithmetic and copies ran while one was open for 0% of the time, Pallas kernels for 36%

profile of v7, /device:TPU:32, one launch (start us, length us, event | category | flops | bytes accessed | tf_op | source)
XLA Modules:
  0.0 57.1 jit_solution(11931551973887780754)
XLA Ops:
  0.0 1.9 %collective-permute-start = (bf16[96,1024]{1,0:T(8,128)(2,1)}, bf16[96,1024]{1,0:T(8,128)(2,1)S(1)}, u32[]{:S(2)}, u32[]{:S(2)}) collective-permute-start(bf16[96,1024]{1,0:T(8,128)(2,1)} %refs_1_.1), channel_id=1, source_target_pairs={{0,32},{1,225},{16,48},{17,241},{2,34},{3,227},{18,50},{19,243},{4... | collective-permute-start | bytes 589832 | tf_op jit(solution)/shard_map/ppermute | solution.py:48
  1.9 4.5 %collective-permute-start.1 = (bf16[96,1024]{1,0:T(8,128)(2,1)}, bf16[96,1024]{1,0:T(8,128)(2,1)S(1)}, u32[]{:S(2)}, u32[]{:S(2)}) collective-permute-start(bf16[96,1024]{1,0:T(8,128)(2,1)} %refs_1_.1), channel_id=1, source_target_pairs={{0,64},{1,193},{16,80},{17,209},{2,66},{3,195},{18,82},{19,211},{4... | collective-permute-start | bytes 589832 | tf_op jit(solution)/shard_map/ppermute | solution.py:48
  6.4 1.5 %collective-permute-start.2 = (bf16[96,1024]{1,0:T(8,128)(2,1)}, bf16[96,1024]{1,0:T(8,128)(2,1)S(1)}, u32[]{:S(2)}, u32[]{:S(2)}) collective-permute-start(bf16[96,1024]{1,0:T(8,128)(2,1)} %refs_1_.1), channel_id=1, source_target_pairs={{0,16},{1,19},{16,0},{17,3},{2,18},{3,17},{18,2},{19,1},{4,20},{5,... | collective-permute-start | bytes 589832 | tf_op jit(solution)/shard_map/ppermute | solution.py:52
  7.9 0.1 stack.23.where
  8.0 6.6 %shard_map.28 = (f32[8,48,128]{2,1,0:T(8,128)S(1)}, f32[8,48,128]{2,1,0:T(8,128)S(1)}, bf16[64,64,1024]{2,1,0:T(8,128)(2,1)S(1)}) custom-call(s32[5]{0:T(128)S(1)} %stack.23.where, bf16[64,64,1024]{2,1,0:T(8,128)(2,1)} %refs_0_.1, bf16[96,1024]{1,0:T(8,128)(2,1)} %refs_1_.1), custom_call_target="tpu_custom_call" | custom-call | flops 805306368 | bytes 16777216 | tf_op jit(solution)/shard_map/pallas_call | solution.py:170
  14.6 0.0 collective-permute-done
  14.6 0.0 collective-permute-done.1
  14.6 0.4 collective-permute-start.4
  15.0 1.3 %collective-permute-start.3 = (bf16[144,1024]{1,0:T(8,128)(2,1)S(1)}, bf16[144,1024]{1,0:T(8,128)(2,1)S(1)}, u32[]{:S(2)}, u32[]{:S(2)}) collective-permute-start(bf16[144,1024]{1,0:T(8,128)(2,1)S(1)} %pad_maximum_fusion), channel_id=1, source_target_pairs={{0,64},{1,193},{16,80},{17,209},{2,66},{3,195},{18,82},{19,211},{4... | collective-permute-start | bytes 884744 | tf_op jit(solution)/shard_map/ppermute | solution.py:48
  16.3 0.5 collective-permute-start.6
  16.9 0.0 collective-permute-done.4.refs_2_
  16.9 5.5 %shard_map.29 = (f32[8,48,128]{2,1,0:T(8,128)S(1)}, f32[8,48,128]{2,1,0:T(8,128)S(1)}) custom-call(s32[5]{0:T(128)S(1)} %stack.23.where, bf16[64,64,1024]{2,1,0:T(8,128)(2,1)S(1)} %get-tuple-element.27.refs_0_, bf16[192,1024]{1,0:T(8,128)(2,1)S(1)} %constant_dynamic-update-slice_fusion.refs_1_, ...), custom_call_target="tpu_custom_call", output_to_operand_aliasing={{0}: (5, {}), {1}: (6, {})} | custom-call | flops 4026531840 | bytes 1048576 | tf_op jit(solution)/shard_map/pallas_call | solution.py:170
  22.3 4.0 %collective-permute-done.3.refs_2_ = bf16[144,1024]{1,0:T(8,128)(2,1)S(1)} collective-permute-done((bf16[144,1024]{1,0:T(8,128)(2,1)S(1)}, bf16[144,1024]{1,0:T(8,128)(2,1)S(1)}, u32[]{:S(2)}, u32[]{:S(2)}) %collective-permute-start.3) | collective-permute-done | bytes 294944 | tf_op jit(solution)/shard_map/ppermute | solution.py:48
  26.4 1.0 %collective-permute-start.5 = (bf16[144,1024]{1,0:T(8,128)(2,1)S(1)}, bf16[144,1024]{1,0:T(8,128)(2,1)S(1)}, u32[]{:S(2)}, u32[]{:S(2)}) collective-permute-start(bf16[144,1024]{1,0:T(8,128)(2,1)S(1)} %collective-permute-done.3.refs_2_), channel_id=1, source_target_pairs={{0,16},{1,19},{16,0},{17,3},{2,18},{3,17},{18,2},{19,1},{4,20},{5,... | collective-permute-start | bytes 884744 | tf_op jit(solution)/shard_map/ppermute | solution.py:52
  27.4 1.2 %collective-permute-start.9 = (bf16[192,1024]{1,0:T(8,128)(2,1)S(1)}, bf16[192,1024]{1,0:T(8,128)(2,1)S(1)}, u32[]{:S(2)}, u32[]{:S(2)}) collective-permute-start(bf16[192,1024]{1,0:T(8,128)(2,1)S(1)} %collective-permute-done.6.refs_1_), channel_id=1, source_target_pairs={{0,1},{1,0},{16,17},{17,16},{2,3},{3,2},{18,19},{19,18},{4,5},{5,4... | collective-permute-start | bytes 1179656 | tf_op jit(solution)/shard_map/ppermute | solution.py:56
  28.6 5.6 %shard_map.30 = (f32[8,48,128]{2,1,0:T(8,128)S(1)}, f32[8,48,128]{2,1,0:T(8,128)S(1)}) custom-call(s32[5]{0:T(128)S(1)} %stack.23.where, bf16[64,64,1024]{2,1,0:T(8,128)(2,1)S(1)} %get-tuple-element.27.refs_0_, bf16[192,1024]{1,0:T(8,128)(2,1)S(1)} %collective-permute-done.6.refs_1_, ...), custom_call_target="tpu_custom_call", output_to_operand_aliasing={{0}: (5, {}), {1}: (6, {})} | custom-call | flops 4026531840 | bytes 1048576 | tf_op jit(solution)/shard_map/pallas_call | solution.py:170
  34.2 0.1 collective-permute-start.8
  34.3 3.1 %shard_map.31 = (f32[8,48,128]{2,1,0:T(8,128)S(1)}, f32[8,48,128]{2,1,0:T(8,128)S(1)}, f32[64,512]{1,0:T(8,128)S(1)}) custom-call(s32[5]{0:T(128)S(1)} %stack.23.where, bf16[64,64,1024]{2,1,0:T(8,128)(2,1)S(1)} %get-tuple-element.27.refs_0_, bf16[192,1024]{1,0:T(8,128)(2,1)S(1)} %collective-permute-done.9.refs_1_, ...), custom_call_target="tpu_custom_call", output_to_operand_aliasing={{0}: (4, {}), {1}: (5, {})} | custom-call | flops 2147483648 | bytes 1048576 | tf_op jit(solution)/shard_map/pallas_call | solution.py:170
  37.5 3.2 %shard_map.32 = (f32[8,48,128]{2,1,0:T(8,128)S(1)}, f32[8,48,128]{2,1,0:T(8,128)S(1)}, f32[64,512]{1,0:T(8,128)S(1)}) custom-call(s32[5]{0:T(128)S(1)} %stack.23.where, bf16[64,64,1024]{2,1,0:T(8,128)(2,1)S(1)} %get-tuple-element.27.refs_0_, ...), custom_call_target="tpu_custom_call", output_to_operand_aliasing={{0}: (4, {}), {1}: (5, {}), {2}: (6, {})} | custom-call | flops 1879048192 | bytes 1048576 | tf_op jit(solution)/shard_map/pallas_call | solution.py:170
  40.7 0.6 %collective-permute-start.10 = (f32[8,48,128]{2,1,0:T(8,128)S(1)}, f32[8,48,128]{2,1,0:T(8,128)S(1)}, u32[]{:S(2)}, u32[]{:S(2)}) collective-permute-start(f32[8,48,128]{2,1,0:T(8,128)S(1)} %get-tuple-element.48), channel_id=1, source_target_pairs={{0,1},{1,0},{16,17},{17,16},{2,3},{3,2},{18,19},{19,18},{4,5},{5,4... | collective-permute-start | bytes 589832 | tf_op jit(solution)/shard_map/ppermute | solution.py:56
  41.3 1.1 %collective-permute-done.10.theirs = f32[8,48,128]{2,1,0:T(8,128)S(1)} collective-permute-done((f32[8,48,128]{2,1,0:T(8,128)S(1)}, f32[8,48,128]{2,1,0:T(8,128)S(1)}, u32[]{:S(2)}, u32[]{:S(2)}) %collective-permute-start.10) | collective-permute-done | bytes 196640 | tf_op jit(solution)/shard_map/ppermute | solution.py:56
  42.4 14.0 %all_to_all.5 = f32[8,48,128]{2,1,0:T(8,128)S(1)} all-to-all(f32[8,48,128]{2,1,0:T(8,128)S(1)} %shard_map.33), channel_id=1, replica_groups={{0,2,4,6,8,10,12,14},{1,3,5,7,9,11,13,15},{16,18,20,22,24,26,28,30},{17..., dimensions={0} | all-to-all | bytes 393216 | tf_op jit(solution)/shard_map/all_to_all | solution.py:302
  56.4 0.1 fusion
  56.4 0.7 %maximum_bitcast_fusion = bf16[96,64]{0,1:T(8,128)(2,1)} fusion(bf16[16,32]{1,0:T(8,128)(2,1)S(1)} %get-tuple-element.51, bf16[16,32]{1,0:T(8,128)(2,1)S(1)} %get-tuple-element.50, bf16[16,32]{1,0:T(8,128)(2,1)S(1)} %get-tuple-element.49, bf16[48,96]{1,0:T(8,128)(2,1)S(1)} %bitcast.8), kind=kLoop, calls=%fused_computation.1 | loop fusion | flops 49152 | bytes 24576 | tf_op jit(solution)/shard_map/transpose | solution.py:304
  (13 shorter events, 0.1 us)
Async XLA Ops:
  0.0 14.6 %collective-permute-start = (bf16[96,1024]{1,0:T(8,128)(2,1)}, bf16[96,1024]{1,0:T(8,128)(2,1)S(1)}, u32[]{:S(2)}, u32[]{:S(2)}) collective-permute-start(bf16[96,1024]{1,0:T(8,128)(2,1)} %refs_1_.1), channel_id=1, source_target_pairs={{0,32},{1,225},{16,48},{17,241},{2,34},{3,227},{18,50},{19,243},{4... | collective-permute-start | bytes 589832 | tf_op jit(solution)/shard_map/ppermute | solution.py:48
  1.9 12.6 %collective-permute-start.1 = (bf16[96,1024]{1,0:T(8,128)(2,1)}, bf16[96,1024]{1,0:T(8,128)(2,1)S(1)}, u32[]{:S(2)}, u32[]{:S(2)}) collective-permute-start(bf16[96,1024]{1,0:T(8,128)(2,1)} %refs_1_.1), channel_id=1, source_target_pairs={{0,64},{1,193},{16,80},{17,209},{2,66},{3,195},{18,82},{19,211},{4... | collective-permute-start | bytes 589832 | tf_op jit(solution)/shard_map/ppermute | solution.py:48
  6.4 8.2 %collective-permute-start.2 = (bf16[96,1024]{1,0:T(8,128)(2,1)}, bf16[96,1024]{1,0:T(8,128)(2,1)S(1)}, u32[]{:S(2)}, u32[]{:S(2)}) collective-permute-start(bf16[96,1024]{1,0:T(8,128)(2,1)} %refs_1_.1), channel_id=1, source_target_pairs={{0,16},{1,19},{16,0},{17,3},{2,18},{3,17},{18,2},{19,1},{4,20},{5,... | collective-permute-start | bytes 589832 | tf_op jit(solution)/shard_map/ppermute | solution.py:52
  14.6 2.2 %collective-permute-start.4 = (bf16[192,1024]{1,0:T(8,128)(2,1)S(1)}, bf16[192,1024]{1,0:T(8,128)(2,1)S(1)}, u32[]{:S(2)}, u32[]{:S(2)}) collective-permute-start(bf16[192,1024]{1,0:T(8,128)(2,1)S(1)} %constant_dynamic-update-slice_fusion.refs_1_), channel_id=1, source_target_pairs={{0,1},{1,0},{16,17},{17,16},{2,3},{3,2},{18,19},{19,18},{4,5},{5,4... | collective-permute-start | bytes 1179656 | tf_op jit(solution)/shard_map/ppermute | solution.py:56
  15.0 11.3 %collective-permute-start.3 = (bf16[144,1024]{1,0:T(8,128)(2,1)S(1)}, bf16[144,1024]{1,0:T(8,128)(2,1)S(1)}, u32[]{:S(2)}, u32[]{:S(2)}) collective-permute-start(bf16[144,1024]{1,0:T(8,128)(2,1)S(1)} %pad_maximum_fusion), channel_id=1, source_target_pairs={{0,64},{1,193},{16,80},{17,209},{2,66},{3,195},{18,82},{19,211},{4... | collective-permute-start | bytes 884744 | tf_op jit(solution)/shard_map/ppermute | solution.py:48
  16.3 11.1 %collective-permute-start.6 = (bf16[192,1024]{1,0:T(8,128)(2,1)S(1)}, bf16[192,1024]{1,0:T(8,128)(2,1)S(1)}, u32[]{:S(2)}, u32[]{:S(2)}) collective-permute-start(bf16[192,1024]{1,0:T(8,128)(2,1)S(1)} %constant_dynamic-update-slice_fusion.refs_1_), channel_id=1, source_target_pairs={{0,16},{1,19},{16,0},{17,3},{2,18},{3,17},{18,2},{19,1},{4,20},{5,... | collective-permute-start | bytes 1179656 | tf_op jit(solution)/shard_map/ppermute | solution.py:52
  26.4 2.3 %collective-permute-start.7 = (bf16[144,1024]{1,0:T(8,128)(2,1)S(1)}, bf16[144,1024]{1,0:T(8,128)(2,1)S(1)}, u32[]{:S(2)}, u32[]{:S(2)}) collective-permute-start(bf16[144,1024]{1,0:T(8,128)(2,1)S(1)} %collective-permute-done.3.refs_2_), channel_id=1, source_target_pairs={{0,1},{1,0},{16,17},{17,16},{2,3},{3,2},{18,19},{19,18},{4,5},{5,4... | collective-permute-start | bytes 884744 | tf_op jit(solution)/shard_map/ppermute | solution.py:56
  26.4 7.8 %collective-permute-start.5 = (bf16[144,1024]{1,0:T(8,128)(2,1)S(1)}, bf16[144,1024]{1,0:T(8,128)(2,1)S(1)}, u32[]{:S(2)}, u32[]{:S(2)}) collective-permute-start(bf16[144,1024]{1,0:T(8,128)(2,1)S(1)} %collective-permute-done.3.refs_2_), channel_id=1, source_target_pairs={{0,16},{1,19},{16,0},{17,3},{2,18},{3,17},{18,2},{19,1},{4,20},{5,... | collective-permute-start | bytes 884744 | tf_op jit(solution)/shard_map/ppermute | solution.py:52
  27.4 6.9 %collective-permute-start.9 = (bf16[192,1024]{1,0:T(8,128)(2,1)S(1)}, bf16[192,1024]{1,0:T(8,128)(2,1)S(1)}, u32[]{:S(2)}, u32[]{:S(2)}) collective-permute-start(bf16[192,1024]{1,0:T(8,128)(2,1)S(1)} %collective-permute-done.6.refs_1_), channel_id=1, source_target_pairs={{0,1},{1,0},{16,17},{17,16},{2,3},{3,2},{18,19},{19,18},{4,5},{5,4... | collective-permute-start | bytes 1179656 | tf_op jit(solution)/shard_map/ppermute | solution.py:56
  34.2 3.3 %collective-permute-start.8 = (bf16[144,1024]{1,0:T(8,128)(2,1)S(1)}, bf16[144,1024]{1,0:T(8,128)(2,1)S(1)}, u32[]{:S(2)}, u32[]{:S(2)}) collective-permute-start(bf16[144,1024]{1,0:T(8,128)(2,1)S(1)} %collective-permute-done.5.refs_2_.refs_1_), channel_id=1, source_target_pairs={{0,1},{1,0},{16,17},{17,16},{2,3},{3,2},{18,19},{19,18},{4,5},{5,4... | collective-permute-start | bytes 884744 | tf_op jit(solution)/shard_map/ppermute | solution.py:56
  40.7 1.7 %collective-permute-start.10 = (f32[8,48,128]{2,1,0:T(8,128)S(1)}, f32[8,48,128]{2,1,0:T(8,128)S(1)}, u32[]{:S(2)}, u32[]{:S(2)}) collective-permute-start(f32[8,48,128]{2,1,0:T(8,128)S(1)} %get-tuple-element.48), channel_id=1, source_target_pairs={{0,1},{1,0},{16,17},{17,16},{2,3},{3,2},{18,19},{19,18},{4,5},{5,4... | collective-permute-start | bytes 589832 | tf_op jit(solution)/shard_map/ppermute | solution.py:56

commit v8 on v7

--- a/solution.py
+++ b/solution.py
@@ -233,11 +233,12 @@
 
     one, two, same_x, give = lax.optimization_barrier((one, two, same_x, give))
     near = rows(one, two)
+    hops = half(two)
+    near, two, hops = lax.optimization_barrier((near, two, hops))
+    four = along_z(hops, 2)
+    three = along_z(two, 1)
+    near_x = along_x(near)
     near_swap = swap(near)
-    both = rows(one, half(two))
-    near, both = lax.optimization_barrier((near, both))
-    far = along_z(both, 2)
-    near_x = along_x(near)
     call = Call(
         "plain",
         0,
@@ -256,7 +257,8 @@
     )
     give, keep = partial_sums(call, where, held, [near, near_swap, same_x], [give, keep])
 
-    far, give = lax.optimization_barrier((far, give))
+    three, four, give = lax.optimization_barrier((three, four, give))
+    far = rows(three, four)
     far_x = along_x(far)
     far_swap = swap(far)
     near_x_swap = swap(near_x)

time: 57.7 us -> 56.8 us (0.984)
  waiting for transfers between devices: 5.12 us -> 1.1 us
  starting transfers between devices: 13.1 us -> 15.9 us
    ppermute x3 -> x4, waiting for transfers between devices: 4.03 us -> 0.01 us  [along_z(): return lax.ppermute(array, AXES, hop(lambda c, x: (0, 0, d * sign(c), 0)))]
    ppermute x3 -> x4, starting transfers between devices: 7.71 us -> 10.4 us  [along_z(): return lax.ppermute(array, AXES, hop(lambda c, x: (0, 0, d * sign(c), 0)))]
  transfers between devices with their start and end apart: 11 -> 12, of which waited for: 2 -> 1; matrix products, arithmetic and copies ran while one was open for 0% -> 0% of each run, Pallas kernels for 36% -> 37%
where the time goes in v8:
time: 56.8 us; the launch traced here: 56.3 us
  Pallas kernels  23.9 us (42%)
  starting transfers between devices  15.9 us (28%)
  blocking collectives  14.3 us (25%)
  waiting for transfers between devices  1.1 us (2%)
  other arithmetic  0.73 us (1%)
    pallas_call x5, Pallas kernels, partial_sums(): pl.pallas_call(functools.partial(collide, call), in_specs=in_specs, out_s...  23.9 us
    all_to_all x1, blocking collectives, local(): lax.all_to_all(pair, 'inp', 0, 0, tiled=True, axis_index_groups=groups)  14.3 us
    ppermute x4, starting transfers between devices, along_z(): return lax.ppermute(array, AXES, hop(lambda c, x: (0, 0, d * sign(c), 0)))  10.4 us
    ppermute x3, starting transfers between devices, along_x(): lax.ppermute(array, AXES, hop(lambda c, x: (sign((x + c) % 2), 0, 0, 0)))  3.56 us
    ppermute x5, starting transfers between devices, swap(): return lax.ppermute(array, AXES, hop(lambda c, x: (0, 0, 0, 1)))  1.93 us
  transfers between devices with their start and end apart: 12, of which 1 were waited for; matrix products, arithmetic and copies ran while one was open for 0% of the time, Pallas kernels for 37%

profile of v8, /device:TPU:32, one launch (start us, length us, event | category | flops | bytes accessed | tf_op | source)
XLA Modules:
  0.0 56.3 jit_solution(13653553800040144708)
XLA Ops:
  0.0 1.9 %collective-permute-start = (bf16[96,1024]{1,0:T(8,128)(2,1)}, bf16[96,1024]{1,0:T(8,128)(2,1)S(1)}, u32[]{:S(2)}, u32[]{:S(2)}) collective-permute-start(bf16[96,1024]{1,0:T(8,128)(2,1)} %refs_1_.1), channel_id=1, source_target_pairs={{0,32},{1,225},{16,48},{17,241},{2,34},{3,227},{18,50},{19,243},{4... | collective-permute-start | bytes 589832 | tf_op jit(solution)/shard_map/ppermute | solution.py:48
  1.9 4.5 %collective-permute-start.1 = (bf16[96,1024]{1,0:T(8,128)(2,1)}, bf16[96,1024]{1,0:T(8,128)(2,1)S(1)}, u32[]{:S(2)}, u32[]{:S(2)}) collective-permute-start(bf16[96,1024]{1,0:T(8,128)(2,1)} %refs_1_.1), channel_id=1, source_target_pairs={{0,64},{1,193},{16,80},{17,209},{2,66},{3,195},{18,82},{19,211},{4... | collective-permute-start | bytes 589832 | tf_op jit(solution)/shard_map/ppermute | solution.py:48
  6.4 1.5 %collective-permute-start.2 = (bf16[96,1024]{1,0:T(8,128)(2,1)}, bf16[96,1024]{1,0:T(8,128)(2,1)S(1)}, u32[]{:S(2)}, u32[]{:S(2)}) collective-permute-start(bf16[96,1024]{1,0:T(8,128)(2,1)} %refs_1_.1), channel_id=1, source_target_pairs={{0,16},{1,19},{16,0},{17,3},{2,18},{3,17},{18,2},{19,1},{4,20},{5,... | collective-permute-start | bytes 589832 | tf_op jit(solution)/shard_map/ppermute | solution.py:52
  7.9 0.1 stack.23.where
  8.0 6.6 %shard_map.28 = (f32[8,48,128]{2,1,0:T(8,128)S(1)}, f32[8,48,128]{2,1,0:T(8,128)S(1)}, bf16[64,64,1024]{2,1,0:T(8,128)(2,1)S(1)}) custom-call(s32[5]{0:T(128)S(1)} %stack.23.where, bf16[64,64,1024]{2,1,0:T(8,128)(2,1)} %refs_0_.1, bf16[96,1024]{1,0:T(8,128)(2,1)} %refs_1_.1), custom_call_target="tpu_custom_call" | custom-call | flops 805306368 | bytes 16777216 | tf_op jit(solution)/shard_map/pallas_call | solution.py:170
  14.6 0.0 collective-permute-done
  14.6 0.0 collective-permute-done.1
  14.6 0.4 collective-permute-start.5
  15.0 0.4 collective-permute-start.7
  15.4 1.0 %collective-permute-start.3 = (bf16[96,1024]{1,0:T(8,128)(2,1)S(1)}, bf16[96,1024]{1,0:T(8,128)(2,1)S(1)}, u32[]{:S(2)}, u32[]{:S(2)}) collective-permute-start(bf16[96,1024]{1,0:T(8,128)(2,1)S(1)} %collective-permute-done.1), channel_id=1, source_target_pairs={{0,32},{1,225},{16,48},{17,241},{2,34},{3,227},{18,50},{19,243},{4... | collective-permute-start | bytes 589832 | tf_op jit(solution)/shard_map/ppermute | solution.py:48
  16.4 3.0 %collective-permute-start.4 = (bf16[48,1024]{1,0:T(8,128)(2,1)S(1)}, bf16[48,1024]{1,0:T(8,128)(2,1)S(1)}, u32[]{:S(2)}, u32[]{:S(2)}) collective-permute-start(bf16[48,1024]{1,0:T(8,128)(2,1)S(1)} %constant_dynamic-slice_fusion), channel_id=1, source_target_pairs={{0,64},{1,193},{16,80},{17,209},{2,66},{3,195},{18,82},{19,211},{4... | collective-permute-start | bytes 294920 | tf_op jit(solution)/shard_map/ppermute | solution.py:48
  19.4 5.5 %shard_map.29 = (f32[8,48,128]{2,1,0:T(8,128)S(1)}, f32[8,48,128]{2,1,0:T(8,128)S(1)}) custom-call(s32[5]{0:T(128)S(1)} %stack.23.where, bf16[64,64,1024]{2,1,0:T(8,128)(2,1)S(1)} %get-tuple-element.29.refs_0_, bf16[192,1024]{1,0:T(8,128)(2,1)S(1)} %pad_maximum_fusion.refs_1_, ...), custom_call_target="tpu_custom_call", output_to_operand_aliasing={{0}: (5, {}), {1}: (6, {})} | custom-call | flops 4026531840 | bytes 1048576 | tf_op jit(solution)/shard_map/pallas_call | solution.py:170
  24.9 0.3 collective-permute-start.8
  25.2 1.7 %collective-permute-start.6 = (bf16[144,1024]{1,0:T(8,128)(2,1)S(1)}, bf16[144,1024]{1,0:T(8,128)(2,1)S(1)}, u32[]{:S(2)}, u32[]{:S(2)}) collective-permute-start(bf16[144,1024]{1,0:T(8,128)(2,1)S(1)} %constant_dynamic-update-slice_fusion.refs_2_), channel_id=1, source_target_pairs={{0,16},{1,19},{16,0},{17,3},{2,18},{3,17},{18,2},{19,1},{4,20},{5,... | collective-permute-start | bytes 884744 | tf_op jit(solution)/shard_map/ppermute | solution.py:52
  26.9 0.6 %collective-permute-start.10 = (bf16[192,1024]{1,0:T(8,128)(2,1)S(1)}, bf16[192,1024]{1,0:T(8,128)(2,1)S(1)}, u32[]{:S(2)}, u32[]{:S(2)}) collective-permute-start(bf16[192,1024]{1,0:T(8,128)(2,1)S(1)} %collective-permute-done.7.refs_1_), channel_id=1, source_target_pairs={{0,1},{1,0},{16,17},{17,16},{2,3},{3,2},{18,19},{19,18},{4,5},{5,4... | collective-permute-start | bytes 1179656 | tf_op jit(solution)/shard_map/ppermute | solution.py:56
  27.5 5.6 %shard_map.30 = (f32[8,48,128]{2,1,0:T(8,128)S(1)}, f32[8,48,128]{2,1,0:T(8,128)S(1)}) custom-call(s32[5]{0:T(128)S(1)} %stack.23.where, bf16[64,64,1024]{2,1,0:T(8,128)(2,1)S(1)} %get-tuple-element.29.refs_0_, bf16[192,1024]{1,0:T(8,128)(2,1)S(1)} %collective-permute-done.7.refs_1_, ...), custom_call_target="tpu_custom_call", output_to_operand_aliasing={{0}: (5, {}), {1}: (6, {})} | custom-call | flops 4026531840 | bytes 1048576 | tf_op jit(solution)/shard_map/pallas_call | solution.py:170
  33.1 0.1 collective-permute-start.9
  33.2 3.1 %shard_map.31 = (f32[8,48,128]{2,1,0:T(8,128)S(1)}, f32[8,48,128]{2,1,0:T(8,128)S(1)}, f32[64,512]{1,0:T(8,128)S(1)}) custom-call(s32[5]{0:T(128)S(1)} %stack.23.where, bf16[64,64,1024]{2,1,0:T(8,128)(2,1)S(1)} %get-tuple-element.29.refs_0_, bf16[192,1024]{1,0:T(8,128)(2,1)S(1)} %collective-permute-done.10.refs_1_, ...), custom_call_target="tpu_custom_call", output_to_operand_aliasing={{0}: (4, {}), {1}: (5, {})} | custom-call | flops 2147483648 | bytes 1048576 | tf_op jit(solution)/shard_map/pallas_call | solution.py:170
  36.3 3.2 %shard_map.32 = (f32[8,48,128]{2,1,0:T(8,128)S(1)}, f32[8,48,128]{2,1,0:T(8,128)S(1)}, f32[64,512]{1,0:T(8,128)S(1)}) custom-call(s32[5]{0:T(128)S(1)} %stack.23.where, bf16[64,64,1024]{2,1,0:T(8,128)(2,1)S(1)} %get-tuple-element.29.refs_0_, ...), custom_call_target="tpu_custom_call", output_to_operand_aliasing={{0}: (4, {}), {1}: (5, {}), {2}: (6, {})} | custom-call | flops 1879048192 | bytes 1048576 | tf_op jit(solution)/shard_map/pallas_call | solution.py:170
  39.5 0.6 %collective-permute-start.11 = (f32[8,48,128]{2,1,0:T(8,128)S(1)}, f32[8,48,128]{2,1,0:T(8,128)S(1)}, u32[]{:S(2)}, u32[]{:S(2)}) collective-permute-start(f32[8,48,128]{2,1,0:T(8,128)S(1)} %get-tuple-element.52), channel_id=1, source_target_pairs={{0,1},{1,0},{16,17},{17,16},{2,3},{3,2},{18,19},{19,18},{4,5},{5,4... | collective-permute-start | bytes 589832 | tf_op jit(solution)/shard_map/ppermute | solution.py:56
  40.1 1.1 %collective-permute-done.11.theirs = f32[8,48,128]{2,1,0:T(8,128)S(1)} collective-permute-done((f32[8,48,128]{2,1,0:T(8,128)S(1)}, f32[8,48,128]{2,1,0:T(8,128)S(1)}, u32[]{:S(2)}, u32[]{:S(2)}) %collective-permute-start.11) | collective-permute-done | bytes 196640 | tf_op jit(solution)/shard_map/ppermute | solution.py:56
  41.2 14.3 %all_to_all.5 = f32[8,48,128]{2,1,0:T(8,128)S(1)} all-to-all(f32[8,48,128]{2,1,0:T(8,128)S(1)} %shard_map.33), channel_id=1, replica_groups={{0,2,4,6,8,10,12,14},{1,3,5,7,9,11,13,15},{16,18,20,22,24,26,28,30},{17..., dimensions={0} | all-to-all | bytes 393216 | tf_op jit(solution)/shard_map/all_to_all | solution.py:304
  55.5 0.1 fusion
  55.6 0.7 %maximum_bitcast_fusion = bf16[96,64]{0,1:T(8,128)(2,1)} fusion(bf16[16,32]{1,0:T(8,128)(2,1)S(1)} %get-tuple-element.55, bf16[16,32]{1,0:T(8,128)(2,1)S(1)} %get-tuple-element.54, bf16[16,32]{1,0:T(8,128)(2,1)S(1)} %get-tuple-element.53, bf16[48,96]{1,0:T(8,128)(2,1)S(1)} %bitcast.8), kind=kLoop, calls=%fused_computation.1 | loop fusion | flops 49152 | bytes 24576 | tf_op jit(solution)/shard_map/transpose | solution.py:306
  (15 shorter events, 0.1 us)
Async XLA Ops:
  0.0 14.6 %collective-permute-start = (bf16[96,1024]{1,0:T(8,128)(2,1)}, bf16[96,1024]{1,0:T(8,128)(2,1)S(1)}, u32[]{:S(2)}, u32[]{:S(2)}) collective-permute-start(bf16[96,1024]{1,0:T(8,128)(2,1)} %refs_1_.1), channel_id=1, source_target_pairs={{0,32},{1,225},{16,48},{17,241},{2,34},{3,227},{18,50},{19,243},{4... | collective-permute-start | bytes 589832 | tf_op jit(solution)/shard_map/ppermute | solution.py:48
  1.9 12.6 %collective-permute-start.1 = (bf16[96,1024]{1,0:T(8,128)(2,1)}, bf16[96,1024]{1,0:T(8,128)(2,1)S(1)}, u32[]{:S(2)}, u32[]{:S(2)}) collective-permute-start(bf16[96,1024]{1,0:T(8,128)(2,1)} %refs_1_.1), channel_id=1, source_target_pairs={{0,64},{1,193},{16,80},{17,209},{2,66},{3,195},{18,82},{19,211},{4... | collective-permute-start | bytes 589832 | tf_op jit(solution)/shard_map/ppermute | solution.py:48
  6.4 8.2 %collective-permute-start.2 = (bf16[96,1024]{1,0:T(8,128)(2,1)}, bf16[96,1024]{1,0:T(8,128)(2,1)S(1)}, u32[]{:S(2)}, u32[]{:S(2)}) collective-permute-start(bf16[96,1024]{1,0:T(8,128)(2,1)} %refs_1_.1), channel_id=1, source_target_pairs={{0,16},{1,19},{16,0},{17,3},{2,18},{3,17},{18,2},{19,1},{4,20},{5,... | collective-permute-start | bytes 589832 | tf_op jit(solution)/shard_map/ppermute | solution.py:52
  14.6 4.7 %collective-permute-start.5 = (bf16[192,1024]{1,0:T(8,128)(2,1)S(1)}, bf16[192,1024]{1,0:T(8,128)(2,1)S(1)}, u32[]{:S(2)}, u32[]{:S(2)}) collective-permute-start(bf16[192,1024]{1,0:T(8,128)(2,1)S(1)} %pad_maximum_fusion.refs_1_), channel_id=1, source_target_pairs={{0,1},{1,0},{16,17},{17,16},{2,3},{3,2},{18,19},{19,18},{4,5},{5,4... | collective-permute-start | bytes 1179656 | tf_op jit(solution)/shard_map/ppermute | solution.py:56
  15.0 11.9 %collective-permute-start.7 = (bf16[192,1024]{1,0:T(8,128)(2,1)S(1)}, bf16[192,1024]{1,0:T(8,128)(2,1)S(1)}, u32[]{:S(2)}, u32[]{:S(2)}) collective-permute-start(bf16[192,1024]{1,0:T(8,128)(2,1)S(1)} %pad_maximum_fusion.refs_1_), channel_id=1, source_target_pairs={{0,16},{1,19},{16,0},{17,3},{2,18},{3,17},{18,2},{19,1},{4,20},{5,... | collective-permute-start | bytes 1179656 | tf_op jit(solution)/shard_map/ppermute | solution.py:52
  15.4 9.5 %collective-permute-start.3 = (bf16[96,1024]{1,0:T(8,128)(2,1)S(1)}, bf16[96,1024]{1,0:T(8,128)(2,1)S(1)}, u32[]{:S(2)}, u32[]{:S(2)}) collective-permute-start(bf16[96,1024]{1,0:T(8,128)(2,1)S(1)} %collective-permute-done.1), channel_id=1, source_target_pairs={{0,32},{1,225},{16,48},{17,241},{2,34},{3,227},{18,50},{19,243},{4... | collective-permute-start | bytes 589832 | tf_op jit(solution)/shard_map/ppermute | solution.py:48
  16.4 8.4 %collective-permute-start.4 = (bf16[48,1024]{1,0:T(8,128)(2,1)S(1)}, bf16[48,1024]{1,0:T(8,128)(2,1)S(1)}, u32[]{:S(2)}, u32[]{:S(2)}) collective-permute-start(bf16[48,1024]{1,0:T(8,128)(2,1)S(1)} %constant_dynamic-slice_fusion), channel_id=1, source_target_pairs={{0,64},{1,193},{16,80},{17,209},{2,66},{3,195},{18,82},{19,211},{4... | collective-permute-start | bytes 294920 | tf_op jit(solution)/shard_map/ppermute | solution.py:48
  24.9 2.6 %collective-permute-start.8 = (bf16[144,1024]{1,0:T(8,128)(2,1)S(1)}, bf16[144,1024]{1,0:T(8,128)(2,1)S(1)}, u32[]{:S(2)}, u32[]{:S(2)}) collective-permute-start(bf16[144,1024]{1,0:T(8,128)(2,1)S(1)} %constant_dynamic-update-slice_fusion.refs_2_), channel_id=1, source_target_pairs={{0,1},{1,0},{16,17},{17,16},{2,3},{3,2},{18,19},{19,18},{4,5},{5,4... | collective-permute-start | bytes 884744 | tf_op jit(solution)/shard_map/ppermute | solution.py:56
  25.2 7.9 %collective-permute-start.6 = (bf16[144,1024]{1,0:T(8,128)(2,1)S(1)}, bf16[144,1024]{1,0:T(8,128)(2,1)S(1)}, u32[]{:S(2)}, u32[]{:S(2)}) collective-permute-start(bf16[144,1024]{1,0:T(8,128)(2,1)S(1)} %constant_dynamic-update-slice_fusion.refs_2_), channel_id=1, source_target_pairs={{0,16},{1,19},{16,0},{17,3},{2,18},{3,17},{18,2},{19,1},{4,20},{5,... | collective-permute-start | bytes 884744 | tf_op jit(solution)/shard_map/ppermute | solution.py:52
  26.9 6.3 %collective-permute-start.10 = (bf16[192,1024]{1,0:T(8,128)(2,1)S(1)}, bf16[192,1024]{1,0:T(8,128)(2,1)S(1)}, u32[]{:S(2)}, u32[]{:S(2)}) collective-permute-start(bf16[192,1024]{1,0:T(8,128)(2,1)S(1)} %collective-permute-done.7.refs_1_), channel_id=1, source_target_pairs={{0,1},{1,0},{16,17},{17,16},{2,3},{3,2},{18,19},{19,18},{4,5},{5,4... | collective-permute-start | bytes 1179656 | tf_op jit(solution)/shard_map/ppermute | solution.py:56
  33.1 3.3 %collective-permute-start.9 = (bf16[144,1024]{1,0:T(8,128)(2,1)S(1)}, bf16[144,1024]{1,0:T(8,128)(2,1)S(1)}, u32[]{:S(2)}, u32[]{:S(2)}) collective-permute-start(bf16[144,1024]{1,0:T(8,128)(2,1)S(1)} %collective-permute-done.6.refs_2_.refs_1_), channel_id=1, source_target_pairs={{0,1},{1,0},{16,17},{17,16},{2,3},{3,2},{18,19},{19,18},{4,5},{5,4... | collective-permute-start | bytes 884744 | tf_op jit(solution)/shard_map/ppermute | solution.py:56
  39.5 1.7 %collective-permute-start.11 = (f32[8,48,128]{2,1,0:T(8,128)S(1)}, f32[8,48,128]{2,1,0:T(8,128)S(1)}, u32[]{:S(2)}, u32[]{:S(2)}) collective-permute-start(f32[8,48,128]{2,1,0:T(8,128)S(1)} %get-tuple-element.52), channel_id=1, source_target_pairs={{0,1},{1,0},{16,17},{17,16},{2,3},{3,2},{18,19},{19,18},{4,5},{5,4... | collective-permute-start | bytes 589832 | tf_op jit(solution)/shard_map/ppermute | solution.py:56

commit v9 on v8

--- a/solution.py
+++ b/solution.py
@@ -233,12 +233,10 @@
 
     one, two, same_x, give = lax.optimization_barrier((one, two, same_x, give))
     near = rows(one, two)
-    hops = half(two)
-    near, two, hops = lax.optimization_barrier((near, two, hops))
-    four = along_z(hops, 2)
     three = along_z(two, 1)
+    four = along_z(half(two), 2)
+    near_swap = swap(near)
     near_x = along_x(near)
-    near_swap = swap(near)
     call = Call(
         "plain",
         0,

time: 56.8 us -> 56.9 us (level)
    ppermute x3, starting transfers between devices: 3.56 us -> 2.91 us  [along_x(): lax.ppermute(array, AXES, hop(lambda c, x: (sign((x + c) % 2), 0, 0, 0)))]
    ppermute x5, starting transfers between devices: 1.93 us -> 2.57 us  [swap(): return lax.ppermute(array, AXES, hop(lambda c, x: (0, 0, 0, 1)))]
where the time goes in v9:
time: 56.9 us; the launch traced here: 56.4 us
  Pallas kernels  23.9 us (42%)
  starting transfers between devices  15.9 us (28%)
  blocking collectives  14.3 us (25%)
  waiting for transfers between devices  1.1 us (2%)
  other arithmetic  0.7 us (1%)
    pallas_call x5, Pallas kernels, partial_sums(): pl.pallas_call(functools.partial(collide, call), in_specs=in_specs, out_s...  23.9 us
    all_to_all x1, blocking collectives, local(): lax.all_to_all(pair, 'inp', 0, 0, tiled=True, axis_index_groups=groups)  14.3 us
    ppermute x4, starting transfers between devices, along_z(): return lax.ppermute(array, AXES, hop(lambda c, x: (0, 0, d * sign(c), 0)))  10.5 us
    ppermute x3, starting transfers between devices, along_x(): lax.ppermute(array, AXES, hop(lambda c, x: (sign((x + c) % 2), 0, 0, 0)))  2.91 us
    ppermute x5, starting transfers between devices, swap(): return lax.ppermute(array, AXES, hop(lambda c, x: (0, 0, 0, 1)))  2.57 us
  transfers between devices with their start and end apart: 12, of which 1 were waited for; matrix products, arithmetic and copies ran while one was open for 0% of the time, Pallas kernels for 37%

profile of v9, /device:TPU:32, one launch (start us, length us, event | category | flops | bytes accessed | tf_op | source)
XLA Modules:
  0.0 56.4 jit_solution(1506696956365944513)
XLA Ops:
  0.0 1.9 %collective-permute-start = (bf16[96,1024]{1,0:T(8,128)(2,1)}, bf16[96,1024]{1,0:T(8,128)(2,1)S(1)}, u32[]{:S(2)}, u32[]{:S(2)}) collective-permute-start(bf16[96,1024]{1,0:T(8,128)(2,1)} %refs_1_.1), channel_id=1, source_target_pairs={{0,32},{1,225},{16,48},{17,241},{2,34},{3,227},{18,50},{19,243},{4... | collective-permute-start | bytes 589832 | tf_op jit(solution)/shard_map/ppermute | solution.py:48
  1.9 4.5 %collective-permute-start.1 = (bf16[96,1024]{1,0:T(8,128)(2,1)}, bf16[96,1024]{1,0:T(8,128)(2,1)S(1)}, u32[]{:S(2)}, u32[]{:S(2)}) collective-permute-start(bf16[96,1024]{1,0:T(8,128)(2,1)} %refs_1_.1), channel_id=1, source_target_pairs={{0,64},{1,193},{16,80},{17,209},{2,66},{3,195},{18,82},{19,211},{4... | collective-permute-start | bytes 589832 | tf_op jit(solution)/shard_map/ppermute | solution.py:48
  6.4 1.5 %collective-permute-start.2 = (bf16[96,1024]{1,0:T(8,128)(2,1)}, bf16[96,1024]{1,0:T(8,128)(2,1)S(1)}, u32[]{:S(2)}, u32[]{:S(2)}) collective-permute-start(bf16[96,1024]{1,0:T(8,128)(2,1)} %refs_1_.1), channel_id=1, source_target_pairs={{0,16},{1,19},{16,0},{17,3},{2,18},{3,17},{18,2},{19,1},{4,20},{5,... | collective-permute-start | bytes 589832 | tf_op jit(solution)/shard_map/ppermute | solution.py:52
  7.9 0.1 stack.23.where
  8.0 6.6 %shard_map.28 = (f32[8,48,128]{2,1,0:T(8,128)S(1)}, f32[8,48,128]{2,1,0:T(8,128)S(1)}, bf16[64,64,1024]{2,1,0:T(8,128)(2,1)S(1)}) custom-call(s32[5]{0:T(128)S(1)} %stack.23.where, bf16[64,64,1024]{2,1,0:T(8,128)(2,1)} %refs_0_.1, bf16[96,1024]{1,0:T(8,128)(2,1)} %refs_1_.1), custom_call_target="tpu_custom_call" | custom-call | flops 805306368 | bytes 16777216 | tf_op jit(solution)/shard_map/pallas_call | solution.py:170
  14.6 0.0 collective-permute-done.2.refs_3_
  14.6 0.4 collective-permute-start.5
  15.0 1.0 %collective-permute-start.3 = (bf16[96,1024]{1,0:T(8,128)(2,1)S(1)}, bf16[96,1024]{1,0:T(8,128)(2,1)S(1)}, u32[]{:S(2)}, u32[]{:S(2)}) collective-permute-start(bf16[96,1024]{1,0:T(8,128)(2,1)S(1)} %collective-permute-done.1), channel_id=1, source_target_pairs={{0,32},{1,225},{16,48},{17,241},{2,34},{3,227},{18,50},{19,243},{4... | collective-permute-start | bytes 589832 | tf_op jit(solution)/shard_map/ppermute | solution.py:48
  16.0 0.4 collective-permute-start.7
  16.4 3.1 %collective-permute-start.4 = (bf16[48,1024]{1,0:T(8,128)(2,1)S(1)}, bf16[48,1024]{1,0:T(8,128)(2,1)S(1)}, u32[]{:S(2)}, u32[]{:S(2)}) collective-permute-start(bf16[48,1024]{1,0:T(8,128)(2,1)S(1)} %constant_dynamic-slice_fusion), channel_id=1, source_target_pairs={{0,64},{1,193},{16,80},{17,209},{2,66},{3,195},{18,82},{19,211},{4... | collective-permute-start | bytes 294920 | tf_op jit(solution)/shard_map/ppermute | solution.py:48
  19.4 0.0 collective-permute-done.5.refs_2_
  19.4 5.5 %shard_map.29 = (f32[8,48,128]{2,1,0:T(8,128)S(1)}, f32[8,48,128]{2,1,0:T(8,128)S(1)}) custom-call(s32[5]{0:T(128)S(1)} %stack.23.where, bf16[64,64,1024]{2,1,0:T(8,128)(2,1)S(1)} %get-tuple-element.26.refs_0_, bf16[192,1024]{1,0:T(8,128)(2,1)S(1)} %constant_dynamic-update-slice_fusion.refs_1_, ...), custom_call_target="tpu_custom_call", output_to_operand_aliasing={{0}: (5, {}), {1}: (6, {})} | custom-call | flops 4026531840 | bytes 1048576 | tf_op jit(solution)/shard_map/pallas_call | solution.py:170
  24.9 0.3 collective-permute-start.8
  25.2 1.1 %collective-permute-start.6 = (bf16[144,1024]{1,0:T(8,128)(2,1)S(1)}, bf16[144,1024]{1,0:T(8,128)(2,1)S(1)}, u32[]{:S(2)}, u32[]{:S(2)}) collective-permute-start(bf16[144,1024]{1,0:T(8,128)(2,1)S(1)} %constant_dynamic-update-slice_fusion.2.refs_2_), channel_id=1, source_target_pairs={{0,16},{1,19},{16,0},{17,3},{2,18},{3,17},{18,2},{19,1},{4,20},{5,... | collective-permute-start | bytes 884744 | tf_op jit(solution)/shard_map/ppermute | solution.py:52
  26.3 1.2 %collective-permute-start.10 = (bf16[192,1024]{1,0:T(8,128)(2,1)S(1)}, bf16[192,1024]{1,0:T(8,128)(2,1)S(1)}, u32[]{:S(2)}, u32[]{:S(2)}) collective-permute-start(bf16[192,1024]{1,0:T(8,128)(2,1)S(1)} %collective-permute-done.7.refs_1_), channel_id=1, source_target_pairs={{0,1},{1,0},{16,17},{17,16},{2,3},{3,2},{18,19},{19,18},{4,5},{5,4... | collective-permute-start | bytes 1179656 | tf_op jit(solution)/shard_map/ppermute | solution.py:56
  27.5 5.6 %shard_map.30 = (f32[8,48,128]{2,1,0:T(8,128)S(1)}, f32[8,48,128]{2,1,0:T(8,128)S(1)}) custom-call(s32[5]{0:T(128)S(1)} %stack.23.where, bf16[64,64,1024]{2,1,0:T(8,128)(2,1)S(1)} %get-tuple-element.26.refs_0_, bf16[192,1024]{1,0:T(8,128)(2,1)S(1)} %collective-permute-done.7.refs_1_, ...), custom_call_target="tpu_custom_call", output_to_operand_aliasing={{0}: (5, {}), {1}: (6, {})} | custom-call | flops 4026531840 | bytes 1048576 | tf_op jit(solution)/shard_map/pallas_call | solution.py:170
  33.1 0.1 collective-permute-start.9
  33.2 3.1 %shard_map.31 = (f32[8,48,128]{2,1,0:T(8,128)S(1)}, f32[8,48,128]{2,1,0:T(8,128)S(1)}, f32[64,512]{1,0:T(8,128)S(1)}) custom-call(s32[5]{0:T(128)S(1)} %stack.23.where, bf16[64,64,1024]{2,1,0:T(8,128)(2,1)S(1)} %get-tuple-element.26.refs_0_, bf16[192,1024]{1,0:T(8,128)(2,1)S(1)} %collective-permute-done.10.refs_1_, ...), custom_call_target="tpu_custom_call", output_to_operand_aliasing={{0}: (4, {}), {1}: (5, {})} | custom-call | flops 2147483648 | bytes 1048576 | tf_op jit(solution)/shard_map/pallas_call | solution.py:170
  36.4 3.2 %shard_map.32 = (f32[8,48,128]{2,1,0:T(8,128)S(1)}, f32[8,48,128]{2,1,0:T(8,128)S(1)}, f32[64,512]{1,0:T(8,128)S(1)}) custom-call(s32[5]{0:T(128)S(1)} %stack.23.where, bf16[64,64,1024]{2,1,0:T(8,128)(2,1)S(1)} %get-tuple-element.26.refs_0_, ...), custom_call_target="tpu_custom_call", output_to_operand_aliasing={{0}: (4, {}), {1}: (5, {}), {2}: (6, {})} | custom-call | flops 1879048192 | bytes 1048576 | tf_op jit(solution)/shard_map/pallas_call | solution.py:170
  39.6 0.6 %collective-permute-start.11 = (f32[8,48,128]{2,1,0:T(8,128)S(1)}, f32[8,48,128]{2,1,0:T(8,128)S(1)}, u32[]{:S(2)}, u32[]{:S(2)}) collective-permute-start(f32[8,48,128]{2,1,0:T(8,128)S(1)} %get-tuple-element.46), channel_id=1, source_target_pairs={{0,1},{1,0},{16,17},{17,16},{2,3},{3,2},{18,19},{19,18},{4,5},{5,4... | collective-permute-start | bytes 589832 | tf_op jit(solution)/shard_map/ppermute | solution.py:56
  40.2 1.1 %collective-permute-done.11.theirs = f32[8,48,128]{2,1,0:T(8,128)S(1)} collective-permute-done((f32[8,48,128]{2,1,0:T(8,128)S(1)}, f32[8,48,128]{2,1,0:T(8,128)S(1)}, u32[]{:S(2)}, u32[]{:S(2)}) %collective-permute-start.11) | collective-permute-done | bytes 196640 | tf_op jit(solution)/shard_map/ppermute | solution.py:56
  41.3 14.3 %all_to_all.5 = f32[8,48,128]{2,1,0:T(8,128)S(1)} all-to-all(f32[8,48,128]{2,1,0:T(8,128)S(1)} %shard_map.33), channel_id=1, replica_groups={{0,2,4,6,8,10,12,14},{1,3,5,7,9,11,13,15},{16,18,20,22,24,26,28,30},{17..., dimensions={0} | all-to-all | bytes 393216 | tf_op jit(solution)/shard_map/all_to_all | solution.py:302
  55.6 0.1 fusion
  55.7 0.7 %maximum_bitcast_fusion = bf16[96,64]{0,1:T(8,128)(2,1)} fusion(bf16[16,32]{1,0:T(8,128)(2,1)S(1)} %get-tuple-element.49, bf16[16,32]{1,0:T(8,128)(2,1)S(1)} %get-tuple-element.48, bf16[16,32]{1,0:T(8,128)(2,1)S(1)} %get-tuple-element.47, bf16[48,96]{1,0:T(8,128)(2,1)S(1)} %bitcast.8), kind=kLoop, calls=%fused_computation | loop fusion | flops 49152 | bytes 24576 | tf_op jit(solution)/shard_map/transpose | solution.py:304
  (16 shorter events, 0.1 us)
Async XLA Ops:
  0.0 14.6 %collective-permute-start = (bf16[96,1024]{1,0:T(8,128)(2,1)}, bf16[96,1024]{1,0:T(8,128)(2,1)S(1)}, u32[]{:S(2)}, u32[]{:S(2)}) collective-permute-start(bf16[96,1024]{1,0:T(8,128)(2,1)} %refs_1_.1), channel_id=1, source_target_pairs={{0,32},{1,225},{16,48},{17,241},{2,34},{3,227},{18,50},{19,243},{4... | collective-permute-start | bytes 589832 | tf_op jit(solution)/shard_map/ppermute | solution.py:48
  1.9 12.6 %collective-permute-start.1 = (bf16[96,1024]{1,0:T(8,128)(2,1)}, bf16[96,1024]{1,0:T(8,128)(2,1)S(1)}, u32[]{:S(2)}, u32[]{:S(2)}) collective-permute-start(bf16[96,1024]{1,0:T(8,128)(2,1)} %refs_1_.1), channel_id=1, source_target_pairs={{0,64},{1,193},{16,80},{17,209},{2,66},{3,195},{18,82},{19,211},{4... | collective-permute-start | bytes 589832 | tf_op jit(solution)/shard_map/ppermute | solution.py:48
  6.4 8.2 %collective-permute-start.2 = (bf16[96,1024]{1,0:T(8,128)(2,1)}, bf16[96,1024]{1,0:T(8,128)(2,1)S(1)}, u32[]{:S(2)}, u32[]{:S(2)}) collective-permute-start(bf16[96,1024]{1,0:T(8,128)(2,1)} %refs_1_.1), channel_id=1, source_target_pairs={{0,16},{1,19},{16,0},{17,3},{2,18},{3,17},{18,2},{19,1},{4,20},{5,... | collective-permute-start | bytes 589832 | tf_op jit(solution)/shard_map/ppermute | solution.py:52
  14.6 4.8 %collective-permute-start.5 = (bf16[192,1024]{1,0:T(8,128)(2,1)S(1)}, bf16[192,1024]{1,0:T(8,128)(2,1)S(1)}, u32[]{:S(2)}, u32[]{:S(2)}) collective-permute-start(bf16[192,1024]{1,0:T(8,128)(2,1)S(1)} %constant_dynamic-update-slice_fusion.refs_1_), channel_id=1, source_target_pairs={{0,1},{1,0},{16,17},{17,16},{2,3},{3,2},{18,19},{19,18},{4,5},{5,4... | collective-permute-start | bytes 1179656 | tf_op jit(solution)/shard_map/ppermute | solution.py:56
  15.0 9.9 %collective-permute-start.3 = (bf16[96,1024]{1,0:T(8,128)(2,1)S(1)}, bf16[96,1024]{1,0:T(8,128)(2,1)S(1)}, u32[]{:S(2)}, u32[]{:S(2)}) collective-permute-start(bf16[96,1024]{1,0:T(8,128)(2,1)S(1)} %collective-permute-done.1), channel_id=1, source_target_pairs={{0,32},{1,225},{16,48},{17,241},{2,34},{3,227},{18,50},{19,243},{4... | collective-permute-start | bytes 589832 | tf_op jit(solution)/shard_map/ppermute | solution.py:48
  16.0 10.3 %collective-permute-start.7 = (bf16[192,1024]{1,0:T(8,128)(2,1)S(1)}, bf16[192,1024]{1,0:T(8,128)(2,1)S(1)}, u32[]{:S(2)}, u32[]{:S(2)}) collective-permute-start(bf16[192,1024]{1,0:T(8,128)(2,1)S(1)} %constant_dynamic-update-slice_fusion.refs_1_), channel_id=1, source_target_pairs={{0,16},{1,19},{16,0},{17,3},{2,18},{3,17},{18,2},{19,1},{4,20},{5,... | collective-permute-start | bytes 1179656 | tf_op jit(solution)/shard_map/ppermute | solution.py:52
  16.4 8.5 %collective-permute-start.4 = (bf16[48,1024]{1,0:T(8,128)(2,1)S(1)}, bf16[48,1024]{1,0:T(8,128)(2,1)S(1)}, u32[]{:S(2)}, u32[]{:S(2)}) collective-permute-start(bf16[48,1024]{1,0:T(8,128)(2,1)S(1)} %constant_dynamic-slice_fusion), channel_id=1, source_target_pairs={{0,64},{1,193},{16,80},{17,209},{2,66},{3,195},{18,82},{19,211},{4... | collective-permute-start | bytes 294920 | tf_op jit(solution)/shard_map/ppermute | solution.py:48
  24.9 2.6 %collective-permute-start.8 = (bf16[144,1024]{1,0:T(8,128)(2,1)S(1)}, bf16[144,1024]{1,0:T(8,128)(2,1)S(1)}, u32[]{:S(2)}, u32[]{:S(2)}) collective-permute-start(bf16[144,1024]{1,0:T(8,128)(2,1)S(1)} %constant_dynamic-update-slice_fusion.2.refs_2_), channel_id=1, source_target_pairs={{0,1},{1,0},{16,17},{17,16},{2,3},{3,2},{18,19},{19,18},{4,5},{5,4... | collective-permute-start | bytes 884744 | tf_op jit(solution)/shard_map/ppermute | solution.py:56
  25.2 7.9 %collective-permute-start.6 = (bf16[144,1024]{1,0:T(8,128)(2,1)S(1)}, bf16[144,1024]{1,0:T(8,128)(2,1)S(1)}, u32[]{:S(2)}, u32[]{:S(2)}) collective-permute-start(bf16[144,1024]{1,0:T(8,128)(2,1)S(1)} %constant_dynamic-update-slice_fusion.2.refs_2_), channel_id=1, source_target_pairs={{0,16},{1,19},{16,0},{17,3},{2,18},{3,17},{18,2},{19,1},{4,20},{5,... | collective-permute-start | bytes 884744 | tf_op jit(solution)/shard_map/ppermute | solution.py:52
  26.3 6.9 %collective-permute-start.10 = (bf16[192,1024]{1,0:T(8,128)(2,1)S(1)}, bf16[192,1024]{1,0:T(8,128)(2,1)S(1)}, u32[]{:S(2)}, u32[]{:S(2)}) collective-permute-start(bf16[192,1024]{1,0:T(8,128)(2,1)S(1)} %collective-permute-done.7.refs_1_), channel_id=1, source_target_pairs={{0,1},{1,0},{16,17},{17,16},{2,3},{3,2},{18,19},{19,18},{4,5},{5,4... | collective-permute-start | bytes 1179656 | tf_op jit(solution)/shard_map/ppermute | solution.py:56
  33.1 3.3 %collective-permute-start.9 = (bf16[144,1024]{1,0:T(8,128)(2,1)S(1)}, bf16[144,1024]{1,0:T(8,128)(2,1)S(1)}, u32[]{:S(2)}, u32[]{:S(2)}) collective-permute-start(bf16[144,1024]{1,0:T(8,128)(2,1)S(1)} %collective-permute-done.6.refs_2_.refs_1_), channel_id=1, source_target_pairs={{0,1},{1,0},{16,17},{17,16},{2,3},{3,2},{18,19},{19,18},{4,5},{5,4... | collective-permute-start | bytes 884744 | tf_op jit(solution)/shard_map/ppermute | solution.py:56
  39.6 1.7 %collective-permute-start.11 = (f32[8,48,128]{2,1,0:T(8,128)S(1)}, f32[8,48,128]{2,1,0:T(8,128)S(1)}, u32[]{:S(2)}, u32[]{:S(2)}) collective-permute-start(f32[8,48,128]{2,1,0:T(8,128)S(1)} %get-tuple-element.46), channel_id=1, source_target_pairs={{0,1},{1,0},{16,17},{17,16},{2,3},{3,2},{18,19},{19,18},{4,5},{5,4... | collective-permute-start | bytes 589832 | tf_op jit(solution)/shard_map/ppermute | solution.py:56
